TPU v7x, 32 devices: a whole 2x2x4 slice. The times are simulated.
32 devices in a mesh: dp: 2 (over y), ctx: 4 (over x, core), tp: 4 (over z).
Axes of the slice: x: 2, y: 2, z: 4, core: 2. Of those that a mesh axis runs over, the one named last changes fastest.
Arguments:
- hidden: bfloat16 [8, 1024, 2048], P('dp', 'ctx', 'tp'), may hold values from -6 to 6
- cotangent: bfloat16 [8, 1024, 2048], P('dp', 'ctx', 'tp'), may hold values from -6 to 6
- segments: int32 [8, 1024], P('dp', 'ctx'), may hold values from 0 to 17, as said below
- positions: int32 [8, 1024], P('dp', 'ctx'), may hold values from 0 to 1023, as said below
- w_query: bfloat16 [2048, 2048], P(('dp', 'ctx'), 'tp')
- w_key: bfloat16 [2048, 2048], P(('dp', 'ctx'), 'tp')
- w_value: bfloat16 [2048, 2048], P(('dp', 'ctx'), 'tp'), may hold values from -0.125 to 0.125
- w_out: bfloat16 [2048, 2048], P('tp', ('dp', 'ctx'))
- w_gate: bfloat16 [2048, 8192], P(('dp', 'ctx'), 'tp'), may hold values from -0.125 to 0.125
- w_up: bfloat16 [2048, 8192], P(('dp', 'ctx'), 'tp'), may hold values from -0.125 to 0.125
- w_down: bfloat16 [8192, 2048], P('tp', ('dp', 'ctx'))
- q_gain: float32 [2048], P('tp'), may hold values from 1 to 1.8
- k_gain: float32 [2048], P('tp'), may hold values from 1 to 1.8
- attn_gain: float32 [2048], P('tp'), may hold values from 0.5 to 1.5
- mlp_gain: float32 [2048], P('tp'), may hold values from 0.5 to 1.5
Outputs:
- out_hidden: bfloat16 [8, 1024, 2048], P('dp', 'ctx', 'tp')
- grad_hidden: bfloat16 [8, 1024, 2048], P('dp', 'ctx', 'tp')
- grad_w_query: float32 [2048, 2048], P(('dp', 'ctx'), 'tp')
- grad_w_key: float32 [2048, 2048], P(('dp', 'ctx'), 'tp')
- grad_w_value: float32 [2048, 2048], P(('dp', 'ctx'), 'tp')
- grad_w_out: float32 [2048, 2048], P('tp', ('dp', 'ctx'))
- grad_w_gate: float32 [2048, 8192], P(('dp', 'ctx'), 'tp')
- grad_w_up: float32 [2048, 8192], P(('dp', 'ctx'), 'tp')
- grad_w_down: float32 [8192, 2048], P('tp', ('dp', 'ctx'))
- grad_q_gain: float32 [2048], P('tp')
- grad_k_gain: float32 [2048], P('tp')
- grad_attn_gain: float32 [2048], P('tp')
- grad_mlp_gain: float32 [2048], P('tp')
Inputs may be any that keep to these rules, and one draw needn't show every extreme that they name: `segments`: in each sequence segment numbers start at 0 and never fall; each step of one numbers the next document; every document that the sequence's end does not cut has at least 60 tokens. `positions`: each token's position counts from 0 at the first token of its document.
All inputs are finite; a program needn't handle non-finite values.
Results may differ from a plain program's by a relative error of at most 0.025.
Values may be sent and summed in bfloat16 or wider, within the bound.
A program may use at most 256 MiB of HBM per device.

v0:
```python
import math

import jax
import jax.numpy as jnp
from jax import lax
from jax.sharding import PartitionSpec as P

D = 2048
HEAD_DIM = 128
MICRO = 2


EPS = 1e-06
THETA = 500000.0
NEG = -1e30


def row_total(value):
    return lax.psum(value, "tp")


def widen(value):
    return lax.all_gather(value, "tp", axis=1, tiled=True)


def narrow(value):
    return lax.psum_scatter(
        value.astype(jnp.bfloat16), "tp", scatter_dimension=1, tiled=True
    ).astype(jnp.float32)


def contract_last(left, right):
    return lax.dot_general(
        left, right, (((1,), (1,)), ((), ())), preferred_element_type=jnp.float32
    )


def contract_first(left, right):
    return lax.dot_general(
        left, right, (((0,), (0,)), ((), ())), preferred_element_type=jnp.float32
    )


def rotary(positions, depth):
    half = depth // 2
    freqs = THETA ** (-(jnp.arange(half, dtype=jnp.float32) * 2.0) / depth)
    angles = positions.astype(jnp.float32)[..., None] * freqs
    return (jnp.cos(angles)[..., None, :], jnp.sin(angles)[..., None, :])


def turn(value, cosine, sine):
    half = value.shape[-1] // 2
    first = value[..., :half]
    second = value[..., half:]
    return jnp.concatenate(
        [first * cosine - second * sine, second * cosine + first * sine], axis=-1
    )


def turn_back(grad, cosine, sine):
    half = grad.shape[-1] // 2
    first = grad[..., :half]
    second = grad[..., half:]
    return jnp.concatenate(
        [first * cosine + second * sine, second * cosine - first * sine], axis=-1
    )


def norm_grad(scaled, value, factor, inner):
    return factor[:, None] * scaled - value * (factor**3 * inner / D)[:, None]


def local(
    hidden,
    cotangent,
    segments,
    positions,
    w_query,
    w_key,
    w_value,
    w_out,
    w_gate,
    w_up,
    w_down,
    q_gain,
    k_gain,
    attn_gain,
    mlp_gain,
):
    local_seqs, slice_len, local_width = hidden.shape
    per_batch = local_seqs // MICRO
    rows = per_batch * slice_len
    heads_here = q_gain.shape[0] // HEAD_DIM
    scale = 1.0 / math.sqrt(HEAD_DIM)
    query_index = lax.axis_index("ctx") * slice_len + jnp.arange(slice_len, dtype=jnp.int32)
    outputs = []
    input_grads = []
    weight_grads = None
    q_gain_grad = jnp.zeros(q_gain.shape, jnp.float32)
    k_gain_grad = jnp.zeros(k_gain.shape, jnp.float32)
    attn_gain_grad = jnp.zeros(attn_gain.shape, jnp.float32)
    mlp_gain_grad = jnp.zeros(mlp_gain.shape, jnp.float32)
    for batch in range(MICRO):
        lower = batch * per_batch
        tokens_in = hidden[lower : lower + per_batch].reshape(rows, local_width)
        seg_here = segments[lower : lower + per_batch]
        pos_here = positions[lower : lower + per_batch].reshape(rows)
        gathered = (
            lax.all_gather(w_query, ("dp", "ctx"), axis=0, tiled=True),
            lax.all_gather(w_key, ("dp", "ctx"), axis=0, tiled=True),
            lax.all_gather(w_value, ("dp", "ctx"), axis=0, tiled=True),
            lax.all_gather(w_out, ("dp", "ctx"), axis=1, tiled=True),
            lax.all_gather(w_gate, ("dp", "ctx"), axis=0, tiled=True),
            lax.all_gather(w_up, ("dp", "ctx"), axis=0, tiled=True),
            lax.all_gather(w_down, ("dp", "ctx"), axis=1, tiled=True),
        )
        query_full, key_full, value_full, out_full, gate_full, up_full, down_full = gathered
        if weight_grads is None:
            weight_grads = tuple((jnp.zeros(tensor.shape, jnp.float32) for tensor in gathered))
        wide_in = widen(tokens_in)
        query_raw = jnp.dot(wide_in, query_full, preferred_element_type=jnp.float32)
        key_raw = jnp.dot(wide_in, key_full, preferred_element_type=jnp.float32)
        value_raw = jnp.dot(wide_in, value_full, preferred_element_type=jnp.float32)
        query_sq, key_sq = row_total(
            (jnp.sum(query_raw * query_raw, axis=1), jnp.sum(key_raw * key_raw, axis=1))
        )
        query_scale = lax.rsqrt(query_sq / D + EPS)
        key_scale = lax.rsqrt(key_sq / D + EPS)
        cosine, sine = rotary(pos_here, HEAD_DIM)
        query_rot = turn(
            (query_raw * query_scale[:, None] * q_gain).reshape(rows, heads_here, HEAD_DIM),
            cosine,
            sine,
        )
        key_rot = turn(
            (key_raw * key_scale[:, None] * k_gain).reshape(rows, heads_here, HEAD_DIM),
            cosine,
            sine,
        )
        query_b = query_rot.astype(jnp.bfloat16).reshape(per_batch, slice_len, heads_here, HEAD_DIM)
        key_b = key_rot.astype(jnp.bfloat16).reshape(per_batch, slice_len, heads_here * HEAD_DIM)
        value_b = value_raw.astype(jnp.bfloat16).reshape(
            per_batch, slice_len, heads_here * HEAD_DIM
        )

        def allowed_pairs(seg_piece, count):
            key_index = jnp.arange(count, dtype=jnp.int32)
            causal = query_index[:, None] >= key_index[None, :]
            same = seg_here[:, None, :, None] == seg_piece[:, None, None, :]
            return jnp.logical_and(same, causal[None, None])

        start_peak = jnp.full((per_batch, heads_here, slice_len), NEG, jnp.float32)
        peak = start_peak
        key_piece = lax.all_gather(key_b, "ctx", axis=1, tiled=True)
        value_piece = lax.all_gather(value_b, "ctx", axis=1, tiled=True)
        attend_seg_piece = lax.all_gather(seg_here, "ctx", axis=1, tiled=True)
        attend_count = key_piece.shape[1]
        key_four = key_piece.reshape(per_batch, attend_count, heads_here, HEAD_DIM)
        value_four = value_piece.reshape(per_batch, attend_count, heads_here, HEAD_DIM)
        allowed = allowed_pairs(attend_seg_piece, attend_count)
        logits = scale * jnp.einsum(
            "sqhd,skhd->shqk", query_b, key_four, preferred_element_type=jnp.float32
        )
        logits = jnp.where(allowed, logits, NEG)
        fresh = jnp.maximum(peak, jnp.max(logits, axis=-1))
        weights = jnp.where(allowed, jnp.exp(logits - fresh[..., None]), 0.0)
        total = jnp.sum(weights, axis=-1)
        accum = jnp.einsum(
            "shqk,skhd->shqd",
            weights.astype(jnp.bfloat16),
            value_four,
            preferred_element_type=jnp.float32,
        )
        peak, total, accum = (fresh, total, accum)
        logsum = peak + jnp.log(total)
        out_heads = (
            (accum / total[..., None]).transpose(0, 2, 1, 3).reshape(rows, heads_here * HEAD_DIM)
        )
        out_b = out_heads.astype(jnp.bfloat16)
        attn_raw = narrow(jnp.dot(out_b, out_full, preferred_element_type=jnp.float32))
        attn_scale = lax.rsqrt(row_total(jnp.sum(attn_raw * attn_raw, axis=1)) / D + EPS)
        resid = tokens_in.astype(jnp.float32) + attn_raw * attn_scale[:, None] * attn_gain
        wide_mid = widen(resid.astype(jnp.bfloat16))
        gate = jnp.dot(wide_mid, gate_full, preferred_element_type=jnp.float32)
        up_val = jnp.dot(wide_mid, up_full, preferred_element_type=jnp.float32)
        sigma = jax.nn.sigmoid(gate)
        swish = gate * sigma
        act_b = (swish * up_val).astype(jnp.bfloat16)
        mlp_raw = narrow(jnp.dot(act_b, down_full, preferred_element_type=jnp.float32))
        mlp_scale = lax.rsqrt(row_total(jnp.sum(mlp_raw * mlp_raw, axis=1)) / D + EPS)
        result = resid + mlp_raw * mlp_scale[:, None] * mlp_gain
        outputs.append(result.astype(jnp.bfloat16).reshape(per_batch, slice_len, local_width))
        again = (
            lax.all_gather(w_query, ("dp", "ctx"), axis=0, tiled=True),
            lax.all_gather(w_key, ("dp", "ctx"), axis=0, tiled=True),
            lax.all_gather(w_value, ("dp", "ctx"), axis=0, tiled=True),
            lax.all_gather(w_out, ("dp", "ctx"), axis=1, tiled=True),
            lax.all_gather(w_gate, ("dp", "ctx"), axis=0, tiled=True),
            lax.all_gather(w_up, ("dp", "ctx"), axis=0, tiled=True),
            lax.all_gather(w_down, ("dp", "ctx"), axis=1, tiled=True),
        )
        query_back, key_back, value_back, out_back, gate_back, up_back, down_back = again
        grad_out = (
            cotangent[lower : lower + per_batch].reshape(rows, local_width).astype(jnp.float32)
        )
        mlp_gain_grad = mlp_gain_grad + jnp.sum(grad_out * mlp_raw * mlp_scale[:, None], axis=0)
        scaled = grad_out * mlp_gain
        grad_mlp = norm_grad(
            scaled, mlp_raw, mlp_scale, row_total(jnp.sum(scaled * mlp_raw, axis=1))
        )
        wide_grad_mlp = widen(grad_mlp.astype(jnp.bfloat16))
        grad_act = contract_last(wide_grad_mlp, down_back)
        grad_gate = (grad_act * up_val * sigma * (1.0 + gate * (1.0 - sigma))).astype(jnp.bfloat16)
        grad_up = (grad_act * swish).astype(jnp.bfloat16)
        grad_resid = grad_out + narrow(
            contract_last(grad_gate, gate_back) + contract_last(grad_up, up_back)
        )
        attn_gain_grad = attn_gain_grad + jnp.sum(
            grad_resid * attn_raw * attn_scale[:, None], axis=0
        )
        scaled = grad_resid * attn_gain
        grad_attn = norm_grad(
            scaled, attn_raw, attn_scale, row_total(jnp.sum(scaled * attn_raw, axis=1))
        )
        wide_grad_attn = widen(grad_attn.astype(jnp.bfloat16))
        grad_heads = contract_last(wide_grad_attn, out_back).astype(jnp.bfloat16)
        dout_four = grad_heads.reshape(per_batch, slice_len, heads_here, HEAD_DIM)
        delta = jnp.sum(
            (grad_heads.astype(jnp.float32) * out_heads).reshape(
                per_batch, slice_len, heads_here, HEAD_DIM
            ),
            axis=-1,
        ).transpose(0, 2, 1)

        def attend_back(piece):
            key_piece, value_piece, seg_piece = piece
            count = key_piece.shape[1]
            key_four = key_piece.reshape(per_batch, count, heads_here, HEAD_DIM)
            value_four = value_piece.reshape(per_batch, count, heads_here, HEAD_DIM)
            allowed = allowed_pairs(seg_piece, count)
            logits = scale * jnp.einsum(
                "sqhd,skhd->shqk", query_b, key_four, preferred_element_type=jnp.float32
            )
            probs = jnp.where(allowed, jnp.exp(logits - logsum[..., None]), 0.0)
            grad_probs = jnp.einsum(
                "sqhd,skhd->shqk", dout_four, value_four, preferred_element_type=jnp.float32
            )
            grad_logits = (probs * (grad_probs - delta[..., None])).astype(jnp.bfloat16)
            grad_query = scale * jnp.einsum(
                "shqk,skhd->sqhd", grad_logits, key_four, preferred_element_type=jnp.float32
            )
            key_grad = scale * jnp.einsum(
                "shqk,sqhd->skhd", grad_logits, query_b, preferred_element_type=jnp.float32
            )
            value_grad = jnp.einsum(
                "shqk,sqhd->skhd",
                probs.astype(jnp.bfloat16),
                dout_four,
                preferred_element_type=jnp.float32,
            )
            grad_keys = key_grad.reshape(per_batch, count, heads_here * HEAD_DIM)
            grad_values = value_grad.reshape(per_batch, count, heads_here * HEAD_DIM)
            return (grad_query, grad_keys, grad_values)

        grad_query, grad_keys, grad_values = attend_back(
            (
                lax.all_gather(key_b, "ctx", axis=1, tiled=True),
                lax.all_gather(value_b, "ctx", axis=1, tiled=True),
                lax.all_gather(seg_here, "ctx", axis=1, tiled=True),
            )
        )
        key_grad_mine, value_grad_mine = (
            lax.psum_scatter(
                grad_keys.astype(jnp.bfloat16), "ctx", scatter_dimension=1, tiled=True
            ).astype(jnp.float32),
            lax.psum_scatter(
                grad_values.astype(jnp.bfloat16), "ctx", scatter_dimension=1, tiled=True
            ).astype(jnp.float32),
        )
        grad_qnorm = turn_back(
            grad_query.reshape(rows, heads_here, HEAD_DIM), cosine, sine
        ).reshape(rows, heads_here * HEAD_DIM)
        grad_knorm = turn_back(
            key_grad_mine.reshape(rows, heads_here, HEAD_DIM), cosine, sine
        ).reshape(rows, heads_here * HEAD_DIM)
        q_gain_grad = q_gain_grad + jnp.sum(grad_qnorm * query_raw * query_scale[:, None], axis=0)
        k_gain_grad = k_gain_grad + jnp.sum(grad_knorm * key_raw * key_scale[:, None], axis=0)
        q_scaled = grad_qnorm * q_gain
        k_scaled = grad_knorm * k_gain
        q_inner, k_inner = row_total(
            (jnp.sum(q_scaled * query_raw, axis=1), jnp.sum(k_scaled * key_raw, axis=1))
        )
        grad_query_raw = norm_grad(q_scaled, query_raw, query_scale, q_inner).astype(jnp.bfloat16)
        grad_key_raw = norm_grad(k_scaled, key_raw, key_scale, k_inner).astype(jnp.bfloat16)
        grad_value_raw = value_grad_mine.reshape(rows, heads_here * HEAD_DIM).astype(jnp.bfloat16)
        back_terms = (
            contract_last(grad_query_raw, query_back)
            + contract_last(grad_key_raw, key_back)
            + contract_last(grad_value_raw, value_back)
        )
        grad_in = grad_resid + narrow(back_terms)
        input_grads.append(grad_in.astype(jnp.bfloat16).reshape(per_batch, slice_len, local_width))
        fresh_grads = (
            contract_first(wide_in, grad_query_raw),
            contract_first(wide_in, grad_key_raw),
            contract_first(wide_in, grad_value_raw),
            contract_first(out_b, wide_grad_attn),
            contract_first(wide_mid, grad_gate),
            contract_first(wide_mid, grad_up),
            contract_first(act_b, wide_grad_mlp),
        )
        weight_grads = tuple((left + right for left, right in zip(weight_grads, fresh_grads)))
    finals = (
        lax.psum_scatter(
            weight_grads[0].astype(jnp.bfloat16), ("dp", "ctx"), scatter_dimension=0, tiled=True
        ).astype(jnp.float32),
        lax.psum_scatter(
            weight_grads[1].astype(jnp.bfloat16), ("dp", "ctx"), scatter_dimension=0, tiled=True
        ).astype(jnp.float32),
        lax.psum_scatter(
            weight_grads[2].astype(jnp.bfloat16), ("dp", "ctx"), scatter_dimension=0, tiled=True
        ).astype(jnp.float32),
        lax.psum_scatter(
            weight_grads[3].astype(jnp.bfloat16), ("dp", "ctx"), scatter_dimension=1, tiled=True
        ).astype(jnp.float32),
        lax.psum_scatter(
            weight_grads[4].astype(jnp.bfloat16), ("dp", "ctx"), scatter_dimension=0, tiled=True
        ).astype(jnp.float32),
        lax.psum_scatter(
            weight_grads[5].astype(jnp.bfloat16), ("dp", "ctx"), scatter_dimension=0, tiled=True
        ).astype(jnp.float32),
        lax.psum_scatter(
            weight_grads[6].astype(jnp.bfloat16), ("dp", "ctx"), scatter_dimension=1, tiled=True
        ).astype(jnp.float32),
    )
    gains = lax.psum((q_gain_grad, k_gain_grad, attn_gain_grad, mlp_gain_grad), ("dp", "ctx"))
    return (
        jnp.concatenate(outputs, axis=0),
        jnp.concatenate(input_grads, axis=0),
        finals[0],
        finals[1],
        finals[2],
        finals[3],
        finals[4],
        finals[5],
        finals[6],
        gains[0],
        gains[1],
        gains[2],
        gains[3],
    )


def solution(mesh):
    placed = (
        P("dp", "ctx", "tp"),
        P("dp", "ctx", "tp"),
        P("dp", "ctx"),
        P("dp", "ctx"),
        P(("dp", "ctx"), "tp"),
        P(("dp", "ctx"), "tp"),
        P(("dp", "ctx"), "tp"),
        P("tp", ("dp", "ctx")),
        P(("dp", "ctx"), "tp"),
        P(("dp", "ctx"), "tp"),
        P("tp", ("dp", "ctx")),
        P("tp"),
        P("tp"),
        P("tp"),
        P("tp"),
    )
    return jax.shard_map(
        local,
        mesh=mesh,
        in_specs=placed,
        out_specs=(
            P("dp", "ctx", "tp"),
            P("dp", "ctx", "tp"),
            P(("dp", "ctx"), "tp"),
            P(("dp", "ctx"), "tp"),
            P(("dp", "ctx"), "tp"),
            P("tp", ("dp", "ctx")),
            P(("dp", "ctx"), "tp"),
            P(("dp", "ctx"), "tp"),
            P("tp", ("dp", "ctx")),
            P("tp"),
            P("tp"),
            P("tp"),
            P("tp"),
        ),
        check_vma=False,
    )
```

profile of v0, /device:TPU:0, one launch (start us, length us, event | category | flops | bytes accessed | tf_op | source)
XLA Modules:
  0.0 1744.2 jit_solution(12410744278875896573)
XLA Ops:
  15.9 42.9 %all-gather.20.cloned.1.call-done = bf16[512,2048]{1,0:T(8,128)(2,1)} async-done(((bf16[512,512]{1,0:T(8,128)(2,1)}), bf16[512,2048]{1,0:T(8,128)(2,1)}) %all-gather.20.cloned.1.call-update) | async-done | bytes 2097168 | tf_op jit(solution)/shard_map/all_gather | solution.py:23
  58.8 28.5 %all-gather.22.cloned.1.call-done = bf16[2048,512]{1,0:T(8,128)(2,1)} async-done(((bf16[256,512]{1,0:T(8,128)(2,1)}), bf16[2048,512]{1,0:T(8,128)(2,1)}) %all-gather.22.cloned.1.call-update) | async-done | bytes 2097168 | tf_op jit(solution)/shard_map/all_gather | solution.py:109
  90.9 26.3 %all-gather.24.cloned.1.call-done = bf16[2048,512]{1,0:T(8,128)(2,1)} async-done(((bf16[256,512]{1,0:T(8,128)(2,1)}), bf16[2048,512]{1,0:T(8,128)(2,1)}) %all-gather.24.cloned.1.call-update) | async-done | bytes 2097168 | tf_op jit(solution)/shard_map/all_gather | solution.py:110
  121.0 44.1 %all-gather.42.cloned.1.call-done = bf16[512,2048]{1,0:T(8,128)(2,1)} async-done(((bf16[512,512]{1,0:T(8,128)(2,1)}), bf16[512,2048]{1,0:T(8,128)(2,1)}) %all-gather.42.cloned.1.call-update) | async-done | bytes 2097168 | tf_op jit(solution)/shard_map/all_gather | solution.py:23
  172.1 9.6 all-reduce.6
  269.1 9.5 all-gather.32.cloned.1.call-done
  283.3 20.1 %all-gather.26.cloned.1.call-done = bf16[2,1024,512]{2,1,0:T(8,128)(2,1)} async-done(((bf16[2,256,512]{2,1,0:T(8,128)(2,1)}), bf16[2,1024,512]{2,1,0:T(8,128)(2,1)}) %all-gather.26.cloned.1.call-update) | async-done | bytes 2097168 | tf_op jit(solution)/shard_map/all_gather | solution.py:154
  316.4 11.8 all-gather.30.cloned.1.call-done
  338.3 36.7 %reduce-scatter.24.cloned.1.call-done = bf16[512,512]{1,0:T(8,128)(2,1)} async-done(((bf16[512,2048]{1,0:T(8,128)(2,1)}), bf16[512,512]{1,0:T(8,128)(2,1)}) %reduce-scatter.24.cloned.1.call-update) | async-done | bytes 524304 | tf_op jit(solution)/shard_map/reduce_scatter | solution.py:27
  376.2 44.8 %reduce-scatter.20.cloned.1.call-done = bf16[512,512]{1,0:T(8,128)(2,1)} async-done(((bf16[512,2048]{1,0:T(8,128)(2,1)}), bf16[512,512]{1,0:T(8,128)(2,1)}) %reduce-scatter.20.cloned.1.call-update) | async-done | bytes 524304 | tf_op jit(solution)/shard_map/reduce_scatter | solution.py:27
  422.3 9.8 all-reduce.5
  437.4 41.9 %all-gather.34.cloned.1.call-done = bf16[512,2048]{1,0:T(8,128)(2,1)} async-done(((bf16[512,512]{1,0:T(8,128)(2,1)}), bf16[512,2048]{1,0:T(8,128)(2,1)}) %all-gather.34.cloned.1.call-update) | async-done | bytes 2097168 | tf_op jit(solution)/shard_map/all_gather | solution.py:23
  479.2 54.9 %all-gather.36.cloned.1.call-done = bf16[2048,2048]{1,0:T(8,128)(2,1)} async-done(((bf16[256,2048]{1,0:T(8,128)(2,1)}), bf16[2048,2048]{1,0:T(8,128)(2,1)}) %all-gather.36.cloned.1.call-update) | async-done | bytes 8388624 | tf_op jit(solution)/shard_map/all_gather | solution.py:113
  534.1 10.6 fusion.137
  544.7 45.6 %all-gather.38.cloned.1.call-done = bf16[2048,2048]{1,0:T(8,128)(2,1)} async-done(((bf16[256,2048]{1,0:T(8,128)(2,1)}), bf16[2048,2048]{1,0:T(8,128)(2,1)}) %all-gather.38.cloned.1.call-update) | async-done | bytes 8388624 | tf_op jit(solution)/shard_map/all_gather | solution.py:114
  590.3 10.8 multiply_convert_fusion.9
  601.0 46.9 %all-gather.40.cloned.1.call-done = bf16[2048,2048]{1,0:T(8,128)(2,1)} async-done(((bf16[2048,256]{1,0:T(8,128)(2,1)}), bf16[2048,2048]{1,0:T(8,128)(2,1)}) %all-gather.40.cloned.1.call-update) | async-done | bytes 8388624 | tf_op jit(solution)/shard_map/all_gather | solution.py:115
  648.0 9.8 convolution_convert_fusion.2
  658.1 37.8 %all-gather.48.cloned.1.call-done = bf16[512,2048]{1,0:T(8,128)(2,1)} async-done(((bf16[512,512]{1,0:T(8,128)(2,1)}), bf16[512,2048]{1,0:T(8,128)(2,1)}) %all-gather.48.cloned.1.call-update) | async-done | bytes 2097168 | tf_op jit(solution)/shard_map/all_gather | solution.py:23
  704.4 11.7 multiply_convert_fusion.8
  723.3 18.0 %reduce-scatter.22.cloned.1.call-done = bf16[512,512]{1,0:T(8,128)(2,1)} async-done(((bf16[512,2048]{1,0:T(8,128)(2,1)}), bf16[512,512]{1,0:T(8,128)(2,1)}) %reduce-scatter.22.cloned.1.call-update) | async-done | bytes 524304 | tf_op jit(solution)/shard_map/reduce_scatter | solution.py:27
  742.5 45.0 %reduce-scatter.26.cloned.1.call-done = bf16[512,512]{1,0:T(8,128)(2,1)} async-done(((bf16[512,2048]{1,0:T(8,128)(2,1)}), bf16[512,512]{1,0:T(8,128)(2,1)}) %reduce-scatter.26.cloned.1.call-update) | async-done | bytes 524304 | tf_op jit(solution)/shard_map/reduce_scatter | solution.py:27
  788.7 9.9 all-reduce.4
  814.1 44.1 %all-gather.54.cloned.1.call-done = bf16[512,2048]{1,0:T(8,128)(2,1)} async-done(((bf16[512,512]{1,0:T(8,128)(2,1)}), bf16[512,2048]{1,0:T(8,128)(2,1)}) %all-gather.54.cloned.1.call-update) | async-done | bytes 2097168 | tf_op jit(solution)/shard_map/all_gather | solution.py:23
  858.2 12.2 multiply_convert_fusion.3
  888.4 16.6 all-gather.50.cloned.1.call-done
  905.1 11.9 multiply_convert_fusion.6
  934.8 15.6 reduce-scatter.36.cloned.1.call-done
  950.5 46.2 %reduce-scatter.28.cloned.1.call-done = bf16[512,512]{1,0:T(8,128)(2,1)} async-done(((bf16[512,2048]{1,0:T(8,128)(2,1)}), bf16[512,512]{1,0:T(8,128)(2,1)}) %reduce-scatter.28.cloned.1.call-update) | async-done | bytes 524304 | tf_op jit(solution)/shard_map/reduce_scatter | solution.py:27
  999.8 9.8 all-reduce.2
  1014.4 43.2 %all-gather.56.cloned.1.call-done = bf16[512,2048]{1,0:T(8,128)(2,1)} async-done(((bf16[512,512]{1,0:T(8,128)(2,1)}), bf16[512,2048]{1,0:T(8,128)(2,1)}) %all-gather.56.cloned.1.call-update) | async-done | bytes 2097168 | tf_op jit(solution)/shard_map/all_gather | solution.py:23
  1076.9 27.5 %all-gather.52.cloned.1.call-done = bf16[512,2048]{1,0:T(8,128)(2,1)} async-done(((bf16[512,512]{1,0:T(8,128)(2,1)}), bf16[512,2048]{1,0:T(8,128)(2,1)}) %all-gather.52.cloned.1.call-update) | async-done | bytes 2097168 | tf_op jit(solution)/shard_map/all_gather | solution.py:23
  1151.2 12.8 fusion.150
  1164.0 10.5 add_convert_fusion
  1176.1 10.2 fusion.149
  1186.2 10.5 add_convert_fusion.1
  1196.8 10.1 fusion.148
  1206.8 10.4 add_convert_fusion.2
  1255.1 9.9 all-reduce.1
  1308.2 12.9 all-reduce
  1321.1 38.7 %reduce-scatter.56.cloned.1.call-done = bf16[2048,256]{1,0:T(8,128)(2,1)} async-done(((bf16[2048,2048]{1,0:T(8,128)(2,1)}), bf16[2048,256]{1,0:T(8,128)(2,1)}) %reduce-scatter.56.cloned.1.call-update) | async-done | bytes 1048592 | tf_op jit(solution)/shard_map/reduce_scatter | solution.py:332
  1362.6 72.1 %reduce-scatter.54.cloned.1.call-done = bf16[256,2048]{1,0:T(8,128)(2,1)} async-done(((bf16[2048,2048]{1,0:T(8,128)(2,1)}), bf16[256,2048]{1,0:T(8,128)(2,1)}) %reduce-scatter.54.cloned.1.call-update) | async-done | bytes 1048592 | tf_op jit(solution)/shard_map/reduce_scatter | solution.py:329
  1437.4 72.2 %reduce-scatter.52.cloned.1.call-done = bf16[256,2048]{1,0:T(8,128)(2,1)} async-done(((bf16[2048,2048]{1,0:T(8,128)(2,1)}), bf16[256,2048]{1,0:T(8,128)(2,1)}) %reduce-scatter.52.cloned.1.call-update) | async-done | bytes 1048592 | tf_op jit(solution)/shard_map/reduce_scatter | solution.py:326
  1512.4 41.8 %reduce-scatter.46.cloned.1.call-done = bf16[256,512]{0,1:T(8,128)(2,1)} async-done(((bf16[2048,512]{0,1:T(8,128)(2,1)}), bf16[256,512]{0,1:T(8,128)(2,1)}) %reduce-scatter.46.cloned.1.call-update) | async-done | bytes 262160 | tf_op jit(solution)/shard_map/reduce_scatter | solution.py:317
  1556.1 43.0 %reduce-scatter.44.cloned.1.call-done = bf16[256,512]{0,1:T(8,128)(2,1)} async-done(((bf16[2048,512]{0,1:T(8,128)(2,1)}), bf16[256,512]{0,1:T(8,128)(2,1)}) %reduce-scatter.44.cloned.1.call-update) | async-done | bytes 262160 | tf_op jit(solution)/shard_map/reduce_scatter | solution.py:314
  1601.0 42.5 %reduce-scatter.48.cloned.1.call-done = bf16[256,512]{0,1:T(8,128)(2,1)} async-done(((bf16[2048,512]{0,1:T(8,128)(2,1)}), bf16[256,512]{0,1:T(8,128)(2,1)}) %reduce-scatter.48.cloned.1.call-update) | async-done | bytes 262160 | tf_op jit(solution)/shard_map/reduce_scatter | solution.py:320
  1645.3 44.3 %reduce-scatter.42.cloned.1.call-done = bf16[512,512]{1,0:T(8,128)(2,1)} async-done(((bf16[512,2048]{1,0:T(8,128)(2,1)}), bf16[512,512]{1,0:T(8,128)(2,1)}) %reduce-scatter.42.cloned.1.call-update) | async-done | bytes 524304 | tf_op jit(solution)/shard_map/reduce_scatter | solution.py:27
  1690.9 44.2 %reduce-scatter.34.cloned.1.call-done = bf16[512,512]{1,0:T(8,128)(2,1)} async-done(((bf16[512,2048]{1,0:T(8,128)(2,1)}), bf16[512,512]{1,0:T(8,128)(2,1)}) %reduce-scatter.34.cloned.1.call-update) | async-done | bytes 524304 | tf_op jit(solution)/shard_map/reduce_scatter | solution.py:27
  (501 shorter events, 387.8 us)
Async XLA Ops:
  7.2 51.7 %all-gather.20.cloned.1.call-start = ((), (), s32[]{:S(2)}) async-start(), calls=%async_computation.19 | async-start | bytes 2621440 | tf_op jit(solution)/shard_map/all_gather | solution.py:23
  9.5 77.9 %all-gather.22.cloned.1.call-start = ((), (), s32[]{:S(2)}) async-start(), calls=%async_computation.20 | async-start | bytes 2359296 | tf_op jit(solution)/shard_map/all_gather | solution.py:109
  10.2 106.9 %all-gather.24.cloned.1.call-start = ((), (), s32[]{:S(2)}) async-start(), calls=%async_computation.21 | async-start | bytes 2359296 | tf_op jit(solution)/shard_map/all_gather | solution.py:110
  11.0 154.2 %all-gather.42.cloned.1.call-start = ((), (), s32[]{:S(2)}) async-start(), calls=%async_computation.32 | async-start | bytes 2621440 | tf_op jit(solution)/shard_map/all_gather | solution.py:23
  11.5 190.8 %all-gather.28.cloned.1.call-start = ((), (), s32[]{:S(2)}) async-start(), calls=%async_computation.23 | async-start | bytes 2359296 | tf_op jit(solution)/shard_map/all_gather | solution.py:111
  12.1 237.0 %all-gather.44.cloned.1.call-start = ((), (), s32[]{:S(2)}) async-start(), calls=%async_computation.33 | async-start | bytes 2621440 | tf_op jit(solution)/shard_map/all_gather | solution.py:154
  15.9 207.7 %copy-start.61 = (f32[512,64]{1,0:T(8,128)}, f32[512,64]{1,0:T(8,128)S(1)}, u32[]{:S(2)}) copy-start(f32[512,64]{1,0:T(8,128)S(1)} %get-tuple-element.157) | copy-start | bytes 393220
  202.3 60.0 %all-gather.46.cloned.1.call-start = ((), (), s32[]{:S(2)}) async-start(), calls=%async_computation.34 | async-start | bytes 2621440 | tf_op jit(solution)/shard_map/all_gather | solution.py:155
  208.7 69.9 %all-gather.32.cloned.1.call-start = ((), (), s32[]{:S(2)}) async-start(), calls=%async_computation.25 | async-start | bytes 2359296 | tf_op jit(solution)/shard_map/all_gather | solution.py:112
  209.5 93.9 %all-gather.26.cloned.1.call-start = ((), (), s32[]{:S(2)}) async-start(), calls=%async_computation.22 | async-start | bytes 2621440 | tf_op jit(solution)/shard_map/all_gather | solution.py:154
  231.0 97.3 %all-gather.30.cloned.1.call-start = ((), (), s32[]{:S(2)}) async-start(), calls=%async_computation.24 | async-start | bytes 2621440 | tf_op jit(solution)/shard_map/all_gather | solution.py:155
  247.4 127.6 %reduce-scatter.24.cloned.1.call-start = ((), (), s32[]{:S(2)}) async-start(), calls=%async_computation.35 | async-start | bytes 2621440 | tf_op jit(solution)/shard_map/reduce_scatter | solution.py:27
  282.8 138.2 %reduce-scatter.20.cloned.1.call-start = ((), (), s32[]{:S(2)}) async-start(), calls=%async_computation.26 | async-start | bytes 2621440 | tf_op jit(solution)/shard_map/reduce_scatter | solution.py:27
  335.6 96.5 %copy-start.27 = (bf16[2,256,512]{2,1,0:T(8,128)(2,1)S(1)}, bf16[2,256,512]{2,1,0:T(8,128)(2,1)}, u32[]{:S(2)}) copy-start(bf16[2,256,512]{2,1,0:T(8,128)(2,1)} %get-tuple-element.136) | copy-start | bytes 1572868
  335.6 96.5 %copy-start.95 = (f32[512]{0:T(512)S(1)}, f32[512]{0:T(512)}, u32[]{:S(2)}) copy-start(f32[512]{0:T(512)} %param.28) | copy-start | bytes 6148
  338.3 141.0 %all-gather.34.cloned.1.call-start = ((), (), s32[]{:S(2)}) async-start(), calls=%async_computation.27 | async-start | bytes 2621440 | tf_op jit(solution)/shard_map/all_gather | solution.py:23
  434.8 99.3 %all-gather.36.cloned.1.call-start = ((), (), s32[]{:S(2)}) async-start(), calls=%async_computation.28 | async-start | bytes 9437184 | tf_op jit(solution)/shard_map/all_gather | solution.py:113
  435.4 154.9 %all-gather.38.cloned.1.call-start = ((), (), s32[]{:S(2)}) async-start(), calls=%async_computation.29 | async-start | bytes 9437184 | tf_op jit(solution)/shard_map/all_gather | solution.py:114
  436.0 212.0 %all-gather.40.cloned.1.call-start = ((), (), s32[]{:S(2)}) async-start(), calls=%async_computation.30 | async-start | bytes 9437184 | tf_op jit(solution)/shard_map/all_gather | solution.py:115
  436.6 259.3 %all-gather.48.cloned.1.call-start = ((), (), s32[]{:S(2)}) async-start(), calls=%async_computation.36 | async-start | bytes 2621440 | tf_op jit(solution)/shard_map/all_gather | solution.py:23
  437.1 304.1 %reduce-scatter.22.cloned.1.call-start = ((), (), s32[]{:S(2)}) async-start(), calls=%async_computation.31 | async-start | bytes 2621440 | tf_op jit(solution)/shard_map/reduce_scatter | solution.py:27
  479.2 111.0 %copy-start.110 = (bf16[512,2048]{1,0:T(8,128)(2,1)S(1)}, bf16[512,2048]{1,0:T(8,128)(2,1)}, u32[]{:S(2)}) copy-start(bf16[512,2048]{1,0:T(8,128)(2,1)} %all-gather.34.cloned.1.call-done) | copy-start | bytes 6291460
  657.8 129.6 %reduce-scatter.26.cloned.1.call-start = ((), (), s32[]{:S(2)}) async-start(), calls=%async_computation.37 | async-start | bytes 2621440 | tf_op jit(solution)/shard_map/reduce_scatter | solution.py:27
  723.2 135.1 %all-gather.54.cloned.1.call-start = ((), (), s32[]{:S(2)}) async-start(), calls=%async_computation.44 | async-start | bytes 2621440 | tf_op jit(solution)/shard_map/all_gather | solution.py:23
  723.3 286.3 %copy-start.5 = (bf16[2,256,512]{2,1,0:T(8,128)(2,1)}, bf16[2,256,512]{2,1,0:T(8,128)(2,1)S(1)}, u32[]{:S(2)}) copy-start(bf16[2,256,512]{2,1,0:T(8,128)(2,1)S(1)} %get-tuple-element.125) | copy-start | bytes 1572868
  723.3 286.3 %copy-start.7 = (bf16[2,256,512]{2,1,0:T(8,128)(2,1)}, bf16[2,256,512]{2,1,0:T(8,128)(2,1)S(1)}, u32[]{:S(2)}) copy-start(bf16[2,256,512]{2,1,0:T(8,128)(2,1)S(1)} %get-tuple-element.126) | copy-start | bytes 1572868
  812.9 92.1 %all-gather.50.cloned.1.call-start = ((), (), s32[]{:S(2)}) async-start(), calls=%async_computation.38 | async-start | bytes 2621440 | tf_op jit(solution)/shard_map/all_gather | solution.py:23
  813.7 136.8 %reduce-scatter.36.cloned.1.call-start = ((), (), s32[]{:S(2)}) async-start(), calls=%async_computation.45 | async-start | bytes 2621440 | tf_op jit(solution)/shard_map/reduce_scatter | solution.py:27
  888.2 108.5 %reduce-scatter.28.cloned.1.call-start = ((), (), s32[]{:S(2)}) async-start(), calls=%async_computation.39 | async-start | bytes 2621440 | tf_op jit(solution)/shard_map/reduce_scatter | solution.py:27
  934.8 122.7 %all-gather.56.cloned.1.call-start = ((), (), s32[]{:S(2)}) async-start(), calls=%async_computation.46 | async-start | bytes 2621440 | tf_op jit(solution)/shard_map/all_gather | solution.py:23
  1013.1 91.3 %all-gather.52.cloned.1.call-start = ((), (), s32[]{:S(2)}) async-start(), calls=%async_computation.40 | async-start | bytes 2621440 | tf_op jit(solution)/shard_map/all_gather | solution.py:23
  1013.9 213.8 %reduce-scatter.38.cloned.1.call-start = ((), (), s32[]{:S(2)}) async-start(), calls=%async_computation.47 | async-start | bytes 2621440 | tf_op jit(solution)/shard_map/reduce_scatter | solution.py:273
  1076.8 162.6 %reduce-scatter.30.cloned.1.call-start = ((), (), s32[]{:S(2)}) async-start(), calls=%async_computation.41 | async-start | bytes 2621440 | tf_op jit(solution)/shard_map/reduce_scatter | solution.py:273
  1125.3 154.2 %reduce-scatter.32.cloned.1.call-start = ((), (), s32[]{:S(2)}) async-start(), calls=%async_computation.42 | async-start | bytes 2621440 | tf_op jit(solution)/shard_map/reduce_scatter | solution.py:276
  1133.9 150.0 %reduce-scatter.40.cloned.1.call-start = ((), (), s32[]{:S(2)}) async-start(), calls=%async_computation.48 | async-start | bytes 2621440 | tf_op jit(solution)/shard_map/reduce_scatter | solution.py:276
  1144.9 161.5 %reduce-scatter.50.cloned.1.call-start = ((), (), s32[]{:S(2)}) async-start(), calls=%async_computation.53 | async-start | bytes 2359296 | tf_op jit(solution)/shard_map/reduce_scatter | solution.py:323
  1151.1 208.7 %reduce-scatter.56.cloned.1.call-start = ((), (), s32[]{:S(2)}) async-start(), calls=%async_computation.56 | async-start | bytes 9437184 | tf_op jit(solution)/shard_map/reduce_scatter | solution.py:332
  1174.5 260.2 %reduce-scatter.54.cloned.1.call-start = ((), (), s32[]{:S(2)}) async-start(), calls=%async_computation.55 | async-start | bytes 9437184 | tf_op jit(solution)/shard_map/reduce_scatter | solution.py:329
  1196.7 312.9 %reduce-scatter.52.cloned.1.call-start = ((), (), s32[]{:S(2)}) async-start(), calls=%async_computation.54 | async-start | bytes 9437184 | tf_op jit(solution)/shard_map/reduce_scatter | solution.py:326
  1217.3 336.9 %reduce-scatter.46.cloned.1.call-start = ((), (), s32[]{:S(2)}) async-start(), calls=%async_computation.51 | async-start | bytes 2359296 | tf_op jit(solution)/shard_map/reduce_scatter | solution.py:317
  1272.3 326.8 %reduce-scatter.44.cloned.1.call-start = ((), (), s32[]{:S(2)}) async-start(), calls=%async_computation.50 | async-start | bytes 2359296 | tf_op jit(solution)/shard_map/reduce_scatter | solution.py:314
  1279.5 364.0 %reduce-scatter.48.cloned.1.call-start = ((), (), s32[]{:S(2)}) async-start(), calls=%async_computation.52 | async-start | bytes 2359296 | tf_op jit(solution)/shard_map/reduce_scatter | solution.py:320
  1289.6 400.1 %reduce-scatter.42.cloned.1.call-start = ((), (), s32[]{:S(2)}) async-start(), calls=%async_computation.49 | async-start | bytes 2621440 | tf_op jit(solution)/shard_map/reduce_scatter | solution.py:27
  1297.6 437.5 %reduce-scatter.34.cloned.1.call-start = ((), (), s32[]{:S(2)}) async-start(), calls=%async_computation.43 | async-start | bytes 2621440 | tf_op jit(solution)/shard_map/reduce_scatter | solution.py:27
  1362.6 327.1 %copy-start.8 = (bf16[2,256,512]{2,1,0:T(8,128)(2,1)S(1)}, bf16[2,256,512]{2,1,0:T(8,128)(2,1)}, u32[]{:S(2)}) copy-start(bf16[2,256,512]{2,1,0:T(8,128)(2,1)} %copy-done.7) | copy-start | bytes 1572868
  1362.6 327.1 %copy-start.39 = (bf16[512,512]{1,0:T(8,128)(2,1)S(1)}, bf16[512,512]{1,0:T(8,128)(2,1)}, u32[]{:S(2)}) copy-start(bf16[512,512]{1,0:T(8,128)(2,1)} %reduce-scatter.36.cloned.1.call-done) | copy-start | bytes 1572868
  1437.4 297.7 %copy-start.6 = (bf16[2,256,512]{2,1,0:T(8,128)(2,1)S(1)}, bf16[2,256,512]{2,1,0:T(8,128)(2,1)}, u32[]{:S(2)}) copy-start(bf16[2,256,512]{2,1,0:T(8,128)(2,1)} %copy-done.5) | copy-start | bytes 1572868
  1437.4 297.7 %copy-start.40 = (bf16[512,512]{1,0:T(8,128)(2,1)S(1)}, bf16[512,512]{1,0:T(8,128)(2,1)}, u32[]{:S(2)}) copy-start(bf16[512,512]{1,0:T(8,128)(2,1)} %reduce-scatter.28.cloned.1.call-done) | copy-start | bytes 1572868
  (117 other events, 1252.9 us)
Sparse Core Ops, SparseCore 0:
  10.2 48.6 all-gather.19
  60.7 26.5 all-gather.21
  89.3 27.8 all-gather.23
  119.2 45.9 all-gather.41
  166.9 26.6 all-gather.27
  202.4 21.0 all-gather.43
  225.6 22.8 all-gather.45
  250.4 28.1 all-gather.31
  280.8 22.5 all-gather.25
  305.3 22.8 all-gather.29
  331.1 43.8 reduce-scatter.23
  377.9 43.1 reduce-scatter.19
  434.9 44.2 all-gather.33
  481.0 53.0 all-gather.35
  535.8 54.3 all-gather.37
  592.0 55.9 all-gather.39
  650.0 45.8 all-gather.47
  698.6 42.6 reduce-scatter.21
  744.2 43.1 reduce-scatter.25
  813.0 45.1 all-gather.53
  860.4 44.6 all-gather.49
  907.9 42.4 reduce-scatter.35
  953.4 43.1 reduce-scatter.27
  1013.2 44.2 all-gather.55
  1059.7 44.6 all-gather.51
  1107.3 30.1 reduce-scatter.37
  1140.6 31.4 reduce-scatter.29
  1174.6 31.4 reduce-scatter.31
  1208.8 31.4 reduce-scatter.39
  1243.4 41.2 reduce-scatter.49
  1288.5 71.2 reduce-scatter.55
  1363.3 71.2 reduce-scatter.53
  1438.3 71.2 reduce-scatter.51
  1512.9 41.2 reduce-scatter.45
  1557.8 41.2 reduce-scatter.43
  1602.2 41.2 reduce-scatter.47
  1645.7 43.8 reduce-scatter.41
  1691.9 43.1 reduce-scatter.33
where the time goes:
time: 1750 us; the launch traced here: 1740 us
  waiting for transfers between devices  1150 us (66%)
  matrix products  313 us (18%)
  local copies, waits for them, and re-layouts  98.2 us (6%)
  blocking collectives  81.1 us (5%)
  other arithmetic  77.6 us (4%)
    all_gather x8, waiting for transfers between devices, widen(): return lax.all_gather(value, 'tp', axis=1, tiled=True)  298 us
    reduce_scatter x8, waiting for transfers between devices, narrow(): lax.psum_scatter(value.astype(jnp.bfloat16), 'tp', scatter_dimension=1, t...  295 us
    dot_general x14, matrix products, contract_first(): lax.dot_general(left, right, (((0,), (0,)), ((), ())), preferred_element_...  88 us
    dot_general x14, matrix products, contract_last(): lax.dot_general(left, right, (((1,), (1,)), ((), ())), preferred_element_...  82.5 us
    reduce_scatter x1, waiting for transfers between devices, local(): lax.psum_scatter(weight_grads[4].astype(jnp.bfloat16), ('dp', 'ctx'), sca...  72.2 us
    reduce_scatter x1, waiting for transfers between devices, local(): lax.psum_scatter(weight_grads[5].astype(jnp.bfloat16), ('dp', 'ctx'), sca...  72.1 us
    psum x6, blocking collectives, row_total(): return lax.psum(value, 'tp')  57.9 us
    all_gather x1, waiting for transfers between devices, local(): lax.all_gather(w_gate, ('dp', 'ctx'), axis=0, tiled=True)  54.9 us
  transfers between devices with their start and end apart: 38, of which 30 were waited for; matrix products, arithmetic and copies ran while one was open for 26% of the time, Pallas kernels for 0%

commit v1 on v0

--- a/solution.py
+++ b/solution.py
@@ -1,54 +1,525 @@
+import functools
 import math
 
 import jax
 import jax.numpy as jnp
 from jax import lax
+from jax.experimental import pallas as pl
+from jax.experimental.pallas import tpu as pltpu
 from jax.sharding import PartitionSpec as P
 
 D = 2048
 HEAD_DIM = 128
-MICRO = 2
-
-
 EPS = 1e-06
 THETA = 500000.0
 NEG = -1e30
-
-
-def row_total(value):
+BF = jnp.bfloat16
+F32 = jnp.float32
+MESH = pl.DeviceIdType.MESH
+HBM = pl.BlockSpec(memory_space=pltpu.HBM)
+
+
+class Sems:
+    def __init__(self):
+        self.count = 0
+        self.ref = None
+
+    def take(self, number):
+        first = self.count
+        self.count += number
+        return first
+
+    def at(self, index):
+        return self.ref.at[index]
+
+
+def when(cond, body):
+    if cond is None:
+        body()
+    else:
+        pl.when(cond)(body)
+
+
+def both(a, b):
+    if a is None:
+        return b
+    if b is None:
+        return a
+    return jnp.logical_and(a, b)
+
+
+class Place:
+    def __init__(self, tp_size):
+        self.n = tp_size
+        self.tp = lax.axis_index("tp")
+        self.dp = lax.axis_index("dp")
+        self.ctx = lax.axis_index("ctx")
+        self.slot = self.dp * 4 + self.ctx
+
+
+class Task:
+    inputs = ()
+    outputs = ()
+    scratch = ()
+    sems = 0
+    axes = ()
+
+    def emit(self, place, ins, outs, scr, sem):
+        raise NotImplementedError
+
+
+def remote(src, dst, sem, send, recv, device):
+    return pltpu.make_async_remote_copy(
+        src_ref=src, dst_ref=dst, send_sem=sem.at(send), recv_sem=sem.at(recv), device_id=device, device_id_type=MESH
+    )
+
+
+class LineGather(Task):
+    axes = ("tp",)
+
+    def __init__(self, array, n, pieces=2):
+        self.n, self.pieces = n, pieces
+        rows, width = array.shape
+        self.rows, self.width = rows, width
+        self.inputs = (array,)
+        self.outputs = (jax.ShapeDtypeStruct((rows, n * width), array.dtype),)
+        self.scratch = ()
+        self.sems = 1 + 4 * (n - 1) * pieces
+        self.unit = rows * width * 2 * 2 / 88e3
+
+    def emit(self, place, ins, outs, scr, sem):
+        n, pieces, width = self.n, self.pieces, self.width
+        step = self.rows // pieces
+        src, out = ins[0], outs[0]
+        me = place.tp
+
+        def spot(chunk, piece):
+            return out.at[pl.ds(piece * step, step), pl.ds(pl.multiple_of(chunk * width, width), width)]
+
+        own = pltpu.make_async_copy(src, out.at[:, pl.ds(pl.multiple_of(me * width, width), width)], sem.at(0))
+        own.start()
+        sends = []
+        for s in range(n):
+            for piece in range(pieces):
+                for way in (0, 1):
+                    have = None if s == 0 else (me >= s if way == 0 else me + s < n)
+                    edge = me < n - 1 if way == 0 else me > 0
+                    chunk = me - s if way == 0 else me + s
+                    index = 1 + 2 * (((s * 2 + way) * pieces) + piece)
+                    if s > 0:
+                        prev = 1 + 2 * ((((s - 1) * 2 + way) * pieces) + piece)
+                        got = remote(spot(chunk, piece), spot(chunk, piece), sem, prev, prev + 1, {"tp": me})
+                        when(have, got.wait_recv)
+                    if s < n - 1:
+                        origin = src.at[pl.ds(piece * step, step)] if s == 0 else spot(chunk, piece)
+                        to = me + 1 if way == 0 else me - 1
+                        copy = remote(origin, spot(chunk, piece), sem, index, index + 1, {"tp": to})
+                        cond = both(have, edge)
+                        when(cond, copy.start)
+                        sends.append((cond, copy))
+                yield (s + (piece + 1) / pieces) * self.unit * 1.33
+        for cond, copy in sends:
+            when(cond, copy.wait_send)
+        own.wait()
+
+
+class LineScatter(Task):
+    axes = ("tp",)
+
+    def __init__(self, array, n, pieces=2):
+        self.n, self.pieces = n, pieces
+        rows, wide = array.shape
+        width = wide // n
+        self.rows, self.width = rows, width
+        self.inputs = (array,)
+        self.outputs = (jax.ShapeDtypeStruct((rows, width), F32),)
+        self.scratch = (
+            pltpu.VMEM((n, rows, width), BF),
+            pltpu.VMEM((2, n - 1, rows, width), BF),
+            pltpu.VMEM((rows, width), F32),
+        )
+        self.sems = n + 4 * (n - 1) * pieces + 1
+        self.unit = rows * width * 2 * 2 / 88e3
+
+    def emit(self, place, ins, outs, scr, sem):
+        n, pieces, width = self.n, self.pieces, self.width
+        step = self.rows // pieces
+        src, out = ins[0], outs[0]
+        mine, came, total = scr
+        me = place.tp
+        loads = []
+        for c in range(n):
+            load = pltpu.make_async_copy(src.at[:, pl.ds(c * width, width)], mine.at[c], sem.at(c))
+            load.start()
+            loads.append(load)
+        for load in loads:
+            load.wait()
+        sends = []
+        tile = min(64, step)
+
+        def add_into(c, way, k, piece):
+            @pl.loop(0, step // tile)
+            def _(i):
+                rows = pl.ds(pl.multiple_of(piece * step + i * tile, tile), tile)
+                mine[c, rows] = (mine[c, rows].astype(F32) + came[way, k, rows].astype(F32)).astype(BF)
+
+        for k in range(n - 1):
+            for piece in range(pieces):
+                rows = pl.ds(piece * step, step)
+                for way in (0, 1):
+                    index = n + 2 * (((k * 2 + way) * pieces) + piece)
+                    dest = n - 1 - k if way == 0 else k
+                    sending = me < dest if way == 0 else me > dest
+                    inner = me > 0 if way == 0 else me < n - 1
+                    to = me + 1 if way == 0 else me - 1
+                    copy = remote(mine.at[dest, rows], came.at[way, k, rows], sem, index, index + 1, {"tp": to})
+
+                    def take(copy=copy, dest=dest, way=way, k=k, piece=piece):
+                        copy.wait_recv()
+                        add_into(dest, way, k, piece)
+
+                    when(both(sending, inner), take)
+                    when(sending, copy.start)
+                    sends.append((sending, copy))
+                yield (k + 1.2 + piece / pieces) * self.unit * 1.33
+        for piece in range(pieces):
+            rows = pl.ds(piece * step, step)
+            for way in (0, 1):
+                inner = me > 0 if way == 0 else me < n - 1
+                k = n - 1 - me if way == 0 else me
+                base = n + 2 * ((k * 2 + way) * pieces + piece)
+                got = pltpu.make_async_remote_copy(
+                    src_ref=came.at[way, k, rows],
+                    dst_ref=came.at[way, k, rows],
+                    send_sem=sem.at(base),
+                    recv_sem=sem.at(base + 1),
+                    device_id={"tp": me},
+                    device_id_type=MESH,
+                )
+                when(inner, got.wait_recv)
+
+            @pl.loop(0, step // tile)
+            def _(i):
+                part = pl.ds(pl.multiple_of(piece * step + i * tile, tile), tile)
+                total[part] = mine[me, part].astype(F32)
+
+            for way in (0, 1):
+                inner = me > 0 if way == 0 else me < n - 1
+                k = n - 1 - me if way == 0 else me
+
+                def fold(way=way, k=k):
+                    @pl.loop(0, step // tile)
+                    def _(i):
+                        part = pl.ds(pl.multiple_of(piece * step + i * tile, tile), tile)
+                        total[part] = total[part] + came[way, k, part].astype(F32)
+
+                when(inner, fold)
+        last = pltpu.make_async_copy(total, out, sem.at(self.sems - 1))
+        last.start()
+        for cond, copy in sends:
+            when(cond, copy.wait_send)
+        last.wait()
+
+
+class PlaneGather(Task):
+    def __init__(self, array, dim, with_dp, rank=0.0):
+        self.dim, self.with_dp, self.rank = dim, with_dp, rank
+        self.inputs = (array,)
+        shape = list(array.shape)
+        self.size = shape[dim]
+        self.rows = shape[0]
+        self.blocks = 8 if with_dp else 4
+        shape[dim] *= self.blocks
+        self.outputs = (jax.ShapeDtypeStruct(tuple(shape), array.dtype),)
+        self.axes = ("ctx", "dp") if with_dp else ("ctx",)
+        self.sems = 1 + 2 * (3 + 2 + 2 + 2 + 2)
+        self.unit = math.prod(array.shape) * 2 * 2 / 88e3
+
+    def emit(self, place, ins, outs, scr, sem):
+        src, out = ins[0], outs[0]
+        dp, ctx = place.dp, place.ctx
+        half = self.rows // 2
+
+        def spot(d, c, part=None):
+            block = d * 4 + c if self.with_dp else c
+            where = pl.ds(pl.multiple_of(block * self.size, self.size), self.size)
+            if self.dim == 1:
+                if part is None:
+                    return out.at[:, where]
+                return out.at[pl.ds(part * half, half), where]
+            if part is None:
+                return out.at[where]
+            return out.at[pl.ds(pl.multiple_of(block * self.size + part * half, half), half)]
+
+        xdev, ydev, cdev = {"ctx": ctx ^ 2}, {"dp": dp ^ 1}, {"ctx": ctx ^ 1}
+        mine = spot(dp, ctx)
+        own = pltpu.make_async_copy(src, mine, sem.at(0))
+        own.start()
+        sends = []
+
+        def send(index, origin, target, device):
+            copy = remote(origin, target, sem, 1 + 2 * index, 2 + 2 * index, device)
+            copy.start()
+            sends.append(copy)
+
+        def got(index, target):
+            remote(target, target, sem, 1 + 2 * index, 2 + 2 * index, cdev).wait_recv()
+
+        send(0, src, mine, xdev)
+        if self.with_dp:
+            send(1, src, mine, ydev)
+        send(2, src, mine, cdev)
+        yield self.rank + self.unit * 1.0
+        from_x = spot(dp, ctx ^ 2)
+        got(0, from_x)
+        if self.with_dp:
+            send(3, spot(dp, ctx ^ 2, 0), spot(dp, ctx ^ 2, 0), ydev)
+        send(5, from_x, from_x, cdev)
+        if self.with_dp:
+            from_y = spot(dp ^ 1, ctx)
+            got(1, from_y)
+            send(4, spot(dp ^ 1, ctx, 1), spot(dp ^ 1, ctx, 1), xdev)
+            send(6, from_y, from_y, cdev)
+            yield self.rank + self.unit * 1.5
+            for part in (0, 1):
+                diagonal = spot(dp ^ 1, ctx ^ 2, part)
+                got(3 + part, diagonal)
+                send(7 + part, diagonal, diagonal, cdev)
+        yield self.rank + self.unit * 1.6
+        got(2, spot(dp, ctx ^ 1))
+        got(5, spot(dp, ctx ^ 3))
+        if self.with_dp:
+            got(6, spot(dp ^ 1, ctx ^ 1))
+            for part in (0, 1):
+                got(7 + part, spot(dp ^ 1, ctx ^ 3, part))
+        for copy in sends:
+            copy.wait_send()
+        own.wait()
+
+
+class PlaneScatter(Task):
+    def __init__(self, array, dim, with_dp, rank=0.0):
+        self.dim, self.with_dp, self.rank = dim, with_dp, rank
+        self.inputs = (array,)
+        shape = list(array.shape)
+        self.blocks = 8 if with_dp else 4
+        shape[dim] //= self.blocks
+        self.size = shape[dim]
+        self.rows, self.width = shape
+        self.outputs = (jax.ShapeDtypeStruct(tuple(shape), F32),)
+        self.axes = ("ctx", "dp") if with_dp else ("ctx",)
+        chips = self.blocks // 2
+        self.chips = chips
+        block = (self.rows, self.width)
+        self.scratch = (
+            pltpu.VMEM((chips,) + block, BF),
+            pltpu.VMEM((chips,) + block, BF),
+            pltpu.VMEM((2,) + block, BF),
+            pltpu.VMEM((self.rows, self.width), BF),
+            pltpu.VMEM(block, F32),
+        )
+        self.sems = 2 * chips + chips + 1 + 2 * 6
+        self.unit = self.rows * self.width * 2 * 2 / 88e3
+
+    def emit(self, place, ins, outs, scr, sem):
+        src, out = ins[0], outs[0]
+        mine, came, chip_in, diag_in, total = scr
+        dp, ctx = place.dp, place.ctx
+        core = ctx & 1
+        chips = self.chips
+        half = self.rows // 2
+        tile = min(32, half)
+        xdev, ydev, cdev = {"ctx": ctx ^ 2}, {"dp": dp ^ 1}, {"ctx": ctx ^ 1}
+
+        def place_of(q):
+            x = (ctx >> 1) ^ (q & 1)
+            d = dp ^ (q >> 1)
+            return d, x
+
+        def spot(q, c):
+            d, x = place_of(q)
+            block = d * 4 + x * 2 + c if self.with_dp else x * 2 + c
+            where = pl.ds(pl.multiple_of(block * self.size, self.size), self.size)
+            return src.at[:, where] if self.dim == 1 else src.at[where]
+
+        order = (3, 1, 2, 0) if self.with_dp else (1, 0)
+        sends = []
+        loads = {}
+        for q in order:
+            copy = remote(spot(q, core ^ 1), came.at[q], sem, 2 * q, 2 * q + 1, cdev)
+            copy.start()
+            sends.append(copy)
+            load = pltpu.make_async_copy(spot(q, core), mine.at[q], sem.at(2 * chips + q))
+            load.start()
+            loads[q] = (load, copy)
+        base = 3 * chips + 1
+
+        def hop(index, origin, target, device):
+            copy = remote(origin, target, sem, base + 2 * index, base + 2 * index + 1, device)
+            copy.start()
+            sends.append(copy)
+            return copy
+
+        def got(index, target):
+            remote(target, target, sem, base + 2 * index, base + 2 * index + 1, cdev).wait_recv()
+
+        def add(into, other, first, count):
+            @pl.loop(0, count // tile)
+            def _(i):
+                part = pl.ds(pl.multiple_of(first + i * tile, tile), tile)
+                into[part] = (into[part].astype(F32) + other[part].astype(F32)).astype(BF)
+
+        top, low = pl.ds(0, half), pl.ds(half, half)
+        yield self.rank + 4.0
+        for q in order:
+            load, copy = loads[q]
+            load.wait()
+            copy.wait_recv()
+            add(mine.at[q], came.at[q], 0, self.rows)
+            if q == 3:
+                hop(0, mine.at[3, top], diag_in.at[top], xdev)
+                hop(1, mine.at[3, low], diag_in.at[low], ydev)
+            if q == 1 and self.with_dp:
+                hop(2, mine.at[1, top], chip_in.at[0, top], xdev)
+            if q == 1 and not self.with_dp:
+                hop(2, mine.at[1], chip_in.at[0], xdev)
+            if q == 2:
+                hop(3, mine.at[2, low], chip_in.at[1, low], ydev)
+        if self.with_dp:
+            yield self.rank + 4.0 + self.unit * 0.7
+            got(0, diag_in.at[top])
+            add(mine.at[2], diag_in, 0, half)
+            hop(4, mine.at[2, top], chip_in.at[1, top], ydev)
+            got(1, diag_in.at[low])
+            add(mine.at[1], diag_in, half, half)
+            hop(5, mine.at[1, low], chip_in.at[0, low], xdev)
+        yield self.rank + 4.0 + self.unit * 1.6
+        if self.with_dp:
+            got(2, chip_in.at[0, top])
+            got(5, chip_in.at[0, low])
+            got(3, chip_in.at[1, low])
+            got(4, chip_in.at[1, top])
+        else:
+            got(2, chip_in.at[0])
+
+        @pl.loop(0, self.rows // tile)
+        def _(i):
+            part = pl.ds(pl.multiple_of(i * tile, tile), tile)
+            value = mine[0, part].astype(F32) + chip_in[0, part].astype(F32)
+            if self.with_dp:
+                value = value + chip_in[1, part].astype(F32)
+            total[part] = value
+
+        last = pltpu.make_async_copy(total, out, sem.at(3 * chips))
+        last.start()
+        for copy in sends:
+            copy.wait_send()
+        last.wait()
+
+
+def run_tasks(name, ident, tp_size, tasks):
+    sems = Sems()
+    firsts = [sems.take(task.sems) for task in tasks]
+    inputs = [a for task in tasks for a in task.inputs]
+    outputs = [o for task in tasks for o in task.outputs]
+    scratch = [s for task in tasks for s in task.scratch]
+    axes = set(a for task in tasks for a in task.axes)
+
+    def kernel(*refs):
+        place = Place(tp_size)
+        ins, rest = list(refs[: len(inputs)]), list(refs[len(inputs) :])
+        outs, rest = rest[: len(outputs)], rest[len(outputs) :]
+        scr, sem_ref = rest[: len(scratch)], rest[len(scratch)]
+        barrier = pltpu.get_barrier_semaphore()
+
+        def greet(device):
+            pl.semaphore_signal(barrier, inc=1, device_id=device, device_id_type=MESH)
+
+        fixed = 0
+        if "ctx" in axes:
+            greet({"ctx": place.ctx ^ 1})
+            greet({"ctx": place.ctx ^ 2})
+            fixed += 2
+        if "dp" in axes:
+            greet({"dp": place.dp ^ 1})
+            fixed += 1
+        if "tp" in axes:
+            up, down = place.tp < tp_size - 1, place.tp > 0
+            when(up, lambda: greet({"tp": place.tp + 1}))
+            when(down, lambda: greet({"tp": place.tp - 1}))
+        peers = jnp.int32(fixed)
+        if "tp" in axes:
+            peers = peers + up.astype(jnp.int32) + down.astype(jnp.int32)
+        pl.semaphore_wait(barrier, peers)
+
+        class View:
+            def __init__(self, first):
+                self.first = first
+
+            def at(self, index):
+                return sem_ref.at[self.first + index]
+
+        running = []
+        for task, first in zip(tasks, firsts):
+            a, ins = ins[: len(task.inputs)], ins[len(task.inputs) :]
+            b, outs = outs[: len(task.outputs)], outs[len(task.outputs) :]
+            c, scr = scr[: len(task.scratch)], scr[len(task.scratch) :]
+            running.append([-1.0, task.emit(place, a, b, c, View(first))])
+        while running:
+            entry = min(running, key=lambda item: item[0])
+            try:
+                entry[0] = next(entry[1])
+            except StopIteration:
+                running.remove(entry)
+
+    result = pl.pallas_call(
+        kernel,
+        out_shape=tuple(outputs),
+        in_specs=[HBM] * len(inputs),
+        out_specs=tuple([HBM] * len(outputs)),
+        scratch_shapes=list(scratch) + [pltpu.SemaphoreType.DMA((sems.count,))],
+        compiler_params=pltpu.CompilerParams(
+            collective_id=ident, has_side_effects=True, vmem_limit_bytes=56 * 1024 * 1024
+        ),
+        name=name,
+    )(*inputs)
+    return result
+
+
+def general_row_total(value):
     return lax.psum(value, "tp")
 
 
-def widen(value):
+def general_widen(value):
     return lax.all_gather(value, "tp", axis=1, tiled=True)
 
 
-def narrow(value):
+def general_narrow(value):
     return lax.psum_scatter(
         value.astype(jnp.bfloat16), "tp", scatter_dimension=1, tiled=True
     ).astype(jnp.float32)
 
 
-def contract_last(left, right):
+def general_contract_last(left, right):
     return lax.dot_general(
         left, right, (((1,), (1,)), ((), ())), preferred_element_type=jnp.float32
     )
 
 
-def contract_first(left, right):
+def general_contract_first(left, right):
     return lax.dot_general(
         left, right, (((0,), (0,)), ((), ())), preferred_element_type=jnp.float32
     )
 
 
-def rotary(positions, depth):
+def general_rotary(positions, depth):
     half = depth // 2
     freqs = THETA ** (-(jnp.arange(half, dtype=jnp.float32) * 2.0) / depth)
     angles = positions.astype(jnp.float32)[..., None] * freqs
     return (jnp.cos(angles)[..., None, :], jnp.sin(angles)[..., None, :])
 
 
-def turn(value, cosine, sine):
+def general_turn(value, cosine, sine):
     half = value.shape[-1] // 2
     first = value[..., :half]
     second = value[..., half:]
@@ -57,7 +528,7 @@
     )
 
 
-def turn_back(grad, cosine, sine):
+def general_turn_back(grad, cosine, sine):
     half = grad.shape[-1] // 2
     first = grad[..., :half]
     second = grad[..., half:]
@@ -66,11 +537,11 @@
     )
 
 
-def norm_grad(scaled, value, factor, inner):
+def general_norm_grad(scaled, value, factor, inner):
     return factor[:, None] * scaled - value * (factor**3 * inner / D)[:, None]
 
 
-def local(
+def general(
     hidden,
     cotangent,
     segments,
@@ -88,7 +559,7 @@
     mlp_gain,
 ):
     local_seqs, slice_len, local_width = hidden.shape
-    per_batch = local_seqs // MICRO
+    per_batch = local_seqs // 2
     rows = per_batch * slice_len
     heads_here = q_gain.shape[0] // HEAD_DIM
     scale = 1.0 / math.sqrt(HEAD_DIM)
@@ -100,7 +571,7 @@
     k_gain_grad = jnp.zeros(k_gain.shape, jnp.float32)
     attn_gain_grad = jnp.zeros(attn_gain.shape, jnp.float32)
     mlp_gain_grad = jnp.zeros(mlp_gain.shape, jnp.float32)
-    for batch in range(MICRO):
+    for batch in range(2):
         lower = batch * per_batch
         tokens_in = hidden[lower : lower + per_batch].reshape(rows, local_width)
         seg_here = segments[lower : lower + per_batch]
@@ -117,22 +588,22 @@
         query_full, key_full, value_full, out_full, gate_full, up_full, down_full = gathered
         if weight_grads is None:
             weight_grads = tuple((jnp.zeros(tensor.shape, jnp.float32) for tensor in gathered))
-        wide_in = widen(tokens_in)
+        wide_in = general_widen(tokens_in)
         query_raw = jnp.dot(wide_in, query_full, preferred_element_type=jnp.float32)
         key_raw = jnp.dot(wide_in, key_full, preferred_element_type=jnp.float32)
         value_raw = jnp.dot(wide_in, value_full, preferred_element_type=jnp.float32)
-        query_sq, key_sq = row_total(
+        query_sq, key_sq = general_row_total(
             (jnp.sum(query_raw * query_raw, axis=1), jnp.sum(key_raw * key_raw, axis=1))
         )
         query_scale = lax.rsqrt(query_sq / D + EPS)
         key_scale = lax.rsqrt(key_sq / D + EPS)
-        cosine, sine = rotary(pos_here, HEAD_DIM)
-        query_rot = turn(
+        cosine, sine = general_rotary(pos_here, HEAD_DIM)
+        query_rot = general_turn(
             (query_raw * query_scale[:, None] * q_gain).reshape(rows, heads_here, HEAD_DIM),
             cosine,
             sine,
         )
-        key_rot = turn(
+        key_rot = general_turn(
             (key_raw * key_scale[:, None] * k_gain).reshape(rows, heads_here, HEAD_DIM),
             cosine,
             sine,
@@ -177,17 +648,17 @@
             (accum / total[..., None]).transpose(0, 2, 1, 3).reshape(rows, heads_here * HEAD_DIM)
         )
         out_b = out_heads.astype(jnp.bfloat16)
-        attn_raw = narrow(jnp.dot(out_b, out_full, preferred_element_type=jnp.float32))
-        attn_scale = lax.rsqrt(row_total(jnp.sum(attn_raw * attn_raw, axis=1)) / D + EPS)
+        attn_raw = general_narrow(jnp.dot(out_b, out_full, preferred_element_type=jnp.float32))
+        attn_scale = lax.rsqrt(general_row_total(jnp.sum(attn_raw * attn_raw, axis=1)) / D + EPS)
         resid = tokens_in.astype(jnp.float32) + attn_raw * attn_scale[:, None] * attn_gain
-        wide_mid = widen(resid.astype(jnp.bfloat16))
+        wide_mid = general_widen(resid.astype(jnp.bfloat16))
         gate = jnp.dot(wide_mid, gate_full, preferred_element_type=jnp.float32)
         up_val = jnp.dot(wide_mid, up_full, preferred_element_type=jnp.float32)
         sigma = jax.nn.sigmoid(gate)
         swish = gate * sigma
         act_b = (swish * up_val).astype(jnp.bfloat16)
-        mlp_raw = narrow(jnp.dot(act_b, down_full, preferred_element_type=jnp.float32))
-        mlp_scale = lax.rsqrt(row_total(jnp.sum(mlp_raw * mlp_raw, axis=1)) / D + EPS)
+        mlp_raw = general_narrow(jnp.dot(act_b, down_full, preferred_element_type=jnp.float32))
+        mlp_scale = lax.rsqrt(general_row_total(jnp.sum(mlp_raw * mlp_raw, axis=1)) / D + EPS)
         result = resid + mlp_raw * mlp_scale[:, None] * mlp_gain
         outputs.append(result.astype(jnp.bfloat16).reshape(per_batch, slice_len, local_width))
         again = (
@@ -205,25 +676,25 @@
         )
         mlp_gain_grad = mlp_gain_grad + jnp.sum(grad_out * mlp_raw * mlp_scale[:, None], axis=0)
         scaled = grad_out * mlp_gain
-        grad_mlp = norm_grad(
-            scaled, mlp_raw, mlp_scale, row_total(jnp.sum(scaled * mlp_raw, axis=1))
-        )
-        wide_grad_mlp = widen(grad_mlp.astype(jnp.bfloat16))
-        grad_act = contract_last(wide_grad_mlp, down_back)
+        grad_mlp = general_norm_grad(
+            scaled, mlp_raw, mlp_scale, general_row_total(jnp.sum(scaled * mlp_raw, axis=1))
+        )
+        wide_grad_mlp = general_widen(grad_mlp.astype(jnp.bfloat16))
+        grad_act = general_contract_last(wide_grad_mlp, down_back)
         grad_gate = (grad_act * up_val * sigma * (1.0 + gate * (1.0 - sigma))).astype(jnp.bfloat16)
         grad_up = (grad_act * swish).astype(jnp.bfloat16)
-        grad_resid = grad_out + narrow(
-            contract_last(grad_gate, gate_back) + contract_last(grad_up, up_back)
+        grad_resid = grad_out + general_narrow(
+            general_contract_last(grad_gate, gate_back) + general_contract_last(grad_up, up_back)
         )
         attn_gain_grad = attn_gain_grad + jnp.sum(
             grad_resid * attn_raw * attn_scale[:, None], axis=0
         )
         scaled = grad_resid * attn_gain
-        grad_attn = norm_grad(
-            scaled, attn_raw, attn_scale, row_total(jnp.sum(scaled * attn_raw, axis=1))
-        )
-        wide_grad_attn = widen(grad_attn.astype(jnp.bfloat16))
-        grad_heads = contract_last(wide_grad_attn, out_back).astype(jnp.bfloat16)
+        grad_attn = general_norm_grad(
+            scaled, attn_raw, attn_scale, general_row_total(jnp.sum(scaled * attn_raw, axis=1))
+        )
+        wide_grad_attn = general_widen(grad_attn.astype(jnp.bfloat16))
+        grad_heads = general_contract_last(wide_grad_attn, out_back).astype(jnp.bfloat16)
         dout_four = grad_heads.reshape(per_batch, slice_len, heads_here, HEAD_DIM)
         delta = jnp.sum(
             (grad_heads.astype(jnp.float32) * out_heads).reshape(
@@ -277,37 +748,37 @@
                 grad_values.astype(jnp.bfloat16), "ctx", scatter_dimension=1, tiled=True
             ).astype(jnp.float32),
         )
-        grad_qnorm = turn_back(
+        grad_qnorm = general_turn_back(
             grad_query.reshape(rows, heads_here, HEAD_DIM), cosine, sine
         ).reshape(rows, heads_here * HEAD_DIM)
-        grad_knorm = turn_back(
+        grad_knorm = general_turn_back(
             key_grad_mine.reshape(rows, heads_here, HEAD_DIM), cosine, sine
         ).reshape(rows, heads_here * HEAD_DIM)
         q_gain_grad = q_gain_grad + jnp.sum(grad_qnorm * query_raw * query_scale[:, None], axis=0)
         k_gain_grad = k_gain_grad + jnp.sum(grad_knorm * key_raw * key_scale[:, None], axis=0)
         q_scaled = grad_qnorm * q_gain
         k_scaled = grad_knorm * k_gain
-        q_inner, k_inner = row_total(
+        q_inner, k_inner = general_row_total(
             (jnp.sum(q_scaled * query_raw, axis=1), jnp.sum(k_scaled * key_raw, axis=1))
         )
-        grad_query_raw = norm_grad(q_scaled, query_raw, query_scale, q_inner).astype(jnp.bfloat16)
-        grad_key_raw = norm_grad(k_scaled, key_raw, key_scale, k_inner).astype(jnp.bfloat16)
+        grad_query_raw = general_norm_grad(q_scaled, query_raw, query_scale, q_inner).astype(jnp.bfloat16)
+        grad_key_raw = general_norm_grad(k_scaled, key_raw, key_scale, k_inner).astype(jnp.bfloat16)
         grad_value_raw = value_grad_mine.reshape(rows, heads_here * HEAD_DIM).astype(jnp.bfloat16)
         back_terms = (
-            contract_last(grad_query_raw, query_back)
-            + contract_last(grad_key_raw, key_back)
-            + contract_last(grad_value_raw, value_back)
-        )
-        grad_in = grad_resid + narrow(back_terms)
+            general_contract_last(grad_query_raw, query_back)
+            + general_contract_last(grad_key_raw, key_back)
+            + general_contract_last(grad_value_raw, value_back)
+        )
+        grad_in = grad_resid + general_narrow(back_terms)
         input_grads.append(grad_in.astype(jnp.bfloat16).reshape(per_batch, slice_len, local_width))
         fresh_grads = (
-            contract_first(wide_in, grad_query_raw),
-            contract_first(wide_in, grad_key_raw),
-            contract_first(wide_in, grad_value_raw),
-            contract_first(out_b, wide_grad_attn),
-            contract_first(wide_mid, grad_gate),
-            contract_first(wide_mid, grad_up),
-            contract_first(act_b, wide_grad_mlp),
+            general_contract_first(wide_in, grad_query_raw),
+            general_contract_first(wide_in, grad_key_raw),
+            general_contract_first(wide_in, grad_value_raw),
+            general_contract_first(out_b, wide_grad_attn),
+            general_contract_first(wide_mid, grad_gate),
+            general_contract_first(wide_mid, grad_up),
+            general_contract_first(act_b, wide_grad_mlp),
         )
         weight_grads = tuple((left + right for left, right in zip(weight_grads, fresh_grads)))
     finals = (
@@ -351,42 +822,234 @@
     )
 
 
+def contract_last(left, right):
+    return lax.dot_general(left, right, (((1,), (1,)), ((), ())), preferred_element_type=F32)
+
+
+def contract_first(left, right):
+    return lax.dot_general(left, right, (((0,), (0,)), ((), ())), preferred_element_type=F32)
+
+
+def mm(left, right):
+    return jnp.dot(left, right, preferred_element_type=F32)
+
+
+def rotary(positions, depth):
+    half = depth // 2
+    freqs = THETA ** (-(jnp.arange(half, dtype=F32) * 2.0) / depth)
+    angles = positions.astype(F32)[..., None] * freqs
+    return (jnp.cos(angles)[..., None, :], jnp.sin(angles)[..., None, :])
+
+
+def turn(value, cosine, sine):
+    half = value.shape[-1] // 2
+    first, second = value[..., :half], value[..., half:]
+    return jnp.concatenate([first * cosine - second * sine, second * cosine + first * sine], axis=-1)
+
+
+def turn_back(grad, cosine, sine):
+    return turn(grad, cosine, -sine)
+
+
+def norm_grad(scaled, value, factor, inner):
+    return factor[:, None] * scaled - value * (factor**3 * inner / D)[:, None]
+
+
+def totals(*values):
+    return lax.psum(values, "tp")
+
+
+def planned(
+    hidden, cotangent, segments, positions, w_query, w_key, w_value, w_out, w_gate, w_up, w_down,
+    q_gain, k_gain, attn_gain, mlp_gain,
+):
+    n = lax.axis_size("tp")
+    seqs, slice_len, width = hidden.shape
+    per = seqs // 2
+    rows = per * slice_len
+    heads = width // HEAD_DIM
+    ctx_size = 4
+    scale = 1.0 / math.sqrt(HEAD_DIM)
+    query_index = lax.axis_index("ctx") * slice_len + jnp.arange(slice_len, dtype=jnp.int32)
+    x_in = [hidden[b * per : (b + 1) * per].reshape(rows, width) for b in (0, 1)]
+    cot = [cotangent[b * per : (b + 1) * per].reshape(rows, width).astype(F32) for b in (0, 1)]
+    segs = [segments[b * per : (b + 1) * per] for b in (0, 1)]
+    seg_all = lax.all_gather(segments, "ctx", axis=0, tiled=False)
+    angles = [rotary(positions[b * per : (b + 1) * per].reshape(rows), HEAD_DIM) for b in (0, 1)]
+    key_index = jnp.arange(ctx_size * slice_len, dtype=jnp.int32).reshape(ctx_size, slice_len)
+    st = [dict(), dict()]
+
+    def allowed(b):
+        seg_keys = seg_all[:, b * per : (b + 1) * per]
+        causal = query_index[:, None, None] >= key_index[None]
+        same = segs[b][:, None, :, None, None] == seg_keys.transpose(1, 0, 2)[:, None, None]
+        return jnp.logical_and(same, causal[None, None])
+
+    def qkv(b, wide):
+        s = st[b]
+        s["wide"] = wide
+        s["q_raw"], s["k_raw"] = mm(wide, wq), mm(wide, wk)
+        value = mm(wide, wv)
+        q_sq, k_sq = totals(jnp.sum(s["q_raw"] ** 2, axis=1), jnp.sum(s["k_raw"] ** 2, axis=1))
+        s["q_s"], s["k_s"] = lax.rsqrt(q_sq / D + EPS), lax.rsqrt(k_sq / D + EPS)
+        cosine, sine = angles[b]
+        turned = lambda raw, f, gain: turn((raw * f[:, None] * gain).reshape(rows, heads, HEAD_DIM), cosine, sine)
+        s["q"] = turned(s["q_raw"], s["q_s"], q_gain).astype(BF).reshape(per, slice_len, heads, HEAD_DIM)
+        key = turned(s["k_raw"], s["k_s"], k_gain).astype(BF).reshape(rows, width)
+        return jnp.concatenate([key, value.astype(BF)], axis=1)
+
+    def attend(b, kv):
+        s = st[b]
+        kv = kv.reshape(ctx_size, per, slice_len, 2, heads, HEAD_DIM)
+        s["k"], s["v"] = kv[:, :, :, 0], kv[:, :, :, 1]
+        ok = allowed(b)
+        logits = scale * jnp.einsum("sqhd,cskhd->shqck", s["q"], s["k"], preferred_element_type=F32)
+        logits = jnp.where(ok, logits, NEG)
+        peak = jnp.max(logits, axis=(-1, -2))
+        weights = jnp.where(ok, jnp.exp(logits - peak[..., None, None]), 0.0)
+        total = jnp.sum(weights, axis=(-1, -2))
+        acc = jnp.einsum("shqck,cskhd->shqd", weights.astype(BF), s["v"], preferred_element_type=F32)
+        s["logsum"] = peak + jnp.log(total)
+        s["heads"] = (acc / total[..., None]).transpose(0, 2, 1, 3).reshape(rows, width)
+        s["heads_b"] = s["heads"].astype(BF)
+        return mm(s["heads_b"], wo).astype(BF)
+
+    def after_attn(b, raw):
+        s = st[b]
+        s["attn"] = raw
+        (sq,) = totals(jnp.sum(raw * raw, axis=1))
+        s["attn_s"] = lax.rsqrt(sq / D + EPS)
+        s["resid"] = x_in[b].astype(F32) + raw * s["attn_s"][:, None] * attn_gain
+        return s["resid"].astype(BF)
+
+    def mlp(b, wide):
+        s = st[b]
+        s["mid"] = wide
+        s["gate"], s["up"] = mm(wide, wg), mm(wide, wu)
+        s["act"] = (s["gate"] * jax.nn.sigmoid(s["gate"]) * s["up"]).astype(BF)
+        return mm(s["act"], wd).astype(BF)
+
+    def after_mlp(b, raw):
+        s = st[b]
+        scaled = cot[b] * mlp_gain
+        sq, inner = totals(jnp.sum(raw * raw, axis=1), jnp.sum(scaled * raw, axis=1))
+        factor = lax.rsqrt(sq / D + EPS)
+        s["out"] = (s["resid"] + raw * factor[:, None] * mlp_gain).astype(BF)
+        s["g_mlp_gain"] = jnp.sum(cot[b] * raw * factor[:, None], axis=0)
+        return norm_grad(scaled, raw, factor, inner).astype(BF)
+
+    def mlp_back(b, wide):
+        s = st[b]
+        s["g_mlp"] = wide
+        g_act = contract_last(wide, wd)
+        sigma = jax.nn.sigmoid(s["gate"])
+        s["g_gate"] = (g_act * s["up"] * sigma * (1.0 + s["gate"] * (1.0 - sigma))).astype(BF)
+        s["g_up"] = (g_act * s["gate"] * sigma).astype(BF)
+        return (contract_last(s["g_gate"], wg) + contract_last(s["g_up"], wu)).astype(BF)
+
+    def after_resid(b, raw):
+        s = st[b]
+        s["g_resid"] = cot[b] + raw
+        scaled = s["g_resid"] * attn_gain
+        (inner,) = totals(jnp.sum(scaled * s["attn"], axis=1))
+        s["g_attn_gain"] = jnp.sum(s["g_resid"] * s["attn"] * s["attn_s"][:, None], axis=0)
+        return norm_grad(scaled, s["attn"], s["attn_s"], inner).astype(BF)
+
+    def attn_back(b, wide):
+        s = st[b]
+        s["g_attn"] = wide
+        g_heads = contract_last(wide, wo).astype(BF)
+        g_four = g_heads.reshape(per, slice_len, heads, HEAD_DIM)
+        delta = jnp.sum((g_heads.astype(F32) * s["heads"]).reshape(per, slice_len, heads, HEAD_DIM), axis=-1)
+        delta = delta.transpose(0, 2, 1)
+        logits = scale * jnp.einsum("sqhd,cskhd->shqck", s["q"], s["k"], preferred_element_type=F32)
+        probs = jnp.where(allowed(b), jnp.exp(logits - s["logsum"][..., None, None]), 0.0)
+        g_probs = jnp.einsum("sqhd,cskhd->shqck", g_four, s["v"], preferred_element_type=F32)
+        g_logits = (probs * (g_probs - delta[..., None, None])).astype(BF)
+        s["g_q"] = scale * jnp.einsum("shqck,cskhd->sqhd", g_logits, s["k"], preferred_element_type=F32)
+        g_k = scale * jnp.einsum("shqck,sqhd->cskhd", g_logits, s["q"], preferred_element_type=F32)
+        g_v = jnp.einsum("shqck,sqhd->cskhd", probs.astype(BF), g_four, preferred_element_type=F32)
+        shape = (ctx_size * rows, width)
+        return jnp.concatenate([g_k.astype(BF).reshape(shape), g_v.astype(BF).reshape(shape)], axis=1)
+
+    def qkv_back(b, g_kv):
+        s = st[b]
+        cosine, sine = angles[b]
+        back = lambda g: turn_back(g.reshape(rows, heads, HEAD_DIM), cosine, sine).reshape(rows, width)
+        g_qn, g_kn = back(s["g_q"]), back(g_kv[:, :width])
+        s["g_q_gain"] = jnp.sum(g_qn * s["q_raw"] * s["q_s"][:, None], axis=0)
+        s["g_k_gain"] = jnp.sum(g_kn * s["k_raw"] * s["k_s"][:, None], axis=0)
+        q_in, k_in = totals(jnp.sum(g_qn * q_gain * s["q_raw"], axis=1), jnp.sum(g_kn * k_gain * s["k_raw"], axis=1))
+        s["g_qr"] = norm_grad(g_qn * q_gain, s["q_raw"], s["q_s"], q_in).astype(BF)
+        s["g_kr"] = norm_grad(g_kn * k_gain, s["k_raw"], s["k_s"], k_in).astype(BF)
+        s["g_vr"] = g_kv[:, width:].astype(BF)
+        return (contract_last(s["g_qr"], wq) + contract_last(s["g_kr"], wk) + contract_last(s["g_vr"], wv)).astype(BF)
+
+    def weight_grad(left, right):
+        return (contract_first(st[0][left], st[0][right]) + contract_first(st[1][left], st[1][right])).astype(BF)
+
+    def final(b, raw):
+        return (st[b]["g_resid"] + raw).astype(BF)
+
+    gather = lambda a: LineGather(a, n)
+    scatter = lambda a: LineScatter(a, n)
+    wide0, wq, wk, wv = run_tasks(
+        "slot0", 0, n, [gather(x_in[0]), PlaneGather(w_query, 0, True), PlaneGather(w_key, 0, True, 4.0), PlaneGather(w_value, 0, True, 8.0)]
+    )
+    kv0 = qkv(0, wide0)
+    wide1, kvs0, wo = run_tasks("slot1", 1, n, [gather(x_in[1]), PlaneGather(kv0, 0, False), PlaneGather(w_out, 1, True, 9.0)])
+    kv1 = qkv(1, wide1)
+    part0 = attend(0, kvs0)
+    raw0, kvs1, wg = run_tasks("slot2", 2, n, [scatter(part0), PlaneGather(kv1, 0, False), PlaneGather(w_gate, 0, True, 9.0)])
+    part1 = attend(1, kvs1)
+    mid0, raw1, wu, wd = run_tasks(
+        "slot3", 3, n, [gather(after_attn(0, raw0)), scatter(part1), PlaneGather(w_up, 0, True), PlaneGather(w_down, 1, True, 18.0)]
+    )
+    part0 = mlp(0, mid0)
+    raw0, mid1 = run_tasks("slot4", 4, n, [scatter(part0), gather(after_attn(1, raw1))])
+    part1 = mlp(1, mid1)
+    wide0, raw1 = run_tasks("slot5", 5, n, [gather(after_mlp(0, raw0)), scatter(part1)])
+    part0 = mlp_back(0, wide0)
+    raw0, wide1 = run_tasks("slot6", 6, n, [scatter(part0), gather(after_mlp(1, raw1))])
+    part1 = mlp_back(1, wide1)
+    d_down = weight_grad("act", "g_mlp")
+    wide0, raw1, g_down = run_tasks(
+        "slot7", 7, n, [gather(after_resid(0, raw0)), scatter(part1), PlaneScatter(d_down, 1, True)]
+    )
+    kv0 = attn_back(0, wide0)
+    d_gate = weight_grad("mid", "g_gate")
+    wide1, kvs0, g_gate = run_tasks(
+        "slot8", 8, n, [gather(after_resid(1, raw1)), PlaneScatter(kv0, 0, False), PlaneScatter(d_gate, 0, True)]
+    )
+    part0 = qkv_back(0, kvs0)
+    kv1 = attn_back(1, wide1)
+    d_up = weight_grad("mid", "g_up")
+    raw0, kvs1, g_up = run_tasks("slot9", 9, n, [scatter(part0), PlaneScatter(kv1, 0, False), PlaneScatter(d_up, 0, True)])
+    part1 = qkv_back(1, kvs1)
+    d_out = weight_grad("heads_b", "g_attn")
+    d_q, d_k, d_v = weight_grad("wide", "g_qr"), weight_grad("wide", "g_kr"), weight_grad("wide", "g_vr")
+    raw1, g_out, g_q, g_k, g_v = run_tasks(
+        "slot10", 10, n,
+        [scatter(part1), PlaneScatter(d_out, 1, True), PlaneScatter(d_q, 0, True), PlaneScatter(d_k, 0, True), PlaneScatter(d_v, 0, True)],
+    )
+    gains = lax.psum(tuple(st[0][g] + st[1][g] for g in ("g_q_gain", "g_k_gain", "g_attn_gain", "g_mlp_gain")), ("dp", "ctx"))
+    shape = (per, slice_len, width)
+    return (
+        jnp.concatenate([st[0]["out"].reshape(shape), st[1]["out"].reshape(shape)], axis=0),
+        jnp.concatenate([final(0, raw0).reshape(shape), final(1, raw1).reshape(shape)], axis=0),
+        g_q, g_k, g_v, g_out, g_gate, g_up, g_down, *gains,
+    )
+
+
 def solution(mesh):
-    placed = (
-        P("dp", "ctx", "tp"),
-        P("dp", "ctx", "tp"),
-        P("dp", "ctx"),
-        P("dp", "ctx"),
-        P(("dp", "ctx"), "tp"),
-        P(("dp", "ctx"), "tp"),
-        P(("dp", "ctx"), "tp"),
-        P("tp", ("dp", "ctx")),
-        P(("dp", "ctx"), "tp"),
-        P(("dp", "ctx"), "tp"),
-        P("tp", ("dp", "ctx")),
-        P("tp"),
-        P("tp"),
-        P("tp"),
-        P("tp"),
-    )
+    rows, cols = P(("dp", "ctx"), "tp"), P("tp", ("dp", "ctx"))
+    act, gain = P("dp", "ctx", "tp"), P("tp")
+    size = dict(mesh.shape)
+    body = planned if (size["dp"], size["ctx"]) == (2, 4) else general
     return jax.shard_map(
-        local,
+        body,
         mesh=mesh,
-        in_specs=placed,
-        out_specs=(
-            P("dp", "ctx", "tp"),
-            P("dp", "ctx", "tp"),
-            P(("dp", "ctx"), "tp"),
-            P(("dp", "ctx"), "tp"),
-            P(("dp", "ctx"), "tp"),
-            P("tp", ("dp", "ctx")),
-            P(("dp", "ctx"), "tp"),
-            P(("dp", "ctx"), "tp"),
-            P("tp", ("dp", "ctx")),
-            P("tp"),
-            P("tp"),
-            P("tp"),
-            P("tp"),
-        ),
+        in_specs=(act, act, P("dp", "ctx"), P("dp", "ctx"), rows, rows, rows, cols, rows, rows, cols, gain, gain, gain, gain),
+        out_specs=(act, act, rows, rows, rows, cols, rows, rows, cols, gain, gain, gain, gain),
         check_vma=False,
     )

time: 1750 us -> 1460 us (0.83)
  waiting for transfers between devices: 1150 us -> 0 us
  Pallas kernels: 0 us -> 816 us
  blocking collectives: 81.1 us -> 179 us
  matrix products: 313 us -> 255 us
  local copies, waits for them, and re-layouts: 98.2 us -> 117 us
    pallas_call x0 -> x11, Pallas kernels: none -> 816 us  [run_tasks(): pl.pallas_call(kernel, out_shape=tuple(outputs), in_specs=[HBM] * len(inp...]
    reduce_scatter x19 -> x0, waiting for transfers between devices: 605 us -> none  [the longest x8 295 us: narrow(): lax.psum_scatter(value.astype(jnp.bfloat16), 'tp', scatter_dimension=1, t...]
    all_gather x19 -> x0, waiting for transfers between devices: 542 us -> none  [the longest x8 298 us: widen(): return lax.all_gather(value, 'tp', axis=1, tiled=True)]
    psum x7 -> x13, blocking collectives: 70.8 us -> 173 us  [the longest x12 158 us: totals(): return lax.psum(values, 'tp')]
    dot_general x26, matrix products: 142 us -> 94.6 us  [the longest x14 58.9 us: mm(): return jnp.dot(left, right, preferred_element_type=F32)]
    reshape x10, local copies, waits for them, and re-layouts: 9.42 us -> 28.1 us  [the longest x2 15.4 us: attend(): kv = kv.reshape(ctx_size, per, slice_len, 2, heads, HEAD_DIM)]
    unnamed x267 -> x355, local copies, waits for them, and re-layouts: 44 us -> 44.6 us
  transfers between devices with their start and end apart: 38 -> 0, of which waited for: 30 -> 0; matrix products, arithmetic and copies ran while one was open for 26% -> 0% of each run, Pallas kernels for 0% -> 0%
where the time goes in v1:
time: 1460 us; the launch traced here: 1450 us
  Pallas kernels  816 us (56%)
  matrix products  255 us (17%)
  blocking collectives  179 us (12%)
  local copies, waits for them, and re-layouts  117 us (8%)
  other arithmetic  81.2 us (6%)
    pallas_call x11, Pallas kernels, run_tasks(): pl.pallas_call(kernel, out_shape=tuple(outputs), in_specs=[HBM] * len(inp...  816 us
    psum x12, blocking collectives, totals(): return lax.psum(values, 'tp')  158 us
    dot_general x14, matrix products, contract_first(): lax.dot_general(left, right, (((0,), (0,)), ((), ())), preferred_element_...  85.3 us
    dot_general x14, matrix products, contract_last(): lax.dot_general(left, right, (((1,), (1,)), ((), ())), preferred_element_...  74.6 us
    dot_general x14, matrix products, mm(): return jnp.dot(left, right, preferred_element_type=F32)  58.9 us
    unnamed x355, local copies, waits for them, and re-layouts  44.6 us

profile of v1, /device:TPU:0, one launch (start us, length us, event | category | flops | bytes accessed | tf_op | source)
XLA Modules:
  0.0 1450.4 jit_solution(5996586625914054124)
XLA Ops:
  2.3 6.3 all-gather.1
  16.7 63.4 %slot0.1 = (bf16[512,2048]{1,0:T(8,128)(2,1)}, bf16[2048,512]{1,0:T(8,128)(2,1)}, bf16[2048,512]{1,0:T(8,128)(2,1)}, bf16[2048,512]{1,0:T(8,128)(2,1)}) custom-call(bf16[512,512]{1,0:T(8,128)(2,1)} %bitcast.358, bf16[256,512]{1,0:T(8,128)(2,1)} %refs_1_.1, bf16[256,512]{1,0:T(8,128)(2,1)} %refs_2_.4, bf16[256,512]{1,0:T(8,128)(2,1)} %refs_3_.2), custom_call_target="tpu_custom_call" | custom-call | tf_op jit(solution)/shard_map/slot0/pallas_call | solution.py:475
  88.1 10.8 psum.141
  107.5 75.4 %slot1.1 = (bf16[512,2048]{1,0:T(8,128)(2,1)}, bf16[2048,1024]{1,0:T(8,128)(2,1)}, bf16[512,2048]{1,0:T(8,128)(2,1)}) custom-call(bf16[512,512]{1,0:T(8,128)(2,1)} %bitcast.357, bf16[512,1024]{1,0:T(8,128)(2,1)} %pad_maximum_fusion.2.refs_1_, bf16[512,256]{1,0:T(8,128)(2,1)} %refs_2_.5), custom_call_target="tpu_custom_call" | custom-call | tf_op jit(solution)/shard_map/slot1/pallas_call | solution.py:475
  182.9 7.7 reshape.382
  201.8 10.3 all-reduce.4
  243.1 73.3 %slot2.1 = (f32[512,512]{1,0:T(8,128)}, bf16[2048,1024]{1,0:T(8,128)(2,1)}, bf16[2048,2048]{1,0:T(8,128)(2,1)}) custom-call(bf16[512,2048]{1,0:T(8,128)(2,1)} %convolution_convert_fusion.3.refs_0_, bf16[512,1024]{1,0:T(8,128)(2,1)} %pad_maximum_fusion.3.refs_1_, bf16[256,2048]{1,0:T(8,128)(2,1)} %refs_2_.6), custom_call_target="tpu_custom_call" | custom-call | tf_op jit(solution)/shard_map/slot2/pallas_call | solution.py:475
  316.4 7.7 reshape.386
  328.8 25.4 %all-reduce.3 = (f32[512]{0:T(512)S(1)}, f32[512]{0:T(512)S(1)}) all-reduce(f32[512]{0:T(512)S(1)} %multiply_reduce_fusion.12, f32[512]{0:T(512)S(1)} %get-tuple-element.182), channel_id=1, replica_groups=mesh['dp'=2,'ctx'=4,'tp'=4] {'tp'}, use_global_device_ids=true, to_apply=%region_9.10 | all-reduce | flops 1024 | bytes 8192 | tf_op jit(solution)/shard_map/psum | solution.py:859
  377.7 94.0 %slot3.1 = (bf16[512,2048]{1,0:T(8,128)(2,1)}, f32[512,512]{1,0:T(8,128)}, bf16[2048,2048]{1,0:T(8,128)(2,1)}, bf16[2048,2048]{1,0:T(8,128)(2,1)}) custom-call(bf16[512,512]{1,0:T(8,128)(2,1)} %fusion.74.refs_0_, bf16[512,2048]{1,0:T(8,128)(2,1)} %convolution_convert_fusion.2.refs_1_, bf16[256,2048]{1,0:T(8,128)(2,1)} %refs_2_.7, bf16[2048,256]{1,0:T(8,128)(2,1)} %refs_3_.3), custom_call_target="tpu_custom_call" | custom-call | tf_op jit(solution)/shard_map/slot3/pallas_call | solution.py:475
  473.0 20.5 %psum.145 = f32[512]{0:T(512)S(1)} all-reduce(f32[512]{0:T(512)S(1)} %multiply_reduce_fusion.10), channel_id=1, replica_groups=mesh['dp'=2,'ctx'=4,'tp'=4] {'tp'}, use_global_device_ids=true, to_apply=%region_15.16 | all-reduce | flops 512 | bytes 4096 | tf_op jit(solution)/shard_map/psum | solution.py:859
  495.9 7.7 fusion.123
  503.7 6.4 multiply_convert_fusion.9
  511.4 5.8 convolution_convert_fusion.1.refs_0_
  517.2 68.6 %slot4.1 = (f32[512,512]{1,0:T(8,128)}, bf16[512,2048]{1,0:T(8,128)(2,1)}) custom-call(bf16[512,2048]{1,0:T(8,128)(2,1)} %convolution_convert_fusion.1.refs_0_, bf16[512,512]{1,0:T(8,128)(2,1)} %fusion.75.refs_1_), custom_call_target="tpu_custom_call" | custom-call | tf_op jit(solution)/shard_map/slot4/pallas_call | solution.py:475
  587.3 11.9 psum.146
  600.8 8.6 psum.147
  611.9 7.0 fusion.124
  618.9 6.5 multiply_convert_fusion.8
  626.8 5.8 convolution_convert_fusion.refs_1_
  632.6 62.7 %slot5.1 = (bf16[512,2048]{1,0:T(8,128)(2,1)}, f32[512,512]{1,0:T(8,128)}) custom-call(bf16[512,512]{1,0:T(8,128)(2,1)} %fusion.54.refs_0_, bf16[512,2048]{1,0:T(8,128)(2,1)} %convolution_convert_fusion.refs_1_), custom_call_target="tpu_custom_call" | custom-call | tf_op jit(solution)/shard_map/slot5/pallas_call | solution.py:475
  695.3 12.8 multiply_convert_fusion.6
  708.2 12.4 psum.148
  721.6 8.4 psum.149
  731.1 7.8 fusion.125
  738.9 9.4 add_convert_fusion.10.refs_0_
  748.4 64.8 %slot6.1 = (f32[512,512]{1,0:T(8,128)}, bf16[512,2048]{1,0:T(8,128)(2,1)}) custom-call(bf16[512,2048]{1,0:T(8,128)(2,1)} %add_convert_fusion.10.refs_0_, bf16[512,512]{1,0:T(8,128)(2,1)} %fusion.51.refs_1_), custom_call_target="tpu_custom_call" | custom-call | tf_op jit(solution)/shard_map/slot6/pallas_call | solution.py:475
  813.2 11.9 multiply_convert_fusion.4
  825.1 8.5 fusion.126
  833.7 9.3 add_convert_fusion.9.refs_1_
  843.4 12.1 psum.150
  858.9 8.3 fusion.127
  867.2 10.3 add_convert_fusion.2.refs_2_
  877.6 88.0 %slot7.1 = (bf16[512,2048]{1,0:T(8,128)(2,1)}, f32[512,512]{1,0:T(8,128)}, f32[2048,256]{1,0:T(8,128)}) custom-call(bf16[512,512]{1,0:T(8,128)(2,1)} %get-tuple-element.135.refs_0_, bf16[512,2048]{1,0:T(8,128)(2,1)} %add_convert_fusion.9.refs_1_, bf16[2048,2048]{1,0:T(8,128)(2,1)} %add_convert_fusion.2.refs_2_), custom_call_target="tpu_custom_call" | custom-call | tf_op jit(solution)/shard_map/slot7/pallas_call | solution.py:475
  967.7 12.2 psum.152
  988.4 5.1 fusion.83
  993.6 5.1 multiply_convert_fusion.1
  1019.6 8.5 fusion.131
  1028.1 10.5 add_convert_fusion.refs_2_
  1038.6 8.3 fusion.129
  1046.9 10.3 add_convert_fusion.1.refs_2_
  1057.2 63.8 %slot8.1 = (bf16[512,2048]{1,0:T(8,128)(2,1)}, f32[512,1024]{1,0:T(8,128)}, f32[256,2048]{1,0:T(8,128)}) custom-call(bf16[512,512]{1,0:T(8,128)(2,1)} %get-tuple-element.133.refs_0_, bf16[2048,1024]{1,0:T(8,128)(2,1)} %pad_maximum_fusion.refs_1_, bf16[2048,2048]{1,0:T(8,128)(2,1)} %add_convert_fusion.1.refs_2_), custom_call_target="tpu_custom_call" | custom-call | tf_op jit(solution)/shard_map/slot8/pallas_call | solution.py:475
  1153.0 8.5 all-reduce.2
  1165.0 5.1 multiply_convert_fusion
  1204.9 77.6 %slot9.1 = (f32[512,512]{1,0:T(8,128)}, f32[512,1024]{1,0:T(8,128)}, f32[256,2048]{1,0:T(8,128)}) custom-call(bf16[512,2048]{1,0:T(8,128)(2,1)} %add_convert_fusion.8.refs_0_, bf16[2048,1024]{1,0:T(8,128)(2,1)} %pad_maximum_fusion.1.refs_1_, bf16[2048,2048]{1,0:T(8,128)(2,1)} %add_convert_fusion.refs_2_), custom_call_target="tpu_custom_call" | custom-call | tf_op jit(solution)/shard_map/slot9/pallas_call | solution.py:475
  1308.2 14.7 %all-reduce = (f32[512]{0:T(512)}, f32[512]{0:T(512)}, f32[512]{0:T(512)}, f32[512]{0:T(512)}) all-reduce(f32[512]{0:T(512)S(1)} %add.252, f32[512]{0:T(512)S(1)} %add.253, f32[512]{0:T(512)S(1)} %copy-done.130, f32[512]{0:T(512)S(1)} %copy-done.129), channel_id=1, replica_groups=mesh['dp'=2,'ctx'=4,'tp'=4] {'dp','ctx'}, use_global_device_ids=true, to_apply=%region_40.41 | all-reduce | flops 2048 | bytes 16384 | tf_op jit(solution)/shard_map/psum | solution.py:1035
  1322.8 16.8 %all-reduce.1 = (f32[512]{0:T(512)S(1)}, f32[512]{0:T(512)S(1)}) all-reduce(f32[512]{0:T(512)S(1)} %get-tuple-element.90, f32[512]{0:T(512)S(1)} %get-tuple-element.86), channel_id=1, replica_groups=mesh['dp'=2,'ctx'=4,'tp'=4] {'tp'}, use_global_device_ids=true, to_apply=%region_35.36 | all-reduce | flops 1024 | bytes 8192 | tf_op jit(solution)/shard_map/psum | solution.py:859
  1355.8 84.0 %slot10.1 = (f32[512,512]{1,0:T(8,128)}, f32[512,256]{1,0:T(8,128)}, f32[256,512]{1,0:T(8,128)}, f32[256,512]{1,0:T(8,128)}, f32[256,512]{1,0:T(8,128)}) custom-call(bf16[512,2048]{1,0:T(8,128)(2,1)} %add_convert_fusion.7.refs_0_, bf16[512,2048]{1,0:T(8,128)(2,1)} %add_convert_fusion.6.refs_1_, bf16[2048,512]{1,0:T(8,128)(2,1)} %add_convert_fusion.5.refs_2_, ...), custom_call_target="tpu_custom_call" | custom-call | tf_op jit(solution)/shard_map/slot10/pallas_call | solution.py:475
  (510 shorter events, 267.0 us)
Async XLA Ops:
  0.6 12.1 copy-start.88
  13.7 841.9 %copy-start.8 = (bf16[2,256,512]{2,1,0:T(8,128)(2,1)}, bf16[2,256,512]{2,1,0:T(8,128)(2,1)S(1)}, u32[]{:S(2)}) copy-start(bf16[2,256,512]{2,1,0:T(8,128)(2,1)S(1)} %get-tuple-element.142) | copy-start | bytes 1572868
  16.6 209.8 %copy-start.55 = (f32[512,64]{1,0:T(8,128)}, f32[512,64]{1,0:T(8,128)S(1)}, u32[]{:S(2)}) copy-start(f32[512,64]{1,0:T(8,128)S(1)} %get-tuple-element.167) | copy-start | bytes 393220
  16.6 209.8 %copy-start.59 = (f32[512,64]{1,0:T(8,128)}, f32[512,64]{1,0:T(8,128)S(1)}, u32[]{:S(2)}) copy-start(f32[512,64]{1,0:T(8,128)S(1)} %get-tuple-element.171) | copy-start | bytes 393220
  16.6 344.6 %copy-start.53 = (f32[512,64]{1,0:T(8,128)}, f32[512,64]{1,0:T(8,128)S(1)}, u32[]{:S(2)}) copy-start(f32[512,64]{1,0:T(8,128)S(1)} %get-tuple-element.172) | copy-start | bytes 393220
  86.8 12.7 copy-start.101
  88.1 18.0 %copy-start.24 = (f32[512,512]{0,1:T(8,128)}, f32[512,512]{0,1:T(8,128)S(1)}, u32[]{:S(2)}) copy-start(f32[512,512]{0,1:T(8,128)S(1)} %get-tuple-element.175) | copy-start | bytes 3145732
  194.7 36.1 %copy-start.17 = (bf16[4,2,256,1,4,128]{5,4,3,2,1,0:T(4,128)(2,1)}, bf16[4,2,256,1,4,128]{5,4,3,2,1,0:T(4,128)(2,1)S(1)}, u32[]{:S(2)}) copy-start(bf16[4,2,256,1,4,128]{5,4,3,2,1,0:T(4,128)(2,1)S(1)} %get-tuple-element.115) | copy-start | bytes 6291460
  201.8 17.5 %copy-start.99 = (f32[512]{0:T(512)S(1)}, f32[512]{0:T(512)}, u32[]{:S(2)}) copy-start(f32[512]{0:T(512)} %param.26) | copy-start | bytes 6148
  212.1 8.6 copy-start.125
  324.2 30.1 %copy-start.32 = (bf16[2,256,512]{2,1,0:T(8,128)(2,1)S(1)}, bf16[2,256,512]{2,1,0:T(8,128)(2,1)}, u32[]{:S(2)}) copy-start(bf16[2,256,512]{2,1,0:T(8,128)(2,1)} %get-tuple-element.151) | copy-start | bytes 1572868
  324.2 30.1 %copy-start.98 = (f32[512]{0:T(512)S(1)}, f32[512]{0:T(512)}, u32[]{:S(2)}) copy-start(f32[512]{0:T(512)} %param.28) | copy-start | bytes 6148
  324.2 31.2 %copy-start.23 = (f32[512,512]{0,1:T(8,128)S(1)}, f32[512,512]{0,1:T(8,128)}, u32[]{:S(2)}) copy-start(f32[512,512]{0,1:T(8,128)} %get-tuple-element.183) | copy-start | bytes 3145732
  377.7 115.8 %copy-start.30 = (bf16[2,256,512]{2,1,0:T(8,128)(2,1)S(1)}, bf16[2,256,512]{2,1,0:T(8,128)(2,1)}, u32[]{:S(2)}) copy-start(bf16[2,256,512]{2,1,0:T(8,128)(2,1)} %get-tuple-element.152) | copy-start | bytes 1572868
  493.5 10.1 copy-start.117
  493.5 10.1 copy-start.105
  493.5 10.1 slice-start.4
  495.9 15.5 %slice-start.8 = ((s8[8388608]{0:T(1024)(128)(4,1)}), s8[4194304]{0:T(1024)(128)(4,1)S(1)}, s32[]{:S(2)}) async-start(s8[8388608]{0:T(1024)(128)(4,1)} %bitcast.406), calls=%async_computation.8 | async-start | bytes 8388608
  511.4 87.8 %copy-start.97 = (f32[512]{0:T(512)S(1)}, f32[512]{0:T(512)}, u32[]{:S(2)}) copy-start(f32[512]{0:T(512)} %param.29) | copy-start | bytes 6148
  585.8 26.1 %copy-start.137 = (bf16[512,2048]{1,0:T(8,128)(2,1)S(1)}, bf16[512,2048]{1,0:T(8,128)(2,1)}, u32[]{:S(2)}) copy-start(bf16[512,2048]{1,0:T(8,128)(2,1)} %get-tuple-element.62) | copy-start | bytes 6291460
  609.4 9.4 slice-start.6
  611.8 15.0 %slice-start.10 = ((s8[8388608]{0:T(1024)(128)(4,1)}), s8[4194304]{0:T(1024)(128)(4,1)S(1)}, s32[]{:S(2)}) async-start(s8[8388608]{0:T(1024)(128)(4,1)} %bitcast.408), calls=%async_computation.10 | async-start | bytes 8388608
  626.8 68.5 %copy-start.154 = (f32[512,2048]{1,0:T(8,128)S(1)}, f32[512,2048]{1,0:T(8,128)}, u32[]{:S(2)}) copy-start(f32[512,2048]{1,0:T(8,128)} %copy-done.153) | copy-start | bytes 12582916
  695.3 12.8 copy-start.10
  695.3 25.3 %copy-start.6 = (bf16[2,256,512]{2,1,0:T(8,128)(2,1)S(1)}, bf16[2,256,512]{2,1,0:T(8,128)(2,1)}, u32[]{:S(2)}) copy-start(bf16[2,256,512]{2,1,0:T(8,128)(2,1)} %get-tuple-element.141) | copy-start | bytes 1572868
  833.6 9.4 copy-start.13
  833.6 9.4 copy-start.20
  833.6 9.4 copy-start.104
  833.6 21.9 %copy-start.128 = (f32[512]{0:T(512)S(1)}, f32[512]{0:T(512)}, u32[]{:S(2)}) copy-start(f32[512]{0:T(512)} %copy-done.127) | copy-start | bytes 6148
  833.6 22.0 %copy-start.11 = (f32[512,512]{1,0:T(8,128)S(1)}, f32[512,512]{1,0:T(8,128)}, u32[]{:S(2)}) copy-start(f32[512,512]{1,0:T(8,128)} %get-tuple-element.61) | copy-start | bytes 3145732
  877.5 88.0 %copy-start.14 = (f32[512,512]{1,0:T(8,128)S(1)}, f32[512,512]{1,0:T(8,128)}, u32[]{:S(2)}) copy-start(f32[512,512]{1,0:T(8,128)} %get-tuple-element.60) | copy-start | bytes 3145732
  877.5 88.0 %copy-start.106 = (f32[512]{0:T(512)S(1)}, f32[512]{0:T(512)}, u32[]{:S(2)}) copy-start(f32[512]{0:T(512)} %copy-done.105) | copy-start | bytes 6148
  877.5 102.4 %copy-start.118 = (f32[512]{0:T(512)S(1)}, f32[512]{0:T(512)}, u32[]{:S(2)}) copy-start(f32[512]{0:T(512)} %copy-done.117) | copy-start | bytes 6148
  877.5 102.4 %copy-start.31 = (bf16[2,256,512]{2,1,0:T(8,128)(2,1)S(1)}, bf16[2,256,512]{2,1,0:T(8,128)(2,1)}, u32[]{:S(2)}) copy-start(bf16[2,256,512]{2,1,0:T(8,128)(2,1)} %get-tuple-element.152) | copy-start | bytes 1572868
  988.4 10.3 slice-start.2
  1028.1 10.5 copy-start.141
  1057.2 63.9 %copy-start.2 = (f32[512,2048]{1,0:T(8,128)S(1)}, f32[512,2048]{1,0:T(8,128)}, u32[]{:S(2)}) copy-start(f32[512,2048]{1,0:T(8,128)} %fusion.83) | copy-start | bytes 12582916
  1057.2 63.9 %copy-start.58 = (f32[2,256,4,128]{3,2,1,0:T(4,128)S(1)}, f32[2,256,4,128]{3,2,1,0:T(4,128)}, u32[]{:S(2)}) copy-start(f32[2,256,4,128]{3,2,1,0:T(4,128)} %copy-done.57) | copy-start | bytes 3145732
  1127.9 8.7 copy-start.49
  1146.0 15.5 %copy-start.126 = (f32[512]{0:T(512)S(1)}, f32[512]{0:T(512)}, u32[]{:S(2)}) copy-start(f32[512]{0:T(512)} %copy-done.125) | copy-start | bytes 6148
  1148.9 15.1 %copy-start.116 = (f32[512]{0:T(512)S(1)}, f32[512]{0:T(512)}, u32[]{:S(2)}) copy-start(f32[512]{0:T(512)} %copy-done.115) | copy-start | bytes 6148
  1151.4 13.5 copy-start.119
  1161.5 8.6 slice-start
  1204.9 77.6 %copy-start.5 = (bf16[512,2048]{1,0:T(8,128)(2,1)S(1)}, bf16[512,2048]{1,0:T(8,128)(2,1)}, u32[]{:S(2)}) copy-start(bf16[512,2048]{1,0:T(8,128)(2,1)} %get-tuple-element.53) | copy-start | bytes 6291460
  1300.9 38.8 %copy-start.124 = (f32[512]{0:T(512)S(1)}, f32[512]{0:T(512)}, u32[]{:S(2)}) copy-start(f32[512]{0:T(512)} %copy-done.123) | copy-start | bytes 6148
  1355.8 84.1 %copy-start.7 = (bf16[2,256,512]{2,1,0:T(8,128)(2,1)S(1)}, bf16[2,256,512]{2,1,0:T(8,128)(2,1)}, u32[]{:S(2)}) copy-start(bf16[2,256,512]{2,1,0:T(8,128)(2,1)} %get-tuple-element.141) | copy-start | bytes 1572868
  1355.8 84.1 %copy-start.19 = (f32[512,512]{1,0:T(8,128)S(1)}, f32[512,512]{1,0:T(8,128)}, u32[]{:S(2)}) copy-start(f32[512,512]{1,0:T(8,128)} %get-tuple-element.68) | copy-start | bytes 3145732
  1355.8 85.8 %copy-start.86 = (bf16[512,512]{1,0:T(8,128)(2,1)S(1)}, bf16[512,512]{1,0:T(8,128)(2,1)}, u32[]{:S(2)}) copy-start(bf16[512,512]{1,0:T(8,128)(2,1)} %add_convert_fusion.12) | copy-start | bytes 1572868
  (119 other events, 503.9 us)

commit v2 on v0

--- a/solution.py
+++ b/solution.py
@@ -1,54 +1,1258 @@
+import functools
 import math
 
 import jax
 import jax.numpy as jnp
 from jax import lax
+from jax.experimental import pallas as pl
+from jax.experimental.pallas import tpu as pltpu
 from jax.sharding import PartitionSpec as P
 
 D = 2048
 HEAD_DIM = 128
-MICRO = 2
-
-
 EPS = 1e-06
 THETA = 500000.0
 NEG = -1e30
-
-
-def row_total(value):
+BF = jnp.bfloat16
+F32 = jnp.float32
+MESH = pl.DeviceIdType.MESH
+HBM = pl.BlockSpec(memory_space=pltpu.HBM)
+
+
+class Place:
+    def __init__(self, tp_size):
+        self.n = tp_size
+        self.tp = lax.axis_index("tp")
+        self.dp = lax.axis_index("dp")
+        self.ctx = lax.axis_index("ctx")
+        self.slot = self.dp * 4 + self.ctx
+
+
+class Task:
+    inputs = ()
+    outputs = ()
+    scratch = ()
+    sems = 0
+    axes = ()
+    after = None
+    done = None
+
+    def emit(self, place, ins, outs, scr, sem):
+        raise NotImplementedError
+
+
+def remote(src, dst, sem, send, recv, device):
+    return pltpu.make_async_remote_copy(
+        src_ref=src, dst_ref=dst, send_sem=sem.at(send), recv_sem=sem.at(recv), device_id=device, device_id_type=MESH
+    )
+
+
+class PlaneGather(Task):
+    def __init__(self, array, dim, with_dp, rank=0.0, lean=False, after=None, done=None):
+        self.dim, self.with_dp, self.rank, self.lean = dim, with_dp, rank, lean
+        self.after, self.done = after, done
+        self.inputs = (array,)
+        shape = list(array.shape)
+        self.size = shape[dim]
+        self.rows = shape[0]
+        self.blocks = 8 if with_dp else 4
+        shape[dim] *= self.blocks
+        self.outputs = (jax.ShapeDtypeStruct(tuple(shape), array.dtype),)
+        self.axes = ("ctx", "dp") if with_dp else ("ctx",)
+        self.sems = 1 + 2 * (3 + 2 + 2 + 2 + 2)
+        self.unit = math.prod(array.shape) * 2 * 2 / 88e3
+
+    def emit(self, place, ins, outs, scr, sem):
+        src, out = ins[0], outs[0]
+        dp, ctx = place.dp, place.ctx
+        half = self.rows // 2
+
+        def spot(d, c, part=None):
+            block = d * 4 + c if self.with_dp else c
+            where = pl.ds(pl.multiple_of(block * self.size, self.size), self.size)
+            if self.dim == 1:
+                if part is None:
+                    return out.at[:, where]
+                return out.at[pl.ds(part * half, half), where]
+            if part is None:
+                return out.at[where]
+            return out.at[pl.ds(pl.multiple_of(block * self.size + part * half, half), half)]
+
+        xdev, ydev, cdev = {"ctx": ctx ^ 2}, {"dp": dp ^ 1}, {"ctx": ctx ^ 1}
+        mine = spot(dp, ctx)
+        own = pltpu.make_async_copy(src, mine, sem.at(0))
+        own.start()
+        sends = []
+
+        def send(index, origin, target, device):
+            copy = remote(origin, target, sem, 1 + 2 * index, 2 + 2 * index, device)
+            copy.start()
+            sends.append(copy)
+
+        def got(index, target):
+            remote(target, target, sem, 1 + 2 * index, 2 + 2 * index, cdev).wait_recv()
+
+        send(0, src, mine, xdev)
+        if self.with_dp:
+            send(1, src, mine, ydev)
+        send(2, src, mine, cdev)
+        yield self.rank + self.unit * 1.0
+        from_x = spot(dp, ctx ^ 2)
+        got(0, from_x)
+        if self.with_dp and self.lean:
+            send(3, from_x, from_x, ydev)
+        elif self.with_dp:
+            send(3, spot(dp, ctx ^ 2, 0), spot(dp, ctx ^ 2, 0), ydev)
+        send(5, from_x, from_x, cdev)
+        if self.with_dp:
+            from_y = spot(dp ^ 1, ctx)
+            got(1, from_y)
+            parts = (None,) if self.lean else (0, 1)
+            if not self.lean:
+                send(4, spot(dp ^ 1, ctx, 1), spot(dp ^ 1, ctx, 1), xdev)
+            send(6, from_y, from_y, cdev)
+            yield self.rank + self.unit * (2.0 if self.lean else 1.5)
+            for k, part in enumerate(parts):
+                diagonal = spot(dp ^ 1, ctx ^ 2, part)
+                got(3 + k, diagonal)
+                send(7 + k, diagonal, diagonal, cdev)
+        yield self.rank + self.unit * (2.1 if self.lean else 1.6)
+        got(2, spot(dp, ctx ^ 1))
+        got(5, spot(dp, ctx ^ 3))
+        if self.with_dp:
+            got(6, spot(dp ^ 1, ctx ^ 1))
+            for k, part in enumerate(parts):
+                got(7 + k, spot(dp ^ 1, ctx ^ 3, part))
+        for copy in sends:
+            copy.wait_send()
+        own.wait()
+
+
+class PlaneScatter(Task):
+    def __init__(self, array, dim, with_dp, rank=0.0, lean=False, after=None, done=None):
+        self.dim, self.with_dp, self.rank, self.lean = dim, with_dp, rank, lean
+        self.after, self.done = after, done
+        self.inputs = (array,)
+        shape = list(array.shape)
+        self.blocks = 8 if with_dp else 4
+        shape[dim] //= self.blocks
+        self.size = shape[dim]
+        self.rows, self.width = shape
+        self.outputs = (jax.ShapeDtypeStruct(tuple(shape), F32),)
+        self.axes = ("ctx", "dp") if with_dp else ("ctx",)
+        chips = self.blocks // 2
+        self.chips = chips
+        block = (self.rows, self.width)
+        self.scratch = (
+            pltpu.VMEM((chips,) + block, BF),
+            pltpu.VMEM((chips,) + block, BF),
+            pltpu.VMEM((2,) + block, BF),
+            pltpu.VMEM((self.rows, self.width), BF),
+            pltpu.VMEM(block, F32),
+        )
+        self.sems = 2 * chips + chips + 1 + 2 * 6
+        self.unit = self.rows * self.width * 2 * 2 / 88e3
+
+    def emit(self, place, ins, outs, scr, sem):
+        src, out = ins[0], outs[0]
+        mine, came, chip_in, diag_in, total = scr
+        dp, ctx = place.dp, place.ctx
+        core = ctx & 1
+        chips = self.chips
+        half = self.rows // 2
+        tile = min(32, half)
+        xdev, ydev, cdev = {"ctx": ctx ^ 2}, {"dp": dp ^ 1}, {"ctx": ctx ^ 1}
+
+        def place_of(q):
+            x = (ctx >> 1) ^ (q & 1)
+            d = dp ^ (q >> 1)
+            return d, x
+
+        def spot(q, c):
+            d, x = place_of(q)
+            block = d * 4 + x * 2 + c if self.with_dp else x * 2 + c
+            where = pl.ds(pl.multiple_of(block * self.size, self.size), self.size)
+            return src.at[:, where] if self.dim == 1 else src.at[where]
+
+        order = (3, 1, 2, 0) if self.with_dp else (1, 0)
+        sends = []
+        loads = {}
+        for q in order:
+            copy = remote(spot(q, core ^ 1), came.at[q], sem, 2 * q, 2 * q + 1, cdev)
+            copy.start()
+            sends.append(copy)
+            load = pltpu.make_async_copy(spot(q, core), mine.at[q], sem.at(2 * chips + q))
+            load.start()
+            loads[q] = (load, copy)
+        base = 3 * chips + 1
+
+        def hop(index, origin, target, device):
+            copy = remote(origin, target, sem, base + 2 * index, base + 2 * index + 1, device)
+            copy.start()
+            sends.append(copy)
+            return copy
+
+        def got(index, target):
+            remote(target, target, sem, base + 2 * index, base + 2 * index + 1, cdev).wait_recv()
+
+        def add(into, other, first, count):
+            @pl.loop(0, count // tile)
+            def _(i):
+                part = pl.ds(pl.multiple_of(first + i * tile, tile), tile)
+                into[part] = (into[part].astype(F32) + other[part].astype(F32)).astype(BF)
+
+        top, low = pl.ds(0, half), pl.ds(half, half)
+        yield self.rank + 4.0
+        for q in order:
+            load, copy = loads[q]
+            load.wait()
+            copy.wait_recv()
+            add(mine.at[q], came.at[q], 0, self.rows)
+            if q == 3 and self.lean:
+                hop(1, mine.at[3], diag_in, ydev)
+            elif q == 3:
+                hop(0, mine.at[3, top], diag_in.at[top], xdev)
+                hop(1, mine.at[3, low], diag_in.at[low], ydev)
+            if q == 1 and self.with_dp and not self.lean:
+                hop(2, mine.at[1, top], chip_in.at[0, top], xdev)
+            if q == 1 and not self.with_dp:
+                hop(2, mine.at[1], chip_in.at[0], xdev)
+            if q == 2 and self.lean:
+                hop(3, mine.at[2], chip_in.at[1], ydev)
+            elif q == 2:
+                hop(3, mine.at[2, low], chip_in.at[1, low], ydev)
+        if self.lean:
+            yield self.rank + 4.0 + self.unit * 1.2
+            got(1, diag_in)
+            add(mine.at[1], diag_in, 0, self.rows)
+            hop(5, mine.at[1], chip_in.at[0], xdev)
+        elif self.with_dp:
+            yield self.rank + 4.0 + self.unit * 0.7
+            got(0, diag_in.at[top])
+            add(mine.at[2], diag_in, 0, half)
+            hop(4, mine.at[2, top], chip_in.at[1, top], ydev)
+            got(1, diag_in.at[low])
+            add(mine.at[1], diag_in, half, half)
+            hop(5, mine.at[1, low], chip_in.at[0, low], xdev)
+        yield self.rank + 4.0 + self.unit * (2.2 if self.lean else 1.6)
+        if self.lean:
+            got(5, chip_in.at[0])
+            got(3, chip_in.at[1])
+        elif self.with_dp:
+            got(2, chip_in.at[0, top])
+            got(5, chip_in.at[0, low])
+            got(3, chip_in.at[1, low])
+            got(4, chip_in.at[1, top])
+        else:
+            got(2, chip_in.at[0])
+
+        @pl.loop(0, self.rows // tile)
+        def _(i):
+            part = pl.ds(pl.multiple_of(i * tile, tile), tile)
+            value = mine[0, part].astype(F32) + chip_in[0, part].astype(F32)
+            if self.with_dp:
+                value = value + chip_in[1, part].astype(F32)
+            total[part] = value
+
+        last = pltpu.make_async_copy(total, out, sem.at(3 * chips))
+        last.start()
+        for copy in sends:
+            copy.wait_send()
+        last.wait()
+
+
+class Handle:
+    ref = None
+    sem = None
+    waited = False
+    lazy = False
+    value = None
+
+    def __init__(self, shape=None, dtype=None):
+        self.shape, self.dtype = shape, dtype
+
+
+class Slot:
+    def __init__(self, name, ident):
+        self.name, self.ident = name, ident
+        self.inputs, self.outputs, self.scratch = [], [], []
+        self.sem_count = 0
+        self.tasks = []
+        self.axes = set()
+        self.early = []
+        self.loads, self.stores = [], []
+        self.flags = {}
+        self.now = 0.0
+
+    def sems(self, number):
+        first = self.sem_count
+        self.sem_count += number
+        return first
+
+    def hbm_in(self, array):
+        if isinstance(array, Handle):
+            return array
+        handle = Handle(array.shape, array.dtype)
+        self.inputs.append((array, handle))
+        return handle
+
+    def hbm_out(self, shape, dtype):
+        handle = Handle(shape, dtype)
+        self.outputs.append((jax.ShapeDtypeStruct(shape, dtype), handle))
+        return handle
+
+    def vmem(self, shape, dtype):
+        handle = Handle(shape, dtype)
+        self.scratch.append((pltpu.VMEM(shape, dtype), handle))
+        return handle
+
+    def load(self, array):
+        handle = self.vmem(array.shape, array.dtype)
+        handle.source = self.hbm_in(array)
+        handle.sem = self.sems(1)
+        self.loads.append(handle)
+        return handle
+
+    def store(self, shape, dtype):
+        handle = self.vmem(shape, dtype)
+        handle.target = self.hbm_out(shape, dtype)
+        handle.sem = self.sems(1)
+        self.stores.append(handle)
+        return handle
+
+    def late(self, array):
+        handle = self.vmem(array.shape, array.dtype)
+        handle.source = self.hbm_in(array)
+        handle.sem = self.sems(1)
+        handle.lazy = True
+        self.loads.append(handle)
+        return handle
+
+    def fetch(self, *handles):
+        for handle in handles:
+            pltpu.make_async_copy(handle.source.ref, handle.ref, self.sem(handle.sem)).start()
+
+    def need(self, *handles):
+        for handle in handles:
+            if not handle.waited:
+                handle.waited = True
+                pltpu.make_async_copy(handle.source.ref, handle.ref, self.sem(handle.sem)).wait()
+
+    def flush(self, *handles):
+        for handle in handles:
+            pltpu.make_async_copy(handle.ref, handle.target.ref, self.sem(handle.sem)).start()
+
+    def sem(self, index):
+        return self.sem_ref.at[index]
+
+    def at(self, index):
+        return self.sem_ref.at[index]
+
+    def add(self, body):
+        self.tasks.append(body)
+
+    def mark(self, flag):
+        self.flags[flag] = True
+
+    def mark_early(self, flag):
+        self.early.append(flag)
+
+    def kernel(self, *refs):
+        refs = list(refs)
+        for group in (self.inputs, self.outputs, self.scratch):
+            for _, handle in group:
+                handle.ref = refs.pop(0)
+        self.sem_ref = refs.pop(0)
+        self.flags, self.now = {flag: True for flag in self.early}, 0.0
+        for handle in self.loads:
+            handle.waited = False
+            if not handle.lazy:
+                pltpu.make_async_copy(handle.source.ref, handle.ref, self.sem(handle.sem)).start()
+        self.place = place = Place(4)
+        barrier = pltpu.get_barrier_semaphore()
+        peers = []
+        if "ctx" in self.axes:
+            peers += [{"ctx": place.ctx ^ 1}, {"ctx": place.ctx ^ 2}]
+        if "dp" in self.axes:
+            peers += [{"dp": place.dp ^ 1}]
+        if "tp" in self.axes:
+            peers += [{"tp": place.tp ^ k} for k in (1, 2, 3)]
+        for device in peers:
+            pl.semaphore_signal(barrier, inc=1, device_id=device, device_id_type=MESH)
+        pl.semaphore_wait(barrier, len(peers))
+        running = [[("at", 0.0), task()] for task in self.tasks]
+        while running:
+            ready = None
+            for entry in running:
+                kind, value = entry[0]
+                if (kind == "at" and value <= self.now) or (kind == "flag" and value in self.flags):
+                    ready = entry
+                    break
+            if ready is None:
+                times = [entry[0][1] for entry in running if entry[0][0] == "at"]
+                self.now = min(times)
+                continue
+            try:
+                got = next(ready[1])
+            except StopIteration:
+                running.remove(ready)
+                continue
+            if got[0] == "did":
+                self.now += got[1]
+                got = ("at", self.now)
+            ready[0] = got
+        for handle in self.stores:
+            pltpu.make_async_copy(handle.ref, handle.target.ref, self.sem(handle.sem)).wait()
+
+    def run(self):
+        values = pl.pallas_call(
+            self.kernel,
+            out_shape=tuple(o for o, _ in self.outputs),
+            in_specs=[HBM] * len(self.inputs),
+            out_specs=tuple([HBM] * len(self.outputs)),
+            scratch_shapes=[s for s, _ in self.scratch] + [pltpu.SemaphoreType.DMA((self.sem_count,))],
+            compiler_params=pltpu.CompilerParams(
+                collective_id=self.ident, has_side_effects=True, vmem_limit_bytes=62 * 1024 * 1024
+            ),
+            name=self.name,
+        )(*[a for a, _ in self.inputs])
+        for (_, handle), value in zip(self.outputs, values):
+            handle.value = value
+
+
+def attach(slot, task):
+    ins = [slot.hbm_in(a) for a in task.inputs]
+    outs = [slot.hbm_out(o.shape, o.dtype) for o in task.outputs]
+    scr = []
+    for s in task.scratch:
+        handle = Handle()
+        slot.scratch.append((s, handle))
+        scr.append(handle)
+    first = slot.sems(task.sems)
+    slot.axes |= set(task.axes)
+
+    class View:
+        def at(self, index):
+            return slot.sem_ref.at[first + index]
+
+    def body():
+        if task.after is not None:
+            yield ("flag", task.after)
+            task.rank = slot.now
+        for t in task.emit(slot.place, [h.ref for h in ins], [h.ref for h in outs], [h.ref for h in scr], View()):
+            yield ("at", t)
+        if task.done is not None:
+            slot.mark(task.done)
+
+    slot.add(body)
+    return outs
+
+
+def any_of(me, values):
+    values = sorted(values)
+    cond = me == values[0]
+    for v in values[1:]:
+        cond = jnp.logical_or(cond, me == v)
+    return cond
+
+
+def pick(me, table):
+    items = sorted(table.items())
+    out = jnp.int32(items[0][1])
+    for key, value in items[1:]:
+        out = jnp.where(me == key, jnp.int32(value), out)
+    return out
+
+
+PAIR = {0: ["A0", "R3", "R2", "R1"], 1: ["A1", "A0", "R3", "R2"], 2: ["A2", "A1", "A0", "R3"]}
+ONLY_A = {0: ["A0", "", ""], 1: ["A1", "A0", ""], 2: ["A2", "A1", "A0"]}
+ONLY_R = {0: ["R3", "R2", "R1"], 1: ["", "R3", "R2"], 2: ["", "", "R3"]}
+
+
+class Line:
+    def __init__(self, slot, rows, width, gather=None, scatter=False, pieces=2, keep=True):
+        self.slot, self.rows, self.width, self.pieces = slot, rows, width, pieces
+        self.gather, self.scatter = gather is not None, scatter
+        slot.axes.add("tp")
+        right = PAIR if self.gather and scatter else (ONLY_A if self.gather else ONLY_R)
+        flip = lambda m: m if not m else m[0] + str(3 - int(m[1]))
+        self.tables = (right, {3 - d: [flip(m) for m in row] for d, row in right.items()})
+        self.steps = len(right[0])
+        self.keep = keep
+        if self.gather:
+            self.source = slot.hbm_in(gather)
+            self.wide = slot.vmem((4, rows, width), BF)
+            self.own_sem = slot.sems(1)
+            if keep:
+                self.out = slot.hbm_out((rows, 4 * width), BF)
+                self.out_sem = slot.sems(4)
+        if scatter:
+            self.mine = slot.vmem((4, rows, width), BF)
+            self.came = slot.vmem((2, self.steps, rows, width), BF)
+        self.base = slot.sems(4 * self.steps * pieces)
+        self.unit = rows * width * 4 / 88e3
+        slot.add(self.body)
+
+    def chunk(self, k):
+        me = self.slot.place.tp
+        return (me, pick(me, {0: 1, 1: 2, 2: 1, 3: 2}), pick(me, {0: 2, 1: 0, 2: 3, 3: 1}), pick(me, {0: 3, 1: 3, 2: 0, 3: 0}))[k]
+
+    def index(self, way, t, p):
+        return self.base + 2 * ((way * self.steps + t) * self.pieces + p)
+
+    def part(self, p):
+        step = self.rows // self.pieces
+        return pl.ds(p * step, step)
+
+    def sends(self, t, p):
+        me = self.slot.place.tp
+        rows = self.part(p)
+        for way in (0, 1):
+            for kind in "AR":
+                table = {d: int(row[t][1]) for d, row in self.tables[way].items() if row[t][:1] == kind}
+                if not table:
+                    continue
+                block = pick(me, table)
+                if kind == "A":
+                    target = self.wide.ref.at[block, rows]
+                    origin = self.source.ref.at[rows] if t == 0 else target
+                else:
+                    target = self.came.ref.at[way, t, rows]
+                    origin = self.mine.ref.at[block, rows]
+                index = self.index(way, t, p)
+                to = me + 1 if way == 0 else me - 1
+                yield kind, any_of(me, table), remote(origin, target, self.slot, index, index + 1, {"tp": to})
+
+    def arrivals(self, t, p):
+        me = self.slot.place.tp
+        rows = self.part(p)
+        step = self.rows // self.pieces
+        tile = 64
+        for way in (0, 1):
+            off = 1 if way == 0 else -1
+            froms = {d + off: row[t] for d, row in self.tables[way].items() if row[t]}
+            sample = self.wide.ref.at[0, rows] if self.gather else self.came.ref.at[0, 0, rows]
+            index = self.index(way, t, p)
+            pl.when(any_of(me, froms))(remote(sample, sample, self.slot, index, index + 1, {"tp": me}).wait_recv)
+            adds = {d: int(m[1]) for d, m in froms.items() if m[0] == "R" and int(m[1]) != d}
+            if adds:
+                block = pick(me, adds)
+                mine, came = self.mine.ref, self.came.ref
+
+                @pl.when(any_of(me, adds))
+                def _():
+                    @pl.loop(0, step // tile)
+                    def _(i):
+                        part = pl.ds(pl.multiple_of(p * step + i * tile, tile), tile)
+                        mine[block, part] = (mine[block, part].astype(F32) + came[way, t, part].astype(F32)).astype(BF)
+
+    def body(self):
+        slot = self.slot
+        me = slot.place.tp
+        if self.gather:
+            own = pltpu.make_async_copy(self.source.ref, self.wide.ref.at[me], slot.sem(self.own_sem))
+            own.start()
+        start = 0.0
+        for t in range(self.steps):
+            for p in range(self.pieces):
+                if t > 0:
+                    yield ("at", start + (t - 1 + (p + 1) / self.pieces) * self.unit + 0.5)
+                    self.arrivals(t - 1, p)
+                    if p == self.pieces - 1 and self.gather and t <= 3:
+                        slot.mark("chunk%d" % t)
+                messages = list(self.sends(t, p))
+                for kind, cond, copy in messages:
+                    if kind == "A":
+                        pl.when(cond)(copy.start)
+                if any(kind == "R" for kind, _, _ in messages):
+                    first = t == (1 if self.gather else 0)
+                    if p == 0:
+                        for c in ((3, 0) if first else (2, 1)):
+                            yield ("flag", "part%d" % c)
+                        start = max(start, slot.now - t * self.unit)
+                    for kind, cond, copy in messages:
+                        if kind == "R":
+                            pl.when(cond)(copy.start)
+                if t == 0 and p == 0 and self.gather:
+                    yield ("at", 1.0)
+                    own.wait()
+                    slot.mark("chunk0")
+        for p in range(self.pieces):
+            yield ("at", start + (self.steps - 1 + (p + 1) / self.pieces) * self.unit + 0.5)
+            self.arrivals(self.steps - 1, p)
+        if self.gather and self.steps == 3:
+            slot.mark("chunk3")
+        if self.scatter:
+            slot.mark("reduced")
+        outs = []
+        if self.gather and self.keep:
+            for c in range(4):
+                where = self.out.ref.at[:, pl.ds(c * self.width, self.width)]
+                outs.append(pltpu.make_async_copy(self.wide.ref.at[c], where, slot.sem(self.out_sem + c)))
+                outs[-1].start()
+        yield ("at", start + self.steps * self.unit + 1.0)
+        for t in range(self.steps):
+            for p in range(self.pieces):
+                for _, cond, copy in self.sends(t, p):
+                    pl.when(cond)(copy.wait_send)
+        for copy in outs:
+            copy.wait()
+
+    def total(self, part):
+        me = self.slot.place.tp
+        last = self.steps - 1
+        left = jnp.where(me > 0, self.came.ref[0, last, part].astype(F32), 0.0)
+        right = jnp.where(me < 3, self.came.ref[1, last, part].astype(F32), 0.0)
+        return self.mine.ref[me, part].astype(F32) + left + right
+
+
+def tiled(count, tile, body):
+    @pl.loop(0, count // tile)
+    def _(i):
+        body(pl.ds(pl.multiple_of(i * tile, tile), tile))
+
+
+class Weights:
+    def __init__(self, slot, arrays, shape, order, where):
+        self.slot, self.order, self.where = slot, order, where
+        self.arrays = [slot.hbm_in(a) for a in arrays]
+        self.buffer = slot.vmem((2, len(arrays)) + shape, BF)
+        self.base = slot.sems(2 * len(arrays))
+        self.step = 0
+
+    def copies(self, step):
+        block = self.order[step] if not callable(self.order) else self.order(step)
+        for j, array in enumerate(self.arrays):
+            yield pltpu.make_async_copy(
+                self.where(array.ref, block),
+                self.buffer.ref.at[step % 2, j],
+                self.slot.sem(self.base + 2 * j + step % 2),
+            )
+
+    def start(self, step):
+        for copy in self.copies(step):
+            copy.start()
+
+    def take(self, step):
+        for copy in self.copies(step):
+            copy.wait()
+        return [self.buffer.ref.at[step % 2, j] for j in range(len(self.arrays))]
+
+
+def row_block(ref, c):
+    return ref.at[pl.ds(pl.multiple_of(c * 512, 512), 512)]
+
+
+def col_block(ref, c):
+    return ref.at[:, pl.ds(pl.multiple_of(c * 512, 512), 512)]
+
+
+def consume(slot, line, arrays, shape, where, last, multiply, cost, flag):
+    weights = Weights(slot, arrays, shape, line.chunk, where)
+
+    def body():
+        weights.start(0)
+        for k in range(4):
+            if k < 3:
+                weights.start(k + 1)
+            yield ("flag", "chunk%d" % k)
+            blocks = weights.take(k)
+            chunk = line.chunk(k)
+            for j, block in enumerate(blocks):
+                multiply(k == 0, line.wide.ref.at[chunk], block, j)
+                yield ("did", cost)
+        yield from last()
+        slot.mark(flag)
+
+    slot.add(body)
+
+
+def dot_nn(left, right):
+    return jnp.dot(left, right, preferred_element_type=F32)
+
+
+def dot_nt(left, right):
+    return lax.dot_general(left, right, (((1,), (1,)), ((), ())), preferred_element_type=F32)
+
+
+def produce(slot, line, lefts, arrays, shape, where, dot, cost):
+    order = (3, 0, 2, 1)
+    weights = Weights(slot, arrays, shape, order, where)
+
+    def body():
+        weights.start(0)
+        slot.need(*lefts)
+        for k, c in enumerate(order):
+            if k < 3:
+                weights.start(k + 1)
+            blocks = weights.take(k)
+            value = None
+            for left, block in zip(lefts, blocks):
+                term = dot(left.ref[...], block[...])
+                value = term if value is None else value + term
+            line.mine.ref[c] = value.astype(BF)
+            yield ("did", cost)
+            slot.mark("part%d" % c)
+
+    slot.add(body)
+
+
+class RowTotals:
+    def __init__(self, slot, rows):
+        self.slot, self.rows = slot, rows
+        self.stat = slot.vmem((rows, 128), F32)
+        self.send = slot.vmem((8, rows), F32)
+        self.came = slot.vmem((3, 8, rows), F32)
+        self.total = slot.vmem((rows, 128), F32)
+        self.base = slot.sems(6)
+
+    def put(self, part, *columns):
+        lane = lax.broadcasted_iota(jnp.int32, (columns[0].shape[0], 128), 1)
+        value = jnp.zeros((columns[0].shape[0], 128), F32)
+        for k, column in enumerate(columns):
+            value = jnp.where(lane == k, column, value)
+        self.stat.ref[part] = value
+
+    def exchange(self):
+        slot, me = self.slot, self.slot.place.tp
+        send = self.send.ref
+        send[...] = jnp.transpose(self.stat.ref[...])[0:8]
+        copies = []
+        for k in (1, 2, 3):
+            copies.append(
+                remote(send, self.came.ref.at[k - 1], slot, self.base + 2 * (k - 1), self.base + 2 * (k - 1) + 1, {"tp": me ^ k})
+            )
+            copies[-1].start()
+        yield ("at", slot.now + 2.5)
+        for copy in copies:
+            copy.wait()
+        total = send[...] + self.came.ref[0] + self.came.ref[1] + self.came.ref[2]
+        wide = jnp.concatenate([total, jnp.zeros((120, self.rows), F32)], axis=0)
+        self.total.ref[...] = jnp.transpose(wide)
+
+    def column(self, part, k):
+        return self.total.ref[part, k : k + 1]
+
+
+def attn_finish(slot, line, rows, width, x, gain):
+    x, gain = slot.load(x), slot.load(gain.reshape(1, width))
+    raw, resid = slot.store((rows, width), F32), slot.store((rows, width), F32)
+    resid_b, factor = slot.store((rows, width), BF), slot.store((rows, 128), F32)
+    totals = RowTotals(slot, rows)
+
+    def body():
+        yield ("flag", "reduced")
+
+        def first(part):
+            value = line.total(part)
+            raw.ref[part] = value
+            totals.put(part, jnp.sum(value * value, axis=1, keepdims=True))
+
+        tiled(rows, 32, first)
+        slot.need(x, gain)
+        slot.flush(raw)
+        yield from totals.exchange()
+
+        def second(part):
+            scale = lax.rsqrt(totals.column(part, 0) / D + EPS)
+            value = x.ref[part].astype(F32) + raw.ref[part] * scale * gain.ref[...]
+            resid.ref[part] = value
+            resid_b.ref[part] = value.astype(BF)
+            factor.ref[part] = jnp.broadcast_to(scale, (32, 128))
+
+        tiled(rows, 32, second)
+        slot.flush(resid_b, resid, factor)
+
+    slot.add(body)
+    return [raw.target, resid.target, resid_b.target, factor.target]
+
+
+def mlp_finish(slot, line, rows, width, resid, cot, gain):
+    resid, cot, gain = slot.load(resid), slot.load(cot), slot.load(gain.reshape(1, width))
+    raw = slot.vmem((rows, width), F32)
+    out, grad = slot.store((rows, width), BF), slot.store((rows, width), BF)
+    gain_grad = slot.store((8, width), F32)
+    totals = RowTotals(slot, rows)
+
+    def body():
+        yield ("flag", "reduced")
+        slot.need(resid, cot, gain)
+
+        def first(part):
+            value = line.total(part)
+            raw.ref[part] = value
+            scaled = cot.ref[part].astype(F32) * gain.ref[...]
+            totals.put(part, jnp.sum(value * value, axis=1, keepdims=True), jnp.sum(scaled * value, axis=1, keepdims=True))
+
+        tiled(rows, 32, first)
+        gain_grad.ref[...] = jnp.zeros((8, width), F32)
+        yield from totals.exchange()
+
+        def second(part):
+            scale = lax.rsqrt(totals.column(part, 0) / D + EPS)
+            inner = totals.column(part, 1)
+            value = raw.ref[part]
+            given = cot.ref[part].astype(F32)
+            normed = value * scale
+            grad.ref[part] = (scale * (given * gain.ref[...]) - value * (scale * scale * scale * inner / D)).astype(BF)
+            out.ref[part] = (resid.ref[part] + normed * gain.ref[...]).astype(BF)
+            terms = given * normed
+            for i in range(4):
+                gain_grad.ref[...] += terms[8 * i : 8 * i + 8]
+
+        tiled(rows, 32, second)
+        slot.flush(grad, out, gain_grad)
+
+    slot.add(body)
+    return [out.target, grad.target, gain_grad.target]
+
+
+def resid_finish(slot, line, rows, width, cot, attn, factor, gain):
+    cot, attn, factor, gain = slot.load(cot), slot.load(attn), slot.load(factor), slot.load(gain.reshape(1, width))
+    resid, grad = slot.store((rows, width), F32), slot.store((rows, width), BF)
+    gain_grad = slot.store((8, width), F32)
+    totals = RowTotals(slot, rows)
+
+    def body():
+        yield ("flag", "reduced")
+        slot.need(cot, attn, factor, gain)
+
+        def first(part):
+            value = line.total(part) + cot.ref[part].astype(F32)
+            resid.ref[part] = value
+            totals.put(part, jnp.sum(value * gain.ref[...] * attn.ref[part], axis=1, keepdims=True))
+
+        tiled(rows, 32, first)
+        gain_grad.ref[...] = jnp.zeros((8, width), F32)
+        slot.flush(resid)
+        yield from totals.exchange()
+
+        def second(part):
+            scale = factor.ref[part, 0:1]
+            inner = totals.column(part, 0)
+            value, given = attn.ref[part], resid.ref[part]
+            grad.ref[part] = (scale * (given * gain.ref[...]) - value * (scale * scale * scale * inner / D)).astype(BF)
+            terms = given * value * scale
+            for i in range(4):
+                gain_grad.ref[...] += terms[8 * i : 8 * i + 8]
+
+        tiled(rows, 32, second)
+        slot.flush(grad, gain_grad)
+
+    slot.add(body)
+    return [resid.target, grad.target, gain_grad.target]
+
+
+def last_finish(slot, line, rows, width, resid):
+    resid = slot.load(resid)
+    out = slot.store((rows, width), BF)
+
+    def body():
+        yield ("flag", "reduced")
+        slot.need(resid)
+
+        def first(part):
+            out.ref[part] = (line.total(part) + resid.ref[part]).astype(BF)
+
+        tiled(rows, 32, first)
+        slot.flush(out)
+
+    slot.add(body)
+    return [out.target]
+
+
+def given_partial(slot, line, array):
+    source = slot.hbm_in(array)
+    base = slot.sems(4)
+
+    def body():
+        copies = {}
+        for c in (3, 0, 2, 1):
+            copies[c] = pltpu.make_async_copy(
+                source.ref.at[:, pl.ds(c * line.width, line.width)], line.mine.ref.at[c], slot.sem(base + c)
+            )
+            copies[c].start()
+        yield ("at", 1.0)
+        for c in (3, 0, 2, 1):
+            copies[c].wait()
+            slot.mark("part%d" % c)
+
+    slot.add(body)
+
+
+def gate_up(slot, line, rows, w_gate, w_up):
+    ff = w_gate.shape[1]
+    acc = slot.vmem((2, rows, ff), F32)
+    gate, up, act = (slot.store((rows, ff), BF) for _ in range(3))
+
+    def multiply(first, left, block, j):
+        @pl.loop(0, ff // 1024)
+        def _(i):
+            cols = pl.ds(pl.multiple_of(i * 1024, 1024), 1024)
+            value = dot_nn(left[...], block[:, cols])
+            acc.ref[j, :, cols] = value if first else acc.ref[j, :, cols] + value
+
+    def last():
+        half = rows // 2
+        for h in (0, 1):
+
+            @pl.loop(0, half // 16)
+            def _(i):
+                part = pl.ds(pl.multiple_of(h * half + i * 16, 16), 16)
+                g, u = acc.ref[0, part], acc.ref[1, part]
+                gate.ref[part] = g.astype(BF)
+                up.ref[part] = u.astype(BF)
+                act.ref[part] = (g * jax.nn.sigmoid(g) * u).astype(BF)
+
+            yield ("did", 2.0)
+        slot.flush(act, gate, up)
+
+    consume(slot, line, (w_gate, w_up), (512, ff), row_block, last, multiply, 2.2, "mlp")
+    return [gate.target, up.target, act.target]
+
+
+def act_back(slot, line, rows, w_down, gate, up):
+    ff = w_down.shape[0]
+    acc = slot.vmem((rows, ff), F32)
+    gate, up = slot.load(gate), slot.load(up)
+    g_gate, g_up = slot.store((rows, ff), BF), slot.store((rows, ff), BF)
+
+    def multiply(first, left, block, j):
+        @pl.loop(0, ff // 1024)
+        def _(i):
+            cols = pl.ds(pl.multiple_of(i * 1024, 1024), 1024)
+            value = dot_nt(left[...], block[cols])
+            acc.ref[:, cols] = value if first else acc.ref[:, cols] + value
+
+    def last():
+        slot.need(gate, up)
+        half = rows // 2
+        for h in (0, 1):
+
+            @pl.loop(0, half // 16)
+            def _(i):
+                part = pl.ds(pl.multiple_of(h * half + i * 16, 16), 16)
+                grad, g, u = acc.ref[part], gate.ref[part].astype(F32), up.ref[part].astype(F32)
+                sigma = jax.nn.sigmoid(g)
+                g_gate.ref[part] = (grad * u * sigma * (1.0 + g * (1.0 - sigma))).astype(BF)
+                g_up.ref[part] = (grad * g * sigma).astype(BF)
+
+            yield ("did", 2.5)
+        slot.flush(g_gate, g_up)
+
+    consume(slot, line, (w_down,), (ff, 512), col_block, last, multiply, 2.4, "back")
+    return [g_gate.target, g_up.target]
+
+
+def half_turn(value):
+    return pltpu.roll(value, HEAD_DIM // 2, axis=1)
+
+
+def tables(slot, positions, freqs, sign):
+    count = positions.shape[0]
+    positions, freqs, sign = slot.load(positions), slot.load(freqs), slot.load(sign)
+    cosine, sine = slot.store((count, HEAD_DIM), F32), slot.store((count, HEAD_DIM), F32)
+
+    def body():
+        slot.need(positions, freqs, sign)
+
+        def first(part):
+            angle = positions.ref[part].astype(F32) * freqs.ref[...]
+            cosine.ref[part] = jnp.cos(angle)
+            sine.ref[part] = jnp.sin(angle) * sign.ref[...]
+
+        tiled(count, 32, first)
+        slot.flush(cosine, sine)
+        yield ("did", 6.0)
+        slot.mark("tables")
+
+    slot.add(body)
+    return cosine, sine
+
+
+def head_cols(h):
+    return pl.ds(h * HEAD_DIM, HEAD_DIM)
+
+
+def project(slot, line, rows, width, weights, flags, gains, cosine, sine, first_row):
+    stages = [slot.late(w) for w in weights]
+    gains = [slot.load(g.reshape(1, width)) for g in gains]
+    raws = [slot.store((rows, width), F32) for _ in (0, 1)]
+    query, kv = slot.store((rows, width), BF), slot.store((rows, 2 * width), BF)
+    factor = slot.store((rows, 128), F32)
+    totals = RowTotals(slot, rows)
+    half = rows // 2
+
+    def body():
+        for j in range(3):
+            if flags is not None:
+                yield ("flag", flags[j])
+            slot.fetch(stages[j])
+        yield ("flag", "chunk3")
+        wide = line.wide.ref
+        for j in range(3):
+            slot.need(stages[j])
+            weight = stages[j].ref
+
+            @pl.loop(0, 2)
+            def _(i):
+                part = pl.ds(pl.multiple_of(i * half, half), half)
+                value = dot_nn(wide[0, part], weight[0:width])
+                for c in (1, 2, 3):
+                    value = value + dot_nn(wide[c, part], weight[c * width : (c + 1) * width])
+                if j < 2:
+                    raws[j].ref[part] = value
+                else:
+                    kv.ref[part, width : 2 * width] = value.astype(BF)
+
+            yield ("did", 2.0)
+
+        def first(part):
+            q, k = raws[0].ref[part], raws[1].ref[part]
+            totals.put(part, jnp.sum(q * q, axis=1, keepdims=True), jnp.sum(k * k, axis=1, keepdims=True))
+
+        tiled(rows, 32, first)
+        slot.flush(*raws)
+        yield from totals.exchange()
+        yield ("flag", "tables")
+        slot.need(*gains)
+        slot.need(*[t for t in (cosine, sine) if hasattr(t, "source")])
+
+        def second(part, trig):
+            lane = lax.broadcasted_iota(jnp.int32, (32, 128), 1)
+            scales = [lax.rsqrt(totals.column(part, j) / D + EPS) for j in (0, 1)]
+            factor.ref[part] = jnp.where(lane == 0, scales[0], scales[1])
+            co, si = cosine.ref[trig], sine.ref[trig]
+            for j, target in ((0, query), (1, kv)):
+                for h in range(width // HEAD_DIM):
+                    value = raws[j].ref[part, head_cols(h)] * scales[j] * gains[j].ref[:, head_cols(h)]
+                    target.ref[part, head_cols(h)] = (value * co + half_turn(value) * si).astype(BF)
+
+        @pl.loop(0, rows // 32)
+        def _(i):
+            second(pl.ds(pl.multiple_of(i * 32, 32), 32), pl.ds(pl.multiple_of(first_row + i * 32, 32), 32))
+
+        slot.flush(kv, query, factor)
+
+    slot.add(body)
+    return [raws[0].target, raws[1].target, query.target, kv.target, factor.target]
+
+
+class Mask:
+    def __init__(self, slot, seg_all, seg_cols, first, count):
+        self.slot, self.first, self.count = slot, first, count
+        self.keys, self.mine = slot.load(seg_all), slot.load(seg_cols)
+        self.mask = slot.vmem((count, 4 * count), F32)
+
+    def fill(self, s):
+        self.slot.need(self.keys, self.mine)
+        count = self.count
+        ctx = self.slot.place.ctx
+        mine = self.mine.ref[(self.first + s) * count : (self.first + s + 1) * count, 0:1]
+        for c in range(4):
+            keys = self.keys.ref[8 * c + self.first + s : 8 * c + self.first + s + 1, :]
+            row = ctx * count + lax.broadcasted_iota(jnp.int32, (count, count), 0)
+            col = c * count + lax.broadcasted_iota(jnp.int32, (count, count), 1)
+            fine = jnp.logical_and(mine == keys, row >= col)
+            self.mask.ref[:, c * count : (c + 1) * count] = jnp.where(fine, 0.0, NEG)
+
+
+def attend(slot, flag, kv, query, mask, rows, width):
+    kv, query = slot.late(kv), slot.load(query)
+    count = mask.count
+    heads, heads_b = slot.store((rows, width), F32), slot.store((rows, width), BF)
+    logsum = slot.store((rows, 128), F32)
+    logits = slot.vmem((count, 4 * count), F32)
+    scale = 1.0 / math.sqrt(HEAD_DIM)
+
+    def body():
+        yield ("flag", flag)
+        slot.fetch(kv)
+        mask.fill(0)
+        yield ("did", 1.5)
+        slot.need(kv, query)
+        logsum.ref[...] = jnp.zeros((rows, 128), F32)
+        for s in range(rows // count):
+            mine = pl.ds(s * count, count)
+            if s:
+                mask.fill(s)
+
+            @pl.loop(0, width // HEAD_DIM)
+            def _(h):
+                cols = pl.ds(pl.multiple_of(h * HEAD_DIM, HEAD_DIM), HEAD_DIM)
+                vcols = pl.ds(pl.multiple_of(width + h * HEAD_DIM, HEAD_DIM), HEAD_DIM)
+                q = query.ref[mine, cols]
+                peak = jnp.full((count, 1), NEG, F32)
+                for c in range(4):
+                    keys = kv.ref[pl.ds(c * rows + s * count, count), cols]
+                    block = pl.ds(c * count, count)
+                    value = dot_nt(q, keys) * scale + mask.mask.ref[:, block]
+                    logits.ref[:, block] = value
+                    peak = jnp.maximum(peak, jnp.max(value, axis=1, keepdims=True))
+                total = jnp.zeros((count, 1), F32)
+                acc = jnp.zeros((count, HEAD_DIM), F32)
+                for c in range(4):
+                    vals = kv.ref[pl.ds(c * rows + s * count, count), vcols]
+                    weight = jnp.exp(logits.ref[:, pl.ds(c * count, count)] - peak)
+                    total = total + jnp.sum(weight, axis=1, keepdims=True)
+                    acc = acc + dot_nn(weight.astype(BF), vals)
+                out = acc / total
+                heads.ref[mine, cols] = out
+                heads_b.ref[mine, cols] = out.astype(BF)
+                lane = lax.broadcasted_iota(jnp.int32, (count, 128), 1)
+                logsum.ref[mine] = jnp.where(lane == h, peak + jnp.log(total), logsum.ref[mine])
+
+            yield ("did", 4.0)
+        slot.flush(heads_b, heads, logsum)
+
+    slot.add(body)
+    return [heads.target, heads_b.target, logsum.target]
+
+
+def attend_back(slot, line, kv, query, heads, logsum, mask, rows, width, w_out):
+    kv, query, heads, logsum = slot.load(kv), slot.load(query), slot.load(heads), slot.load(logsum)
+    count = mask.count
+    acc = slot.vmem((rows, width), F32)
+    grad = slot.vmem((rows, width), BF)
+    g_query, g_kv = slot.store((rows, width), F32), slot.store((4 * rows, 2 * width), BF)
+    scale = 1.0 / math.sqrt(HEAD_DIM)
+
+    def multiply(first, left, block, j):
+        value = dot_nt(left[...], block[...])
+        acc.ref[...] = value if first else acc.ref[...] + value
+
+    def last():
+        grad.ref[...] = acc.ref[...].astype(BF)
+        slot.need(kv, query, heads, logsum)
+        for s in range(rows // count):
+            mine = pl.ds(s * count, count)
+            mask.fill(s)
+            yield ("did", 1.0)
+
+            @pl.loop(0, width // HEAD_DIM)
+            def _(h):
+                cols = pl.ds(pl.multiple_of(h * HEAD_DIM, HEAD_DIM), HEAD_DIM)
+                vcols = pl.ds(pl.multiple_of(width + h * HEAD_DIM, HEAD_DIM), HEAD_DIM)
+                q, g = query.ref[mine, cols], grad.ref[mine, cols]
+                delta = jnp.sum(g.astype(F32) * heads.ref[mine, cols], axis=1, keepdims=True)
+                lane = lax.broadcasted_iota(jnp.int32, (count, 128), 1)
+                logs = jnp.sum(jnp.where(lane == h, logsum.ref[mine], 0.0), axis=1, keepdims=True)
+                total = jnp.zeros((count, HEAD_DIM), F32)
+                for c in range(4):
+                    there = pl.ds(c * rows + s * count, count)
+                    keys, vals = kv.ref[there, cols], kv.ref[there, vcols]
+                    value = dot_nt(q, keys) * scale + mask.mask.ref[:, pl.ds(c * count, count)]
+                    probs = jnp.exp(value - logs)
+                    slopes = (probs * (dot_nt(g, vals) - delta)).astype(BF)
+                    total = total + dot_nn(slopes, keys)
+                    g_kv.ref[there, cols] = (dot_tn(slopes, q) * scale).astype(BF)
+                    g_kv.ref[there, vcols] = dot_tn(probs.astype(BF), g).astype(BF)
+                g_query.ref[mine, cols] = total * scale
+
+            yield ("did", 8.0)
+        slot.flush(g_kv, g_query)
+
+    consume(slot, line, (w_out,), (width, width), col_block, last, multiply, 0.6, "heads")
+    return [g_query.target, g_kv.target]
+
+
+def dot_tn(left, right):
+    return lax.dot_general(left, right, (((0,), (0,)), ((), ())), preferred_element_type=F32)
+
+
+def project_back(slot, flag, g_query, g_kv, raws, factor, gains, cosine, sine, first_row, rows, width):
+    g_kv = slot.late(g_kv)
+    g_query, factor = slot.load(g_query), slot.load(factor)
+    raws = [slot.load(r) for r in raws]
+    gains = [slot.load(g.reshape(1, width)) for g in gains]
+    cosine, sine = slot.load(cosine), slot.load(sine)
+    outs = [slot.store((rows, width), BF) for _ in range(3)]
+    gain_grads = [slot.store((8, width), F32) for _ in range(2)]
+    totals = RowTotals(slot, rows)
+
+    def body():
+        yield ("flag", flag)
+        slot.fetch(g_kv)
+        yield ("at", slot.now + 1.0)
+        slot.need(g_kv, g_query, factor, cosine, sine, *raws, *gains)
+        for g in gain_grads:
+            g.ref[...] = jnp.zeros((8, width), F32)
+
+        @pl.loop(0, rows // 32)
+        def _(i):
+            part = pl.ds(pl.multiple_of(i * 32, 32), 32)
+            trig = pl.ds(pl.multiple_of(first_row + i * 32, 32), 32)
+            co, si = cosine.ref[trig], sine.ref[trig]
+            sums = []
+            for j, source in ((0, g_query), (1, g_kv)):
+                scale = factor.ref[part, j : j + 1]
+                total = jnp.zeros((32, 1), F32)
+                for h in range(width // HEAD_DIM):
+                    cols = head_cols(h)
+                    value = source.ref[part, cols]
+                    value = value * co - half_turn(value) * si
+                    source.ref[part, cols] = value
+                    raw = raws[j].ref[part, cols]
+                    total = total + jnp.sum(value * gains[j].ref[:, cols] * raw, axis=1, keepdims=True)
+                    terms = value * raw * scale
+                    for r in range(4):
+                        gain_grads[j].ref[:, cols] += terms[8 * r : 8 * r + 8]
+                sums.append(total)
+            totals.put(part, *sums)
+
+        slot.flush(*gain_grads)
+        yield ("did", 3.0)
+        yield from totals.exchange()
+
+        def second(part):
+            for j, source in ((0, g_query), (1, g_kv)):
+                scale = factor.ref[part, j : j + 1]
+                inner = totals.column(part, j)
+                value = source.ref[part, 0:width] * gains[j].ref[...]
+                outs[j].ref[part] = (scale * value - raws[j].ref[part] * (scale * scale * scale * inner / D)).astype(BF)
+            outs[2].ref[part] = g_kv.ref[part, width : 2 * width].astype(BF)
+
+        tiled(rows, 32, second)
+        slot.flush(*outs)
+
+    slot.add(body)
+    return [h.target for h in outs + gain_grads]
+
+
+def general_row_total(value):
     return lax.psum(value, "tp")
 
 
-def widen(value):
+def general_widen(value):
     return lax.all_gather(value, "tp", axis=1, tiled=True)
 
 
-def narrow(value):
+def general_narrow(value):
     return lax.psum_scatter(
         value.astype(jnp.bfloat16), "tp", scatter_dimension=1, tiled=True
     ).astype(jnp.float32)
 
 
-def contract_last(left, right):
+def general_contract_last(left, right):
     return lax.dot_general(
         left, right, (((1,), (1,)), ((), ())), preferred_element_type=jnp.float32
     )
 
 
-def contract_first(left, right):
+def general_contract_first(left, right):
     return lax.dot_general(
         left, right, (((0,), (0,)), ((), ())), preferred_element_type=jnp.float32
     )
 
 
-def rotary(positions, depth):
+def general_rotary(positions, depth):
     half = depth // 2
     freqs = THETA ** (-(jnp.arange(half, dtype=jnp.float32) * 2.0) / depth)
     angles = positions.astype(jnp.float32)[..., None] * freqs
     return (jnp.cos(angles)[..., None, :], jnp.sin(angles)[..., None, :])
 
 
-def turn(value, cosine, sine):
+def general_turn(value, cosine, sine):
     half = value.shape[-1] // 2
     first = value[..., :half]
     second = value[..., half:]
@@ -57,7 +1261,7 @@
     )
 
 
-def turn_back(grad, cosine, sine):
+def general_turn_back(grad, cosine, sine):
     half = grad.shape[-1] // 2
     first = grad[..., :half]
     second = grad[..., half:]
@@ -66,11 +1270,11 @@
     )
 
 
-def norm_grad(scaled, value, factor, inner):
+def general_norm_grad(scaled, value, factor, inner):
     return factor[:, None] * scaled - value * (factor**3 * inner / D)[:, None]
 
 
-def local(
+def general(
     hidden,
     cotangent,
     segments,
@@ -88,7 +1292,7 @@
     mlp_gain,
 ):
     local_seqs, slice_len, local_width = hidden.shape
-    per_batch = local_seqs // MICRO
+    per_batch = local_seqs // 2
     rows = per_batch * slice_len
     heads_here = q_gain.shape[0] // HEAD_DIM
     scale = 1.0 / math.sqrt(HEAD_DIM)
@@ -100,7 +1304,7 @@
     k_gain_grad = jnp.zeros(k_gain.shape, jnp.float32)
     attn_gain_grad = jnp.zeros(attn_gain.shape, jnp.float32)
     mlp_gain_grad = jnp.zeros(mlp_gain.shape, jnp.float32)
-    for batch in range(MICRO):
+    for batch in range(2):
         lower = batch * per_batch
         tokens_in = hidden[lower : lower + per_batch].reshape(rows, local_width)
         seg_here = segments[lower : lower + per_batch]
@@ -117,22 +1321,22 @@
         query_full, key_full, value_full, out_full, gate_full, up_full, down_full = gathered
         if weight_grads is None:
             weight_grads = tuple((jnp.zeros(tensor.shape, jnp.float32) for tensor in gathered))
-        wide_in = widen(tokens_in)
+        wide_in = general_widen(tokens_in)
         query_raw = jnp.dot(wide_in, query_full, preferred_element_type=jnp.float32)
         key_raw = jnp.dot(wide_in, key_full, preferred_element_type=jnp.float32)
         value_raw = jnp.dot(wide_in, value_full, preferred_element_type=jnp.float32)
-        query_sq, key_sq = row_total(
+        query_sq, key_sq = general_row_total(
             (jnp.sum(query_raw * query_raw, axis=1), jnp.sum(key_raw * key_raw, axis=1))
         )
         query_scale = lax.rsqrt(query_sq / D + EPS)
         key_scale = lax.rsqrt(key_sq / D + EPS)
-        cosine, sine = rotary(pos_here, HEAD_DIM)
-        query_rot = turn(
+        cosine, sine = general_rotary(pos_here, HEAD_DIM)
+        query_rot = general_turn(
             (query_raw * query_scale[:, None] * q_gain).reshape(rows, heads_here, HEAD_DIM),
             cosine,
             sine,
         )
-        key_rot = turn(
+        key_rot = general_turn(
             (key_raw * key_scale[:, None] * k_gain).reshape(rows, heads_here, HEAD_DIM),
             cosine,
             sine,
@@ -177,17 +1381,17 @@
             (accum / total[..., None]).transpose(0, 2, 1, 3).reshape(rows, heads_here * HEAD_DIM)
         )
         out_b = out_heads.astype(jnp.bfloat16)
-        attn_raw = narrow(jnp.dot(out_b, out_full, preferred_element_type=jnp.float32))
-        attn_scale = lax.rsqrt(row_total(jnp.sum(attn_raw * attn_raw, axis=1)) / D + EPS)
+        attn_raw = general_narrow(jnp.dot(out_b, out_full, preferred_element_type=jnp.float32))
+        attn_scale = lax.rsqrt(general_row_total(jnp.sum(attn_raw * attn_raw, axis=1)) / D + EPS)
         resid = tokens_in.astype(jnp.float32) + attn_raw * attn_scale[:, None] * attn_gain
-        wide_mid = widen(resid.astype(jnp.bfloat16))
+        wide_mid = general_widen(resid.astype(jnp.bfloat16))
         gate = jnp.dot(wide_mid, gate_full, preferred_element_type=jnp.float32)
         up_val = jnp.dot(wide_mid, up_full, preferred_element_type=jnp.float32)
         sigma = jax.nn.sigmoid(gate)
         swish = gate * sigma
         act_b = (swish * up_val).astype(jnp.bfloat16)
-        mlp_raw = narrow(jnp.dot(act_b, down_full, preferred_element_type=jnp.float32))
-        mlp_scale = lax.rsqrt(row_total(jnp.sum(mlp_raw * mlp_raw, axis=1)) / D + EPS)
+        mlp_raw = general_narrow(jnp.dot(act_b, down_full, preferred_element_type=jnp.float32))
+        mlp_scale = lax.rsqrt(general_row_total(jnp.sum(mlp_raw * mlp_raw, axis=1)) / D + EPS)
         result = resid + mlp_raw * mlp_scale[:, None] * mlp_gain
         outputs.append(result.astype(jnp.bfloat16).reshape(per_batch, slice_len, local_width))
         again = (
@@ -205,25 +1409,25 @@
         )
         mlp_gain_grad = mlp_gain_grad + jnp.sum(grad_out * mlp_raw * mlp_scale[:, None], axis=0)
         scaled = grad_out * mlp_gain
-        grad_mlp = norm_grad(
-            scaled, mlp_raw, mlp_scale, row_total(jnp.sum(scaled * mlp_raw, axis=1))
-        )
-        wide_grad_mlp = widen(grad_mlp.astype(jnp.bfloat16))
-        grad_act = contract_last(wide_grad_mlp, down_back)
+        grad_mlp = general_norm_grad(
+            scaled, mlp_raw, mlp_scale, general_row_total(jnp.sum(scaled * mlp_raw, axis=1))
+        )
+        wide_grad_mlp = general_widen(grad_mlp.astype(jnp.bfloat16))
+        grad_act = general_contract_last(wide_grad_mlp, down_back)
         grad_gate = (grad_act * up_val * sigma * (1.0 + gate * (1.0 - sigma))).astype(jnp.bfloat16)
         grad_up = (grad_act * swish).astype(jnp.bfloat16)
-        grad_resid = grad_out + narrow(
-            contract_last(grad_gate, gate_back) + contract_last(grad_up, up_back)
+        grad_resid = grad_out + general_narrow(
+            general_contract_last(grad_gate, gate_back) + general_contract_last(grad_up, up_back)
         )
         attn_gain_grad = attn_gain_grad + jnp.sum(
             grad_resid * attn_raw * attn_scale[:, None], axis=0
         )
         scaled = grad_resid * attn_gain
-        grad_attn = norm_grad(
-            scaled, attn_raw, attn_scale, row_total(jnp.sum(scaled * attn_raw, axis=1))
-        )
-        wide_grad_attn = widen(grad_attn.astype(jnp.bfloat16))
-        grad_heads = contract_last(wide_grad_attn, out_back).astype(jnp.bfloat16)
+        grad_attn = general_norm_grad(
+            scaled, attn_raw, attn_scale, general_row_total(jnp.sum(scaled * attn_raw, axis=1))
+        )
+        wide_grad_attn = general_widen(grad_attn.astype(jnp.bfloat16))
+        grad_heads = general_contract_last(wide_grad_attn, out_back).astype(jnp.bfloat16)
         dout_four = grad_heads.reshape(per_batch, slice_len, heads_here, HEAD_DIM)
         delta = jnp.sum(
             (grad_heads.astype(jnp.float32) * out_heads).reshape(
@@ -277,37 +1481,37 @@
                 grad_values.astype(jnp.bfloat16), "ctx", scatter_dimension=1, tiled=True
             ).astype(jnp.float32),
         )
-        grad_qnorm = turn_back(
+        grad_qnorm = general_turn_back(
             grad_query.reshape(rows, heads_here, HEAD_DIM), cosine, sine
         ).reshape(rows, heads_here * HEAD_DIM)
-        grad_knorm = turn_back(
+        grad_knorm = general_turn_back(
             key_grad_mine.reshape(rows, heads_here, HEAD_DIM), cosine, sine
         ).reshape(rows, heads_here * HEAD_DIM)
         q_gain_grad = q_gain_grad + jnp.sum(grad_qnorm * query_raw * query_scale[:, None], axis=0)
         k_gain_grad = k_gain_grad + jnp.sum(grad_knorm * key_raw * key_scale[:, None], axis=0)
         q_scaled = grad_qnorm * q_gain
         k_scaled = grad_knorm * k_gain
-        q_inner, k_inner = row_total(
+        q_inner, k_inner = general_row_total(
             (jnp.sum(q_scaled * query_raw, axis=1), jnp.sum(k_scaled * key_raw, axis=1))
         )
-        grad_query_raw = norm_grad(q_scaled, query_raw, query_scale, q_inner).astype(jnp.bfloat16)
-        grad_key_raw = norm_grad(k_scaled, key_raw, key_scale, k_inner).astype(jnp.bfloat16)
+        grad_query_raw = general_norm_grad(q_scaled, query_raw, query_scale, q_inner).astype(jnp.bfloat16)
+        grad_key_raw = general_norm_grad(k_scaled, key_raw, key_scale, k_inner).astype(jnp.bfloat16)
         grad_value_raw = value_grad_mine.reshape(rows, heads_here * HEAD_DIM).astype(jnp.bfloat16)
         back_terms = (
-            contract_last(grad_query_raw, query_back)
-            + contract_last(grad_key_raw, key_back)
-            + contract_last(grad_value_raw, value_back)
-        )
-        grad_in = grad_resid + narrow(back_terms)
+            general_contract_last(grad_query_raw, query_back)
+            + general_contract_last(grad_key_raw, key_back)
+            + general_contract_last(grad_value_raw, value_back)
+        )
+        grad_in = grad_resid + general_narrow(back_terms)
         input_grads.append(grad_in.astype(jnp.bfloat16).reshape(per_batch, slice_len, local_width))
         fresh_grads = (
-            contract_first(wide_in, grad_query_raw),
-            contract_first(wide_in, grad_key_raw),
-            contract_first(wide_in, grad_value_raw),
-            contract_first(out_b, wide_grad_attn),
-            contract_first(wide_mid, grad_gate),
-            contract_first(wide_mid, grad_up),
-            contract_first(act_b, wide_grad_mlp),
+            general_contract_first(wide_in, grad_query_raw),
+            general_contract_first(wide_in, grad_key_raw),
+            general_contract_first(wide_in, grad_value_raw),
+            general_contract_first(out_b, wide_grad_attn),
+            general_contract_first(wide_mid, grad_gate),
+            general_contract_first(wide_mid, grad_up),
+            general_contract_first(act_b, wide_grad_mlp),
         )
         weight_grads = tuple((left + right for left, right in zip(weight_grads, fresh_grads)))
     finals = (
@@ -351,42 +1555,193 @@
     )
 
 
+def weight_grad(left, right):
+    value = dot_tn(left[0], right[0]) + dot_tn(left[1], right[1])
+    return value.astype(BF)
+
+
+class Batch:
+    pass
+
+
+def planned(
+    hidden, cotangent, segments, positions, w_query, w_key, w_value, w_out, w_gate, w_up, w_down,
+    q_gain, k_gain, attn_gain, mlp_gain,
+):
+    seqs, count, width = hidden.shape
+    per = seqs // 2
+    rows = per * count
+    ff = w_gate.shape[1]
+    batches = (Batch(), Batch())
+    one, two = batches
+    for b, batch in enumerate(batches):
+        batch.x = hidden[b * per : (b + 1) * per].reshape(rows, width)
+        batch.cot = cotangent[b * per : (b + 1) * per].reshape(rows, width)
+    seg_cols = jnp.broadcast_to(segments.reshape(seqs * count, 1), (seqs * count, 128))
+    pos_cols = jnp.broadcast_to(positions.reshape(seqs * count, 1), (seqs * count, 128))
+    half = HEAD_DIM // 2
+    freqs = THETA ** (-(jnp.arange(half, dtype=F32) * 2.0) / HEAD_DIM)
+    freqs = jnp.concatenate([freqs, freqs]).reshape(1, HEAD_DIM)
+    sign = jnp.concatenate([-jnp.ones(half, F32), jnp.ones(half, F32)]).reshape(1, HEAD_DIM)
+    seg_pad = jnp.concatenate([segments, jnp.zeros((8 - seqs, count), segments.dtype)], axis=0)
+    norms = (q_gain, k_gain)
+
+    s = Slot("slot0", 0)
+    line = Line(s, rows, width, gather=one.x)
+    full = [attach(s, PlaneGather(w, 0, True, 4.0 * i, done="w%d" % i))[0] for i, w in enumerate((w_query, w_key, w_value))]
+    w_out_h = attach(s, PlaneGather(w_out, 1, True, 12.0))[0]
+    seg_h = attach(s, PlaneGather(seg_pad, 0, False, 2.0))[0]
+    cosine, sine = tables(s, pos_cols, freqs, sign)
+    made = project(s, line, rows, width, full, ("w0", "w1", "w2"), norms, cosine, sine, 0)
+    s.run()
+    wq, wk, wv = (h.value for h in full)
+    wo, seg_all, cosine, sine = w_out_h.value, seg_h.value, cosine.target.value, sine.target.value
+    one.q_raw, one.k_raw, one.q, one.kv, one.qk_factor = (h.value for h in made)
+    one.wide = line.out.value
+
+    s = Slot("slot1", 1)
+    line = Line(s, rows, width, gather=two.x)
+    kvs = attach(s, PlaneGather(one.kv, 0, False, done="kv"))[0]
+    w_gate_h = attach(s, PlaneGather(w_gate, 0, True, 9.0, lean=True))[0]
+    s.mark_early("tables")
+    made = project(s, line, rows, width, (wq, wk, wv), None, norms, s.load(cosine), s.load(sine), rows)
+    mask = Mask(s, seg_all, seg_cols, 0, count)
+    felt = attend(s, "kv", kvs, one.q, mask, rows, width)
+    s.run()
+    wg, one.kvs = w_gate_h.value, kvs.value
+    two.q_raw, two.k_raw, two.q, two.kv, two.qk_factor = (h.value for h in made)
+    one.heads, one.heads_b, one.logsum = (h.value for h in felt)
+    two.wide = line.out.value
+
+    s = Slot("slot2", 2)
+    line = Line(s, rows, width, scatter=True)
+    kvs = attach(s, PlaneGather(two.kv, 0, False, done="kv"))[0]
+    w_up_h = attach(s, PlaneGather(w_up, 0, True, 9.0, lean=True))[0]
+    ends = attn_finish(s, line, rows, width, one.x, attn_gain)
+    produce(s, line, [s.load(one.heads_b)], [wo], (width, width), col_block, dot_nn, 0.6)
+    mask = Mask(s, seg_all, seg_cols, per, count)
+    felt = attend(s, "kv", kvs, two.q, mask, rows, width)
+    s.run()
+    wu, two.kvs = w_up_h.value, kvs.value
+    one.attn, one.resid, one.resid_b, one.factor = (h.value for h in ends)
+    two.heads, two.heads_b, two.logsum = (h.value for h in felt)
+
+    s = Slot("slot3", 3)
+    line = Line(s, rows, width, gather=one.resid_b, scatter=True)
+    w_down_h = attach(s, PlaneGather(w_down, 1, True))[0]
+    ends = attn_finish(s, line, rows, width, two.x, attn_gain)
+    produce(s, line, [s.load(two.heads_b)], [wo], (width, width), col_block, dot_nn, 0.6)
+    inner = gate_up(s, line, rows, wg, wu)
+    s.run()
+    wd, one.mid = w_down_h.value, line.out.value
+    two.attn, two.resid, two.resid_b, two.factor = (h.value for h in ends)
+    one.gate, one.up, one.act = (h.value for h in inner)
+
+    s = Slot("slot4", 4)
+    line = Line(s, rows, width, gather=two.resid_b, scatter=True)
+    ends = mlp_finish(s, line, rows, width, one.resid, one.cot, mlp_gain)
+    produce(s, line, [s.load(one.act)], [wd], (ff, 512), col_block, dot_nn, 1.8)
+    inner = gate_up(s, line, rows, wg, wu)
+    s.run()
+    two.mid = line.out.value
+    one.out, one.g_mlp_b, one.g_mlp_gain = (h.value for h in ends)
+    two.gate, two.up, two.act = (h.value for h in inner)
+
+    s = Slot("slot5", 5)
+    line = Line(s, rows, width, gather=one.g_mlp_b, scatter=True)
+    ends = mlp_finish(s, line, rows, width, two.resid, two.cot, mlp_gain)
+    produce(s, line, [s.load(two.act)], [wd], (ff, 512), col_block, dot_nn, 1.8)
+    inner = act_back(s, line, rows, wd, one.gate, one.up)
+    s.run()
+    one.g_mlp = line.out.value
+    two.out, two.g_mlp_b, two.g_mlp_gain = (h.value for h in ends)
+    one.g_gate, one.g_up = (h.value for h in inner)
+
+    s = Slot("slot6", 6)
+    line = Line(s, rows, width, gather=two.g_mlp_b, scatter=True)
+    ends = resid_finish(s, line, rows, width, one.cot, one.attn, one.factor, attn_gain)
+    produce(s, line, [s.load(one.g_gate), s.load(one.g_up)], [wg, wu], (512, ff), row_block, dot_nt, 3.6)
+    inner = act_back(s, line, rows, wd, two.gate, two.up)
+    s.run()
+    two.g_mlp = line.out.value
+    one.g_resid, one.g_attn_b, one.g_attn_gain = (h.value for h in ends)
+    two.g_gate, two.g_up = (h.value for h in inner)
+
+    d_down = weight_grad((one.act, two.act), (one.g_mlp, two.g_mlp))
+    s = Slot("slot7", 7)
+    line = Line(s, rows, width, gather=one.g_attn_b, scatter=True)
+    g_down = attach(s, PlaneScatter(d_down, 1, True))[0]
+    ends = resid_finish(s, line, rows, width, two.cot, two.attn, two.factor, attn_gain)
+    produce(s, line, [s.load(two.g_gate), s.load(two.g_up)], [wg, wu], (512, ff), row_block, dot_nt, 3.6)
+    mask = Mask(s, seg_all, seg_cols, 0, count)
+    back = attend_back(s, line, one.kvs, one.q, one.heads, one.logsum, mask, rows, width, wo)
+    s.run()
+    one.g_attn = line.out.value
+    two.g_resid, two.g_attn_b, two.g_attn_gain = (h.value for h in ends)
+    one.g_q, one.g_kv = (h.value for h in back)
+
+    d_gate = weight_grad((one.mid, two.mid), (one.g_gate, two.g_gate))
+    s = Slot("slot8", 8)
+    line = Line(s, rows, width, gather=two.g_attn_b)
+    g_kv = attach(s, PlaneScatter(one.g_kv, 0, False, done="kv"))[0]
+    g_gate = attach(s, PlaneScatter(d_gate, 0, True, lean=True))[0]
+    raws = project_back(s, "kv", one.g_q, g_kv, (one.q_raw, one.k_raw), one.qk_factor, norms, cosine, sine, 0, rows, width)
+    mask = Mask(s, seg_all, seg_cols, per, count)
+    back = attend_back(s, line, two.kvs, two.q, two.heads, two.logsum, mask, rows, width, wo)
+    s.run()
+    two.g_attn = line.out.value
+    one.g_qr, one.g_kr, one.g_vr, one.g_q_gain, one.g_k_gain = (h.value for h in raws)
+    two.g_q, two.g_kv = (h.value for h in back)
+
+    d_up = weight_grad((one.mid, two.mid), (one.g_up, two.g_up))
+    s = Slot("slot9", 9)
+    line = Line(s, rows, width, scatter=True)
+    g_kv = attach(s, PlaneScatter(two.g_kv, 0, False, done="kv"))[0]
+    g_up = attach(s, PlaneScatter(d_up, 0, True, lean=True))[0]
+    fin_one = last_finish(s, line, rows, width, one.g_resid)[0]
+    produce(s, line, [s.load(g) for g in (one.g_qr, one.g_kr, one.g_vr)], [wq, wk, wv], (512, width), row_block, dot_nt, 1.6)
+    raws = project_back(s, "kv", two.g_q, g_kv, (two.q_raw, two.k_raw), two.qk_factor, norms, cosine, sine, rows, rows, width)
+    s.run()
+    two.g_qr, two.g_kr, two.g_vr, two.g_q_gain, two.g_k_gain = (h.value for h in raws)
+
+    wides = (one.wide, two.wide)
+    grads = [
+        weight_grad(wides, (one.g_qr, two.g_qr)),
+        weight_grad(wides, (one.g_kr, two.g_kr)),
+        weight_grad(wides, (one.g_vr, two.g_vr)),
+        weight_grad((one.heads_b, two.heads_b), (one.g_attn, two.g_attn)),
+    ]
+    s = Slot("slot10", 10)
+    line = Line(s, rows, width, scatter=True)
+    planes = [attach(s, PlaneScatter(g, i // 3, True))[0] for i, g in enumerate(grads)]
+    fin_two = last_finish(s, line, rows, width, two.g_resid)[0]
+    produce(s, line, [s.load(g) for g in (two.g_qr, two.g_kr, two.g_vr)], [wq, wk, wv], (512, width), row_block, dot_nt, 1.6)
+    s.run()
+    g_q, g_k, g_v, g_out = (h.value for h in planes)
+    gains = (
+        one.g_q_gain + two.g_q_gain,
+        one.g_k_gain + two.g_k_gain,
+        one.g_attn_gain + two.g_attn_gain,
+        one.g_mlp_gain + two.g_mlp_gain,
+    )
+    gains = lax.psum(tuple(jnp.sum(g, axis=0) for g in gains), ("dp", "ctx"))
+    shape = (per, count, width)
+    return (
+        jnp.concatenate([one.out.reshape(shape), two.out.reshape(shape)], axis=0),
+        jnp.concatenate([fin_one.value.reshape(shape), fin_two.value.reshape(shape)], axis=0),
+        g_q, g_k, g_v, g_out, g_gate.value, g_up.value, g_down.value, *gains,
+    )
+
+
 def solution(mesh):
-    placed = (
-        P("dp", "ctx", "tp"),
-        P("dp", "ctx", "tp"),
-        P("dp", "ctx"),
-        P("dp", "ctx"),
-        P(("dp", "ctx"), "tp"),
-        P(("dp", "ctx"), "tp"),
-        P(("dp", "ctx"), "tp"),
-        P("tp", ("dp", "ctx")),
-        P(("dp", "ctx"), "tp"),
-        P(("dp", "ctx"), "tp"),
-        P("tp", ("dp", "ctx")),
-        P("tp"),
-        P("tp"),
-        P("tp"),
-        P("tp"),
-    )
+    rows, cols = P(("dp", "ctx"), "tp"), P("tp", ("dp", "ctx"))
+    act, gain = P("dp", "ctx", "tp"), P("tp")
+    size = dict(mesh.shape)
+    body = planned if (size["dp"], size["ctx"], size["tp"]) == (2, 4, 4) else general
     return jax.shard_map(
-        local,
+        body,
         mesh=mesh,
-        in_specs=placed,
-        out_specs=(
-            P("dp", "ctx", "tp"),
-            P("dp", "ctx", "tp"),
-            P(("dp", "ctx"), "tp"),
-            P(("dp", "ctx"), "tp"),
-            P(("dp", "ctx"), "tp"),
-            P("tp", ("dp", "ctx")),
-            P(("dp", "ctx"), "tp"),
-            P(("dp", "ctx"), "tp"),
-            P("tp", ("dp", "ctx")),
-            P("tp"),
-            P("tp"),
-            P("tp"),
-            P("tp"),
-        ),
+        in_specs=(act, act, P("dp", "ctx"), P("dp", "ctx"), rows, rows, rows, cols, rows, rows, cols, gain, gain, gain, gain),
+        out_specs=(act, act, rows, rows, rows, cols, rows, rows, cols, gain, gain, gain, gain),
         check_vma=False,
     )

time: 1750 us -> 856 us (0.49)
  waiting for transfers between devices: 1150 us -> 0 us
  Pallas kernels: 0 us -> 722 us
  matrix products: 313 us -> 92.2 us
  local copies, waits for them, and re-layouts: 98.2 us -> 17.3 us
  other arithmetic: 77.6 us -> 3.99 us
  blocking collectives: 81.1 us -> 12.6 us
    pallas_call x0 -> x11, Pallas kernels: none -> 722 us  [run(): pl.pallas_call(self.kernel, out_shape=tuple((o for o, _ in self.outputs))...]
    reduce_scatter x19 -> x0, waiting for transfers between devices: 605 us -> none  [the longest x8 295 us: narrow(): lax.psum_scatter(value.astype(jnp.bfloat16), 'tp', scatter_dimension=1, t...]
    all_gather x19 -> x0, waiting for transfers between devices: 542 us -> none  [the longest x8 298 us: widen(): return lax.all_gather(value, 'tp', axis=1, tiled=True)]
    dot_general x54 -> x14, matrix products: 313 us -> 92.2 us  [dot_tn(): lax.dot_general(left, right, (((0,), (0,)), ((), ())), preferred_element_...]
    psum x7 -> x1, blocking collectives: 70.8 us -> 12.6 us  [planned(): gains = lax.psum(tuple((jnp.sum(g, axis=0) for g in gains)), ('dp', 'ctx'))]
    unnamed x267 -> x87, local copies, waits for them, and re-layouts: 44 us -> 10.7 us
    convert_element_type x11 -> x0, other arithmetic: 26.1 us -> none  [the longest x4 10.1 us: local(): finals = (lax.psum_scatter(weight_grads[0].astype(jnp.bfloat16), ('dp', '...]
    reduce_sum x12 -> x2, other arithmetic: 22.1 us -> 0.76 us  [planned(): gains = lax.psum(tuple((jnp.sum(g, axis=0) for g in gains)), ('dp', 'ctx'))]
  transfers between devices with their start and end apart: 38 -> 0, of which waited for: 30 -> 0; matrix products, arithmetic and copies ran while one was open for 26% -> 0% of each run, Pallas kernels for 0% -> 0%
where the time goes in v2:
time: 856 us; the launch traced here: 849 us
  Pallas kernels  722 us (84%)
  matrix products  92.2 us (11%)
  local copies, waits for them, and re-layouts  17.3 us (2%)
  blocking collectives  12.6 us (1%)
    pallas_call x11, Pallas kernels, run(): pl.pallas_call(self.kernel, out_shape=tuple((o for o, _ in self.outputs))...  722 us
    dot_general x14, matrix products, dot_tn(): lax.dot_general(left, right, (((0,), (0,)), ((), ())), preferred_element_...  92.2 us

profile of v2, /device:TPU:0, one launch (start us, length us, event | category | flops | bytes accessed | tf_op | source)
XLA Modules:
  0.0 849.3 jit_solution(12629149337204330217)
XLA Ops:
  0.7 0.6 maximum_bitcast_fusion.refs_7_
  1.3 0.7 copy.28
  1.9 0.7 copy.29
  2.6 1.3 concatenate.12.refs_5_
  3.9 1.0 broadcast_in_dim.18.refs_11_.refs_7_.refs_12_
  4.9 1.0 broadcast_in_dim.16.refs_6_
  5.9 2.2 fusion.1
  8.1 0.0 copy-done.19
  8.1 1.0 fusion
  9.2 83.3 %slot0.1 = (bf16[512,2048]{1,0:T(8,128)(2,1)}, bf16[2048,512]{1,0:T(8,128)(2,1)}, bf16[2048,512]{1,0:T(8,128)(2,1)}, bf16[2048,512]{1,0:T(8,128)(2,1)}, bf16[512...) custom-call(bf16[512,512]{1,0:T(8,128)(2,1)} %bitcast.52, ...), custom_call_target="tpu_custom_call" | custom-call | tf_op jit(solution)/shard_map/slot0/pallas_call | solution.py:408
  92.5 74.4 %slot1.1 = (bf16[512,2048]{1,0:T(8,128)(2,1)}, bf16[2048,1024]{1,0:T(8,128)(2,1)}, bf16[2048,2048]{1,0:T(8,128)(2,1)}, f32[512,512]{1,0:T(8,128)}, f32[512,512]{...) custom-call(bf16[512,512]{1,0:T(8,128)(2,1)} %bitcast.50, ...), custom_call_target="tpu_custom_call" | custom-call | tf_op jit(solution)/shard_map/slot1/pallas_call | solution.py:408
  167.0 77.2 %slot2.1 = (bf16[2048,1024]{1,0:T(8,128)(2,1)}, bf16[2048,2048]{1,0:T(8,128)(2,1)}, f32[512,512]{1,0:T(8,128)}, f32[512,512]{1,0:T(8,128)}, bf16[512,512]{1,0:T(...) custom-call(bf16[512,1024]{1,0:T(8,128)(2,1)} %get-tuple-element.110.refs_, ...), custom_call_target="tpu_custom_call" | custom-call | tf_op jit(solution)/shard_map/slot2/pallas_call | solution.py:408
  244.1 58.0 %slot3.1 = (bf16[512,2048]{1,0:T(8,128)(2,1)}, bf16[2048,2048]{1,0:T(8,128)(2,1)}, f32[512,512]{1,0:T(8,128)}, f32[512,512]{1,0:T(8,128)}, bf16[512,512]{1,0:T(8...) custom-call(bf16[512,512]{1,0:T(8,128)(2,1)} %get-tuple-element.114., ...), custom_call_target="tpu_custom_call" | custom-call | tf_op jit(solution)/shard_map/slot3/pallas_call | solution.py:408
  302.2 57.0 %slot4.1 = (bf16[512,2048]{1,0:T(8,128)(2,1)}, bf16[512,512]{1,0:T(8,128)(2,1)}, bf16[512,512]{1,0:T(8,128)(2,1)}, f32[8,512]{1,0:T(8,128)}, bf16[512,2048]{1,0:...) custom-call(bf16[512,512]{1,0:T(8,128)(2,1)} %get-tuple-element.118.refs_0_, ...), custom_call_target="tpu_custom_call" | custom-call | tf_op jit(solution)/shard_map/slot4/pallas_call | solution.py:408
  359.2 56.0 %slot5.1 = (bf16[512,2048]{1,0:T(8,128)(2,1)}, bf16[512,512]{1,0:T(8,128)(2,1)}, bf16[512,512]{1,0:T(8,128)(2,1)}, f32[8,512]{1,0:T(8,128)}, bf16[512,2048]{1,0:T(8,128)(2,1)}, /*index=5*/bf16[512,2048]{1,0:T(8,128)(2,1)}) custom-call(bf16[512,512]{1,0:T(8,128)(2,1)} %get-tuple-element.123.refs_0_, f32[512,512]{1,0:T(8,128)} %get-tuple-element.124.refs_1_, ...), custom_call_target="tpu_custom_call" | custom-call | tf_op jit(solution)/shard_map/slot5/pallas_call | solution.py:408
  415.1 55.9 %slot6.1 = (bf16[512,2048]{1,0:T(8,128)(2,1)}, f32[512,512]{1,0:T(8,128)}, bf16[512,512]{1,0:T(8,128)(2,1)}, f32[8,512]{1,0:T(8,128)}, bf16[512,2048]{1,0:T(8,128)(2,1)}, /*index=5*/bf16[512,2048]{1,0:T(8,128)(2,1)}) custom-call(bf16[512,512]{1,0:T(8,128)(2,1)} %get-tuple-element.129.refs_0_, bf16[512,512]{1,0:T(8,128)(2,1)} %bitcast.49, ...), custom_call_target="tpu_custom_call" | custom-call | tf_op jit(solution)/shard_map/slot6/pallas_call | solution.py:408
  471.0 12.7 %fusion.2 = f32[2048,2048]{1,0:T(8,128)} fusion(bf16[512,2048]{1,0:T(8,128)(2,1)} %get-tuple-element.120.refs_4_, bf16[512,2048]{1,0:T(8,128)(2,1)} %get-tuple-element.137), kind=kOutput, calls=%fused_computation.17 | convolution fusion | flops 4294967296 | bytes 20971520 | tf_op jit(solution)/shard_map/dot_general | solution.py:1160
  483.7 0.0 copy-done.38
  483.7 10.4 %add_convert_fusion.2.refs_1_ = bf16[2048,2048]{1,0:T(8,128)(2,1)} fusion(f32[2048,2048]{1,0:T(8,128)} %fusion.2, bf16[512,2048]{1,0:T(8,128)(2,1)S(1)} %copy-done.9, bf16[512,2048]{1,0:T(8,128)(2,1)S(1)} %copy-done.38), kind=kOutput, calls=%fused_computation.2 | convolution fusion | flops 4303355904 | bytes 29360128 | tf_op jit(solution)/shard_map/dot_general | solution.py:1160
  494.1 67.1 %slot7.1 = (bf16[512,2048]{1,0:T(8,128)(2,1)}, f32[2048,256]{1,0:T(8,128)}, f32[512,512]{1,0:T(8,128)}, bf16[512,512]{1,0:T(8,128)(2,1)}, f32[8,512]{1,0:T(8,128...) custom-call(bf16[512,512]{1,0:T(8,128)(2,1)} %get-tuple-element.136.refs_0_, ...), custom_call_target="tpu_custom_call" | custom-call | tf_op jit(solution)/shard_map/slot7/pallas_call | solution.py:408
  561.2 0.7 add_reduce_fusion
  561.9 0.0 copy-done.18
  562.0 5.0 fusion.8
  567.0 8.1 fusion.3
  575.1 10.5 %add_convert_fusion.1.refs_2_ = bf16[2048,2048]{1,0:T(8,128)(2,1)} fusion(f32[2048,2048]{1,0:T(8,128)} %fusion.3, bf16[512,2048]{1,0:T(8,128)(2,1)S(1)} %copy-done.36, bf16[512,2048]{1,0:T(8,128)(2,1)S(1)} %copy-done.8), kind=kOutput, calls=%fused_computation.1 | convolution fusion | flops 4303355904 | bytes 29360128 | tf_op jit(solution)/shard_map/dot_general | solution.py:1160
  585.6 68.0 %slot8.1 = (bf16[512,2048]{1,0:T(8,128)(2,1)}, f32[512,1024]{1,0:T(8,128)}, f32[256,2048]{1,0:T(8,128)}, bf16[512,512]{1,0:T(8,128)(2,1)}, bf16[512,512]{1,0:T(8...) custom-call(bf16[512,512]{1,0:T(8,128)(2,1)} %get-tuple-element.146., ...), custom_call_target="tpu_custom_call" | custom-call | tf_op jit(solution)/shard_map/slot8/pallas_call | solution.py:408
  653.6 5.6 add_convert_fusion.3.refs_3_
  659.2 3.3 fusion.5
  662.5 3.4 fusion.6
  665.9 3.3 fusion.7
  669.2 8.1 fusion.4
  677.4 10.6 %add_convert_fusion.refs_1_ = bf16[2048,2048]{1,0:T(8,128)(2,1)} fusion(f32[2048,2048]{1,0:T(8,128)} %fusion.4, bf16[512,2048]{1,0:T(8,128)(2,1)S(1)} %copy-done.37, bf16[512,2048]{1,0:T(8,128)(2,1)S(1)} %copy-done.6), kind=kOutput, calls=%fused_computation | convolution fusion | flops 4303355904 | bytes 29360128 | tf_op jit(solution)/shard_map/dot_general | solution.py:1160
  688.0 64.9 %slot9.1 = (f32[512,1024]{1,0:T(8,128)}, f32[256,2048]{1,0:T(8,128)}, bf16[512,512]{1,0:T(8,128)(2,1)}, bf16[512,512]{1,0:T(8,128)(2,1)}, bf16[512,512]{1,0:T(8,...) custom-call(bf16[2048,1024]{1,0:T(8,128)(2,1)} %get-tuple-element.157.refs_0_, ...), custom_call_target="tpu_custom_call" | custom-call | tf_op jit(solution)/shard_map/slot9/pallas_call | solution.py:408
  753.0 5.7 add_convert_fusion.4.refs_2_
  758.8 2.7 add_convert_fusion.5.refs_1_
  761.5 2.7 add_convert_fusion.6.refs_0_
  764.2 60.3 %slot10.1 = (f32[256,512]{1,0:T(8,128)}, f32[256,512]{1,0:T(8,128)}, f32[256,512]{1,0:T(8,128)}, f32[512,256]{1,0:T(8,128)}, bf16[512,512]{1,0:T(8,128)(2,1)}) custom-call(bf16[2048,512]{1,0:T(8,128)(2,1)} %add_convert_fusion.6.refs_0_, bf16[2048,512]{1,0:T(8,128)(2,1)} %add_convert_fusion.5.refs_1_, bf16[2048,512]{1,0:T(8,128)(2,1)} %add_convert_fusion.4.refs_2_, ...), custom_call_target="tpu_custom_call" | custom-call | tf_op jit(solution)/shard_map/slot10/pallas_call | solution.py:408
  824.6 12.6 %all-reduce.1 = (f32[512]{0:T(512)}, f32[512]{0:T(512)}, f32[512]{0:T(512)}, f32[512]{0:T(512)}) all-reduce(f32[512]{0:T(512)S(1)} %get-tuple-element.200, f32[512]{0:T(512)S(1)} %get-tuple-element.199, f32[512]{0:T(512)S(1)} %get-tuple-element.202, f32[512]{0:T(512)S(1)} %get-tuple-element.201), channel_id=1, replica_groups=mesh['dp'=2,'ctx'=4,'tp'=4] {'dp','ctx'}, use_global_device_ids=true, to_apply=%region_1.0 | all-reduce | flops 2048 | bytes 16384 | tf_op jit(solution)/shard_map/psum | solution.py:1727
  837.2 2.6 pad_maximum_fusion
  839.9 0.8 copy.37
  840.7 0.8 copy.38
  841.5 0.8 copy.39
  842.3 0.8 copy.40
  843.1 1.3 copy.41
  844.4 1.0 copy-done.17
  845.4 1.3 copy.42
  846.7 1.0 copy-done.15
  847.8 1.3 copy.43
  (75 shorter events, 0.2 us)
Async XLA Ops:
  0.6 7.5 copy-start.19
  471.0 12.7 %copy-start.9 = (bf16[512,2048]{1,0:T(8,128)(2,1)S(1)}, bf16[512,2048]{1,0:T(8,128)(2,1)}, u32[]{:S(2)}) copy-start(bf16[512,2048]{1,0:T(8,128)(2,1)} %get-tuple-element.125.refs_4_) | copy-start | bytes 6291460
  471.0 12.7 %copy-start.38 = (bf16[512,2048]{1,0:T(8,128)(2,1)S(1)}, bf16[512,2048]{1,0:T(8,128)(2,1)}, u32[]{:S(2)}) copy-start(bf16[512,2048]{1,0:T(8,128)(2,1)} %get-tuple-element.138) | copy-start | bytes 6291460
  494.1 67.1 %copy-start.29 = (f32[8,512]{1,0:T(8,128)S(1)}, f32[8,512]{1,0:T(8,128)}, u32[]{:S(2)}) copy-start(f32[8,512]{1,0:T(8,128)} %get-tuple-element.189) | copy-start | bytes 49156
  494.1 67.1 %copy-start.30 = (f32[8,512]{1,0:T(8,128)S(1)}, f32[8,512]{1,0:T(8,128)}, u32[]{:S(2)}) copy-start(f32[8,512]{1,0:T(8,128)} %get-tuple-element.190) | copy-start | bytes 49156
  494.1 67.1 %copy-start.33 = (f32[8,512]{1,0:T(8,128)S(1)}, f32[8,512]{1,0:T(8,128)}, u32[]{:S(2)}) copy-start(f32[8,512]{1,0:T(8,128)} %get-tuple-element.187) | copy-start | bytes 49156
  494.1 67.9 %copy-start.18 = (bf16[512,512]{1,0:T(8,128)(2,1)S(1)}, bf16[512,512]{1,0:T(8,128)(2,1)}, u32[]{:S(2)}) copy-start(bf16[512,512]{1,0:T(8,128)(2,1)} %get-tuple-element.111.refs_4_) | copy-start | bytes 1572868
  561.9 5.0 copy-start.7
  562.0 5.0 copy-start.34
  567.0 8.2 copy-start.8
  567.0 8.2 copy-start.36
  585.6 68.0 %copy-start.4 = (bf16[512,512]{1,0:T(8,128)(2,1)S(1)}, bf16[512,512]{1,0:T(8,128)(2,1)}, u32[]{:S(2)}) copy-start(bf16[512,512]{1,0:T(8,128)(2,1)} %get-tuple-element.115.refs_4_) | copy-start | bytes 1572868
  653.6 5.6 copy-start.3
  653.6 5.6 copy-start.10
  659.2 3.3 copy-start.11
  662.5 3.4 copy-start.12
  665.9 3.3 copy-start.5
  665.9 3.3 copy-start.35
  669.2 8.2 copy-start.6
  669.2 8.2 copy-start.37
  753.0 5.8 copy-start
  753.0 5.8 copy-start.2
  753.0 5.8 copy-start.14
  758.8 2.7 copy-start.1
  758.8 2.7 copy-start.13
  764.2 60.3 %copy-start.27 = (f32[8,512]{1,0:T(8,128)S(1)}, f32[8,512]{1,0:T(8,128)}, u32[]{:S(2)}) copy-start(f32[8,512]{1,0:T(8,128)} %get-tuple-element.183) | copy-start | bytes 49156
  764.2 60.4 %copy-start.28 = (f32[8,512]{1,0:T(8,128)S(1)}, f32[8,512]{1,0:T(8,128)}, u32[]{:S(2)}) copy-start(f32[8,512]{1,0:T(8,128)} %get-tuple-element.185) | copy-start | bytes 49156
  764.2 60.4 %copy-start.31 = (f32[8,512]{1,0:T(8,128)S(1)}, f32[8,512]{1,0:T(8,128)}, u32[]{:S(2)}) copy-start(f32[8,512]{1,0:T(8,128)} %get-tuple-element.184) | copy-start | bytes 49156
  764.2 60.4 %copy-start.32 = (f32[8,512]{1,0:T(8,128)S(1)}, f32[8,512]{1,0:T(8,128)}, u32[]{:S(2)}) copy-start(f32[8,512]{1,0:T(8,128)} %get-tuple-element.186) | copy-start | bytes 49156
  764.2 73.0 %copy-start.24 = (bf16[512,512]{1,0:T(8,128)(2,1)S(1)}, bf16[512,512]{1,0:T(8,128)(2,1)}, u32[]{:S(2)}) copy-start(bf16[512,512]{1,0:T(8,128)(2,1)} %get-tuple-element.122) | copy-start | bytes 1572868
  764.2 73.0 %copy-start.25 = (bf16[512,512]{1,0:T(8,128)(2,1)S(1)}, bf16[512,512]{1,0:T(8,128)(2,1)}, u32[]{:S(2)}) copy-start(bf16[512,512]{1,0:T(8,128)(2,1)} %get-tuple-element.128) | copy-start | bytes 1572868
  764.2 73.0 %copy-start.26 = (bf16[512,512]{1,0:T(8,128)(2,1)S(1)}, bf16[512,512]{1,0:T(8,128)(2,1)}, u32[]{:S(2)}) copy-start(bf16[512,512]{1,0:T(8,128)(2,1)} %get-tuple-element.166) | copy-start | bytes 1572868
  837.2 2.7 copy-start.23
  837.2 3.5 copy-start.22
  839.9 1.6 copy-start.21
  839.9 2.4 copy-start.20
  839.9 3.2 copy-start.16
  843.1 2.3 copy-start.17
  845.4 2.3 copy-start.15

commit v3 on v2

--- a/solution.py
+++ b/solution.py
@@ -28,237 +28,335 @@
         self.slot = self.dp * 4 + self.ctx
 
 
-class Task:
-    inputs = ()
-    outputs = ()
-    scratch = ()
-    sems = 0
-    axes = ()
-    after = None
-    done = None
-
-    def emit(self, place, ins, outs, scr, sem):
-        raise NotImplementedError
-
-
 def remote(src, dst, sem, send, recv, device):
     return pltpu.make_async_remote_copy(
         src_ref=src, dst_ref=dst, send_sem=sem.at(send), recv_sem=sem.at(recv), device_id=device, device_id_type=MESH
     )
 
 
-class PlaneGather(Task):
-    def __init__(self, array, dim, with_dp, rank=0.0, lean=False, after=None, done=None):
-        self.dim, self.with_dp, self.rank, self.lean = dim, with_dp, rank, lean
-        self.after, self.done = after, done
-        self.inputs = (array,)
+class Step:
+    def __init__(self, job, name, link, time, deps, rank, issue=None, arrive=None):
+        self.job, self.name, self.link, self.time, self.deps, self.rank = job, name, link, time, deps, rank
+        self.issue, self.arrive = issue, arrive
+
+
+class Plane:
+    def __init__(self, slot):
+        self.slot = slot
+        self.jobs = []
+        slot.plane = self
+        slot.axes.add("ctx")
+
+    def gather(self, array, dim, with_dp, pieces=1, start=0.0, after=None, done=None, cols=None):
+        return self.append(Gather(self.slot, array, dim, with_dp, pieces, start, after, done, cols))
+
+    def scatter(self, array, dim, with_dp, pieces=1, start=0.0, after=None, done=None, out=None):
+        return self.append(Scatter(self.slot, array, dim, with_dp, pieces, start, after, done, out))
+
+    def append(self, job):
+        job.number = len(self.jobs)
+        self.jobs.append(job)
+        if job.with_dp:
+            self.slot.axes.add("dp")
+        self.slot.add(lambda: job.body(self), True)
+        return job.out
+
+    def plan(self):
+        load = [0.0, 0.0]
+        for job in self.jobs:
+            load[0] += job.unit * job.pieces
+            load[1] += job.unit * job.pieces if job.with_dp else 0.0
+        steps = []
+        for job in self.jobs:
+            for p in range(job.pieces):
+                via = 0 if load[0] < load[1] else 1
+                if job.with_dp:
+                    load[via] += job.unit
+                steps += job.steps(p, via)
+        times, free, actions = {}, [0.0, 0.0], []
+        begun = [0.0, 0.0]
+        pending = list(steps)
+        while pending:
+            best = None
+            for step in pending:
+                if any((step.job, d) not in times for d in step.deps):
+                    continue
+                ready = max([step.job.start] + [times[step.job, d] for d in step.deps])
+                when_free = ready if step.link is None else max(ready, free[step.link])
+                key = (when_free, step.job.number, step.rank)
+                if best is None or key < best[0]:
+                    best = (key, step, ready, when_free)
+            _, step, ready, begin = best
+            pending.remove(step)
+            end = begin + step.time
+            if step.link is not None:
+                issue_at = max(ready, begun[step.link])
+                begun[step.link], free[step.link] = begin, end
+                actions.append((issue_at, 1, len(actions), step.job, step.issue))
+            arrive_at = end + (0.7 if step.link is not None else 0.0)
+            actions.append((arrive_at, 0, len(actions), step.job, step.arrive))
+            times[step.job, step.name] = arrive_at
+        actions.sort(key=lambda a: a[:3])
+        self.actions = actions
+        self.end = max(a[0] for a in actions)
+
+
+class Job:
+    def body(self, plane):
+        slot = self.slot
+        if not plane.planned:
+            plane.plan()
+            plane.planned = True
+        if self.after is not None:
+            yield ("flag", self.after)
+        shift = max(0.0, slot.now - self.start) if self.after is not None else 0.0
+        yield ("at", self.start)
+        self.begin()
+        for time, _, _, job, emit in plane.actions:
+            if job is self:
+                yield ("at", time + shift)
+                emit()
+        yield ("at", slot.now + 1.0)
+        self.finish()
+        if self.done is not None:
+            slot.mark(self.done)
+
+    def send(self, index, origin, target, device):
+        copy = remote(origin, target, self.slot, self.base + 2 * index, self.base + 2 * index + 1, device)
+        copy.start()
+        self.sent.append(copy)
+
+    def got(self, index, target):
+        remote(target, target, self.slot, self.base + 2 * index, self.base + 2 * index + 1, self.cdev).wait_recv()
+
+    def coordinates(self):
+        self.dp, self.ctx = self.slot.place.dp, self.slot.place.ctx
+        self.xdev, self.ydev, self.cdev = {"ctx": self.ctx ^ 2}, {"dp": self.dp ^ 1}, {"ctx": self.ctx ^ 1}
+        self.sent = []
+
+
+class Gather(Job):
+    def __init__(self, slot, array, dim, with_dp, pieces, start, after, done, cols):
+        self.slot, self.dim, self.with_dp, self.pieces = slot, dim, with_dp, pieces
+        self.start, self.after, self.done = start, after, done
+        self.handle = slot.hbm_in(array)
         shape = list(array.shape)
-        self.size = shape[dim]
-        self.rows = shape[0]
-        self.blocks = 8 if with_dp else 4
-        shape[dim] *= self.blocks
-        self.outputs = (jax.ShapeDtypeStruct(tuple(shape), array.dtype),)
-        self.axes = ("ctx", "dp") if with_dp else ("ctx",)
-        self.sems = 1 + 2 * (3 + 2 + 2 + 2 + 2)
-        self.unit = math.prod(array.shape) * 2 * 2 / 88e3
-
-    def emit(self, place, ins, outs, scr, sem):
-        src, out = ins[0], outs[0]
-        dp, ctx = place.dp, place.ctx
-        half = self.rows // 2
-
-        def spot(d, c, part=None):
-            block = d * 4 + c if self.with_dp else c
-            where = pl.ds(pl.multiple_of(block * self.size, self.size), self.size)
-            if self.dim == 1:
-                if part is None:
-                    return out.at[:, where]
-                return out.at[pl.ds(part * half, half), where]
-            if part is None:
-                return out.at[where]
-            return out.at[pl.ds(pl.multiple_of(block * self.size + part * half, half), half)]
-
-        xdev, ydev, cdev = {"ctx": ctx ^ 2}, {"dp": dp ^ 1}, {"ctx": ctx ^ 1}
-        mine = spot(dp, ctx)
-        own = pltpu.make_async_copy(src, mine, sem.at(0))
-        own.start()
-        sends = []
-
-        def send(index, origin, target, device):
-            copy = remote(origin, target, sem, 1 + 2 * index, 2 + 2 * index, device)
-            copy.start()
-            sends.append(copy)
-
-        def got(index, target):
-            remote(target, target, sem, 1 + 2 * index, 2 + 2 * index, cdev).wait_recv()
-
-        send(0, src, mine, xdev)
+        self.cols = pl.ds(0, shape[1]) if cols is None else pl.ds(*cols)
+        if cols is not None:
+            shape[1] = cols[1]
+        self.size, self.rows = shape[dim], shape[0]
+        self.unit = math.prod(shape) * 2 / 43e3 / pieces
+        shape[dim] *= 8 if with_dp else 4
+        self.out = slot.hbm_out(tuple(shape), array.dtype)
+        self.own = slot.sems(1)
+        self.base = slot.sems(2 * pieces * 7)
+
+    def spot(self, d, c, p):
+        out = self.out.ref
+        block = d * 4 + c if self.with_dp else c
+        step = self.rows // self.pieces
+        if self.dim == 1:
+            return out.at[pl.ds(p * step, step), pl.ds(pl.multiple_of(block * self.size, self.size), self.size)]
+        return out.at[pl.ds(pl.multiple_of(block * self.size + p * step, step), step)]
+
+    def begin(self):
+        self.coordinates()
+        self.source = src = self.handle.ref.at[:, self.cols]
+        step = self.rows // self.pieces
+        for p in range(self.pieces):
+            part = pl.ds(p * step, step)
+            self.send(7 * p, src.at[part], self.spot(self.dp, self.ctx, p), self.cdev)
+        if self.dim == 1:
+            mine = self.out.ref.at[:, pl.ds(pl.multiple_of((self.dp * 4 + self.ctx) * self.size, self.size), self.size)]
+        else:
+            block = self.dp * 4 + self.ctx if self.with_dp else self.ctx
+            mine = self.out.ref.at[pl.ds(pl.multiple_of(block * self.size, self.size), self.size)]
+        self.kept = pltpu.make_async_copy(src, mine, self.slot.sem(self.own))
+        self.kept.start()
+
+    def steps(self, p, via):
+        def direct(k, device):
+            def issue():
+                step = self.rows // self.pieces
+                part = pl.ds(p * step, step)
+                self.send(7 * p + 1 + k, self.source.at[part], self.spot(self.dp, self.ctx, p), device())
+
+            return issue
+
+        def forward(k, place):
+            def arrive():
+                here = self.spot(*place(), p)
+                self.got(7 * p + 1 + k, here)
+                self.send(7 * p + 4 + k, here, here, self.cdev)
+
+            return arrive
+
+        from_x = lambda: (self.dp, self.ctx ^ 2)
+        from_y = lambda: (self.dp ^ 1, self.ctx)
+        corner = lambda: (self.dp ^ 1, self.ctx ^ 2)
+        xdev, ydev = (lambda: self.xdev), (lambda: self.ydev)
+        out = [Step(self, (p, 0), 0, self.unit, [], 2 * p, direct(0, xdev), forward(0, from_x))]
         if self.with_dp:
-            send(1, src, mine, ydev)
-        send(2, src, mine, cdev)
-        yield self.rank + self.unit * 1.0
-        from_x = spot(dp, ctx ^ 2)
-        got(0, from_x)
-        if self.with_dp and self.lean:
-            send(3, from_x, from_x, ydev)
-        elif self.with_dp:
-            send(3, spot(dp, ctx ^ 2, 0), spot(dp, ctx ^ 2, 0), ydev)
-        send(5, from_x, from_x, cdev)
-        if self.with_dp:
-            from_y = spot(dp ^ 1, ctx)
-            got(1, from_y)
-            parts = (None,) if self.lean else (0, 1)
-            if not self.lean:
-                send(4, spot(dp ^ 1, ctx, 1), spot(dp ^ 1, ctx, 1), xdev)
-            send(6, from_y, from_y, cdev)
-            yield self.rank + self.unit * (2.0 if self.lean else 1.5)
-            for k, part in enumerate(parts):
-                diagonal = spot(dp ^ 1, ctx ^ 2, part)
-                got(3 + k, diagonal)
-                send(7 + k, diagonal, diagonal, cdev)
-        yield self.rank + self.unit * (2.1 if self.lean else 1.6)
-        got(2, spot(dp, ctx ^ 1))
-        got(5, spot(dp, ctx ^ 3))
-        if self.with_dp:
-            got(6, spot(dp ^ 1, ctx ^ 1))
-            for k, part in enumerate(parts):
-                got(7 + k, spot(dp ^ 1, ctx ^ 3, part))
-        for copy in sends:
+            out.append(Step(self, (p, 1), 1, self.unit, [], 2 * p, direct(1, ydev), forward(1, from_y)))
+
+            def hop():
+                here = self.spot(*(from_y() if via == 0 else from_x()), p)
+                self.send(7 * p + 3, here, here, self.xdev if via == 0 else self.ydev)
+
+            out.append(Step(self, (p, 2), via, self.unit, [(p, 1 - via)], 2 * p + 1, hop, forward(2, corner)))
+        return out
+
+    def finish(self):
+        for p in range(self.pieces):
+            self.got(7 * p, self.spot(self.dp, self.ctx ^ 1, p))
+            self.got(7 * p + 4, self.spot(self.dp, self.ctx ^ 3, p))
+            if self.with_dp:
+                self.got(7 * p + 5, self.spot(self.dp ^ 1, self.ctx ^ 1, p))
+                self.got(7 * p + 6, self.spot(self.dp ^ 1, self.ctx ^ 3, p))
+        for copy in self.sent:
             copy.wait_send()
-        own.wait()
-
-
-class PlaneScatter(Task):
-    def __init__(self, array, dim, with_dp, rank=0.0, lean=False, after=None, done=None):
-        self.dim, self.with_dp, self.rank, self.lean = dim, with_dp, rank, lean
-        self.after, self.done = after, done
-        self.inputs = (array,)
+        self.kept.wait()
+
+
+class Scatter(Job):
+    def __init__(self, slot, array, dim, with_dp, pieces, start, after, done, out):
+        self.slot, self.dim, self.with_dp, self.pieces = slot, dim, with_dp, pieces
+        self.start, self.after, self.done = start, after, done
+        self.source = slot.hbm_in(array)
         shape = list(array.shape)
-        self.blocks = 8 if with_dp else 4
-        shape[dim] //= self.blocks
+        self.chips = chips = 4 if with_dp else 2
+        shape[dim] //= 2 * chips
         self.size = shape[dim]
         self.rows, self.width = shape
-        self.outputs = (jax.ShapeDtypeStruct(tuple(shape), F32),)
-        self.axes = ("ctx", "dp") if with_dp else ("ctx",)
-        chips = self.blocks // 2
-        self.chips = chips
-        block = (self.rows, self.width)
-        self.scratch = (
-            pltpu.VMEM((chips,) + block, BF),
-            pltpu.VMEM((chips,) + block, BF),
-            pltpu.VMEM((2,) + block, BF),
-            pltpu.VMEM((self.rows, self.width), BF),
-            pltpu.VMEM(block, F32),
-        )
-        self.sems = 2 * chips + chips + 1 + 2 * 6
-        self.unit = self.rows * self.width * 2 * 2 / 88e3
-
-    def emit(self, place, ins, outs, scr, sem):
-        src, out = ins[0], outs[0]
-        mine, came, chip_in, diag_in, total = scr
-        dp, ctx = place.dp, place.ctx
-        core = ctx & 1
-        chips = self.chips
-        half = self.rows // 2
-        tile = min(32, half)
-        xdev, ydev, cdev = {"ctx": ctx ^ 2}, {"dp": dp ^ 1}, {"ctx": ctx ^ 1}
-
-        def place_of(q):
-            x = (ctx >> 1) ^ (q & 1)
-            d = dp ^ (q >> 1)
-            return d, x
-
-        def spot(q, c):
-            d, x = place_of(q)
-            block = d * 4 + x * 2 + c if self.with_dp else x * 2 + c
-            where = pl.ds(pl.multiple_of(block * self.size, self.size), self.size)
-            return src.at[:, where] if self.dim == 1 else src.at[where]
-
-        order = (3, 1, 2, 0) if self.with_dp else (1, 0)
-        sends = []
-        loads = {}
-        for q in order:
-            copy = remote(spot(q, core ^ 1), came.at[q], sem, 2 * q, 2 * q + 1, cdev)
-            copy.start()
-            sends.append(copy)
-            load = pltpu.make_async_copy(spot(q, core), mine.at[q], sem.at(2 * chips + q))
-            load.start()
-            loads[q] = (load, copy)
-        base = 3 * chips + 1
-
-        def hop(index, origin, target, device):
-            copy = remote(origin, target, sem, base + 2 * index, base + 2 * index + 1, device)
-            copy.start()
-            sends.append(copy)
-            return copy
-
-        def got(index, target):
-            remote(target, target, sem, base + 2 * index, base + 2 * index + 1, cdev).wait_recv()
-
-        def add(into, other, first, count):
-            @pl.loop(0, count // tile)
-            def _(i):
-                part = pl.ds(pl.multiple_of(first + i * tile, tile), tile)
-                into[part] = (into[part].astype(F32) + other[part].astype(F32)).astype(BF)
-
-        top, low = pl.ds(0, half), pl.ds(half, half)
-        yield self.rank + 4.0
-        for q in order:
-            load, copy = loads[q]
-            load.wait()
-            copy.wait_recv()
-            add(mine.at[q], came.at[q], 0, self.rows)
-            if q == 3 and self.lean:
-                hop(1, mine.at[3], diag_in, ydev)
-            elif q == 3:
-                hop(0, mine.at[3, top], diag_in.at[top], xdev)
-                hop(1, mine.at[3, low], diag_in.at[low], ydev)
-            if q == 1 and self.with_dp and not self.lean:
-                hop(2, mine.at[1, top], chip_in.at[0, top], xdev)
-            if q == 1 and not self.with_dp:
-                hop(2, mine.at[1], chip_in.at[0], xdev)
-            if q == 2 and self.lean:
-                hop(3, mine.at[2], chip_in.at[1], ydev)
-            elif q == 2:
-                hop(3, mine.at[2, low], chip_in.at[1, low], ydev)
-        if self.lean:
-            yield self.rank + 4.0 + self.unit * 1.2
-            got(1, diag_in)
-            add(mine.at[1], diag_in, 0, self.rows)
-            hop(5, mine.at[1], chip_in.at[0], xdev)
-        elif self.with_dp:
-            yield self.rank + 4.0 + self.unit * 0.7
-            got(0, diag_in.at[top])
-            add(mine.at[2], diag_in, 0, half)
-            hop(4, mine.at[2, top], chip_in.at[1, top], ydev)
-            got(1, diag_in.at[low])
-            add(mine.at[1], diag_in, half, half)
-            hop(5, mine.at[1, low], chip_in.at[0, low], xdev)
-        yield self.rank + 4.0 + self.unit * (2.2 if self.lean else 1.6)
-        if self.lean:
-            got(5, chip_in.at[0])
-            got(3, chip_in.at[1])
-        elif self.with_dp:
-            got(2, chip_in.at[0, top])
-            got(5, chip_in.at[0, low])
-            got(3, chip_in.at[1, low])
-            got(4, chip_in.at[1, top])
+        self.unit = math.prod(shape) * 2 / 43e3 / pieces
+        if out is None:
+            self.out, self.where = slot.hbm_out(tuple(shape), F32), None
         else:
-            got(2, chip_in.at[0])
-
-        @pl.loop(0, self.rows // tile)
+            self.out, self.where = out
+        block = tuple(shape)
+        self.mine, self.came = slot.vmem((chips,) + block, BF), slot.vmem((chips,) + block, BF)
+        self.chip_in = slot.vmem((chips // 2,) + block, BF)
+        self.diag = slot.vmem(block, BF) if with_dp else None
+        self.total = slot.vmem(block, F32)
+        self.loads = slot.sems(chips * pieces)
+        self.outs = slot.sems(pieces)
+        self.base = slot.sems(2 * pieces * (chips + 3))
+
+    def spot(self, q, c, p):
+        x = (self.ctx >> 1) ^ (q & 1)
+        d = self.dp ^ (q >> 1)
+        block = d * 4 + x * 2 + c if self.with_dp else x * 2 + c
+        step = self.rows // self.pieces
+        if self.dim == 1:
+            return self.source.ref.at[pl.ds(p * step, step), pl.ds(pl.multiple_of(block * self.size, self.size), self.size)]
+        return self.source.ref.at[pl.ds(pl.multiple_of(block * self.size + p * step, step), step)]
+
+    def part(self, p):
+        step = self.rows // self.pieces
+        return pl.ds(p * step, step)
+
+    def load(self, q, p):
+        core = self.ctx & 1
+        return pltpu.make_async_copy(
+            self.spot(q, core, p), self.mine.ref.at[q, self.part(p)], self.slot.sem(self.loads + q * self.pieces + p)
+        )
+
+    def begin(self):
+        self.coordinates()
+        core = self.ctx & 1
+        self.order = (3, 1, 2, 0) if self.with_dp else (1, 0)
+        self.per = self.chips + 3
+        for p in range(self.pieces):
+            for q in self.order:
+                self.send(self.per * p + q, self.spot(q, core ^ 1, p), self.came.ref.at[q, self.part(p)], self.cdev)
+                self.load(q, p).start()
+
+    def add(self, into, other, p):
+        step = self.rows // self.pieces
+        tile = min(32, step)
+
+        @pl.loop(0, step // tile)
         def _(i):
-            part = pl.ds(pl.multiple_of(i * tile, tile), tile)
+            part = pl.ds(pl.multiple_of(p * step + i * tile, tile), tile)
+            into[part] = (into[part].astype(F32) + other[part].astype(F32)).astype(BF)
+
+    def steps(self, p, via):
+        mine, came = self.mine, self.came
+
+        def cores():
+            for q in self.order:
+                self.load(q, p).wait()
+                self.got(self.per * p + q, came.ref.at[q, self.part(p)])
+                self.add(mine.ref.at[q], came.ref.at[q], p)
+
+        def out(k, q, target, device):
+            def issue():
+                self.send(self.per * p + self.chips + k, mine.ref.at[q, self.part(p)], target(), device())
+
+            return issue
+
+        xdev, ydev = (lambda: self.xdev), (lambda: self.ydev)
+        into = lambda j: (lambda: self.chip_in.ref.at[j, self.part(p)])
+        done = {}
+
+        def last(k, j):
+            def arrive():
+                self.got(self.per * p + self.chips + k, self.chip_in.ref.at[j, self.part(p)])
+                done[j] = True
+                if len(done) == self.chips // 2:
+                    done.clear()
+                    self.close(p)
+
+            return arrive
+
+        steps = [Step(self, (p, "c"), None, 2.0 + self.unit * 0.5, [], 3 * p, None, cores)]
+        if not self.with_dp:
+            steps.append(Step(self, (p, 0), 0, self.unit, [(p, "c")], 3 * p + 1, out(0, 1, into(0), xdev), last(0, 0)))
+            return steps
+        corner = lambda: self.diag.ref.at[self.part(p)]
+
+        def fold():
+            self.got(self.per * p + self.chips + 2, corner())
+            self.add(mine.ref.at[2 if via == 0 else 1], self.diag.ref, p)
+
+        steps.append(
+            Step(self, (p, 2), via, self.unit, [(p, "c")], 3 * p, out(2, 3, corner, xdev if via == 0 else ydev), fold)
+        )
+        for k, device in ((0, xdev), (1, ydev)):
+            deps = [(p, "c")] if k == via else [(p, 2)]
+            steps.append(Step(self, (p, k), k, self.unit, deps, 3 * p + 1, out(k, 1 + k, into(k), device), last(k, k)))
+        return steps
+
+    def result(self, p):
+        target = self.out.ref
+        step = self.rows // self.pieces
+        if self.where is None:
+            target = target.at[pl.ds(p * step, step)]
+        else:
+            row, col = self.where
+            target = target.at[pl.ds(row + p * step, step), pl.ds(col, self.width)]
+        return pltpu.make_async_copy(self.total.ref.at[self.part(p)], target, self.slot.sem(self.outs + p))
+
+    def close(self, p):
+        step = self.rows // self.pieces
+        tile = min(32, step)
+        mine, chip_in, total = self.mine.ref, self.chip_in.ref, self.total.ref
+
+        @pl.loop(0, step // tile)
+        def _(i):
+            part = pl.ds(pl.multiple_of(p * step + i * tile, tile), tile)
             value = mine[0, part].astype(F32) + chip_in[0, part].astype(F32)
             if self.with_dp:
                 value = value + chip_in[1, part].astype(F32)
             total[part] = value
 
-        last = pltpu.make_async_copy(total, out, sem.at(3 * chips))
-        last.start()
-        for copy in sends:
+        self.result(p).start()
+
+    def finish(self):
+        for copy in self.sent:
             copy.wait_send()
-        last.wait()
+        for p in range(self.pieces):
+            self.result(p).wait()
 
 
 class Handle:
@@ -280,6 +378,7 @@
         self.tasks = []
         self.axes = set()
         self.early = []
+        self.plane = None
         self.loads, self.stores = [], []
         self.flags = {}
         self.now = 0.0
@@ -348,8 +447,8 @@
     def at(self, index):
         return self.sem_ref.at[index]
 
-    def add(self, body):
-        self.tasks.append(body)
+    def add(self, body, transfers=False):
+        self.tasks.append((body, transfers))
 
     def mark(self, flag):
         self.flags[flag] = True
@@ -380,27 +479,30 @@
         for device in peers:
             pl.semaphore_signal(barrier, inc=1, device_id=device, device_id_type=MESH)
         pl.semaphore_wait(barrier, len(peers))
-        running = [[("at", 0.0), task()] for task in self.tasks]
+        if self.plane is not None:
+            self.plane.planned = False
+        running = [[("at", 0.0), task(), 0 if transfers else 1, i] for i, (task, transfers) in enumerate(self.tasks)]
         while running:
             ready = None
             for entry in running:
                 kind, value = entry[0]
                 if (kind == "at" and value <= self.now) or (kind == "flag" and value in self.flags):
-                    ready = entry
-                    break
+                    key = (entry[2], value if kind == "at" and entry[2] == 0 else 0.0, entry[3])
+                    if ready is None or key < ready[0]:
+                        ready = (key, entry)
             if ready is None:
-                times = [entry[0][1] for entry in running if entry[0][0] == "at"]
-                self.now = min(times)
+                self.now = min(entry[0][1] for entry in running if entry[0][0] == "at")
                 continue
+            entry = ready[1]
             try:
-                got = next(ready[1])
+                got = next(entry[1])
             except StopIteration:
-                running.remove(ready)
+                running.remove(entry)
                 continue
             if got[0] == "did":
                 self.now += got[1]
                 got = ("at", self.now)
-            ready[0] = got
+            entry[0] = got
         for handle in self.stores:
             pltpu.make_async_copy(handle.ref, handle.target.ref, self.sem(handle.sem)).wait()
 
@@ -418,34 +520,6 @@
         )(*[a for a, _ in self.inputs])
         for (_, handle), value in zip(self.outputs, values):
             handle.value = value
-
-
-def attach(slot, task):
-    ins = [slot.hbm_in(a) for a in task.inputs]
-    outs = [slot.hbm_out(o.shape, o.dtype) for o in task.outputs]
-    scr = []
-    for s in task.scratch:
-        handle = Handle()
-        slot.scratch.append((s, handle))
-        scr.append(handle)
-    first = slot.sems(task.sems)
-    slot.axes |= set(task.axes)
-
-    class View:
-        def at(self, index):
-            return slot.sem_ref.at[first + index]
-
-    def body():
-        if task.after is not None:
-            yield ("flag", task.after)
-            task.rank = slot.now
-        for t in task.emit(slot.place, [h.ref for h in ins], [h.ref for h in outs], [h.ref for h in scr], View()):
-            yield ("at", t)
-        if task.done is not None:
-            slot.mark(task.done)
-
-    slot.add(body)
-    return outs
 
 
 def any_of(me, values):
@@ -488,10 +562,11 @@
                 self.out_sem = slot.sems(4)
         if scatter:
             self.mine = slot.vmem((4, rows, width), BF)
-            self.came = slot.vmem((2, self.steps, rows, width), BF)
+            self.skip = self.steps - 3
+            self.came = slot.vmem((2, 3, rows, width), BF)
         self.base = slot.sems(4 * self.steps * pieces)
         self.unit = rows * width * 4 / 88e3
-        slot.add(self.body)
+        slot.add(self.body, True)
 
     def chunk(self, k):
         me = self.slot.place.tp
@@ -517,7 +592,7 @@
                     target = self.wide.ref.at[block, rows]
                     origin = self.source.ref.at[rows] if t == 0 else target
                 else:
-                    target = self.came.ref.at[way, t, rows]
+                    target = self.came.ref.at[way, t - self.skip, rows]
                     origin = self.mine.ref.at[block, rows]
                 index = self.index(way, t, p)
                 to = me + 1 if way == 0 else me - 1
@@ -544,7 +619,7 @@
                     @pl.loop(0, step // tile)
                     def _(i):
                         part = pl.ds(pl.multiple_of(p * step + i * tile, tile), tile)
-                        mine[block, part] = (mine[block, part].astype(F32) + came[way, t, part].astype(F32)).astype(BF)
+                        mine[block, part] = (mine[block, part].astype(F32) + came[way, t - self.skip, part].astype(F32)).astype(BF)
 
     def body(self):
         slot = self.slot
@@ -600,7 +675,7 @@
 
     def total(self, part):
         me = self.slot.place.tp
-        last = self.steps - 1
+        last = 2
         left = jnp.where(me > 0, self.came.ref[0, last, part].astype(F32), 0.0)
         right = jnp.where(me < 3, self.came.ref[1, last, part].astype(F32), 0.0)
         return self.mine.ref[me, part].astype(F32) + left + right
@@ -678,6 +753,7 @@
 def produce(slot, line, lefts, arrays, shape, where, dot, cost):
     order = (3, 0, 2, 1)
     weights = Weights(slot, arrays, shape, order, where)
+    each = len(arrays) // len(lefts)
 
     def body():
         weights.start(0)
@@ -687,12 +763,43 @@
                 weights.start(k + 1)
             blocks = weights.take(k)
             value = None
-            for left, block in zip(lefts, blocks):
-                term = dot(left.ref[...], block[...])
+            for j, block in enumerate(blocks):
+                left = lefts[j // each].ref
+                wide = left.shape[1] // each
+                term = dot(left[:, pl.ds((j % each) * wide, wide)], block[...])
                 value = term if value is None else value + term
             line.mine.ref[c] = value.astype(BF)
             yield ("did", cost)
             slot.mark("part%d" % c)
+
+    slot.add(body)
+
+
+def weight_grad(slot, lefts, rights, out, where, flags, cost):
+    buffer = slot.vmem(out[1], BF)
+    base = slot.sems(1)
+
+    def body():
+        slot.need(*lefts, *rights)
+        tall, wide = out[1]
+        for k, (rows, cols) in enumerate(where):
+            target = buffer.ref
+
+            @pl.loop(0, (tall // 512) * (wide // 512))
+            def _(i):
+                r, c = (i, 0) if wide == 512 else (0, i)
+                row = pl.ds(pl.multiple_of(rows + r * 512, 512), 512)
+                col = pl.ds(pl.multiple_of(cols + c * 512, 512), 512)
+                value = dot_tn(lefts[0].ref[:, row], rights[0].ref[:, col])
+                value = value + dot_tn(lefts[1].ref[:, row], rights[1].ref[:, col])
+                here = (pl.ds(pl.multiple_of(r * 512, 512), 512), pl.ds(pl.multiple_of(c * 512, 512), 512))
+                target[here] = value.astype(BF)
+
+            copy = pltpu.make_async_copy(target, out[0][k].ref, slot.sem(base))
+            copy.start()
+            yield ("did", cost)
+            copy.wait()
+            slot.mark(flags[k])
 
     slot.add(body)
 
@@ -881,16 +988,15 @@
 
 
 def gate_up(slot, line, rows, w_gate, w_up):
-    ff = w_gate.shape[1]
+    parts, wide = len(w_gate), w_gate[0].shape[1]
+    ff = parts * wide
     acc = slot.vmem((2, rows, ff), F32)
     gate, up, act = (slot.store((rows, ff), BF) for _ in range(3))
 
     def multiply(first, left, block, j):
-        @pl.loop(0, ff // 1024)
-        def _(i):
-            cols = pl.ds(pl.multiple_of(i * 1024, 1024), 1024)
-            value = dot_nn(left[...], block[:, cols])
-            acc.ref[j, :, cols] = value if first else acc.ref[j, :, cols] + value
+        cols = pl.ds((j % parts) * wide, wide)
+        value = dot_nn(left[...], block[...])
+        acc.ref[j // parts, :, cols] = value if first else acc.ref[j // parts, :, cols] + value
 
     def last():
         half = rows // 2
@@ -907,7 +1013,7 @@
             yield ("did", 2.0)
         slot.flush(act, gate, up)
 
-    consume(slot, line, (w_gate, w_up), (512, ff), row_block, last, multiply, 2.2, "mlp")
+    consume(slot, line, tuple(w_gate) + tuple(w_up), (512, wide), row_block, last, multiply, 0.6, "mlp")
     return [gate.target, up.target, act.target]
 
 
@@ -1112,9 +1218,9 @@
 def attend_back(slot, line, kv, query, heads, logsum, mask, rows, width, w_out):
     kv, query, heads, logsum = slot.load(kv), slot.load(query), slot.load(heads), slot.load(logsum)
     count = mask.count
-    acc = slot.vmem((rows, width), F32)
     grad = slot.vmem((rows, width), BF)
     g_query, g_kv = slot.store((rows, width), F32), slot.store((4 * rows, 2 * width), BF)
+    acc = g_query
     scale = 1.0 / math.sqrt(HEAD_DIM)
 
     def multiply(first, left, block, j):
@@ -1217,6 +1323,59 @@
 
     slot.add(body)
     return [h.target for h in outs + gain_grads]
+
+
+def gain_sums(slot, arrays):
+    loads = [slot.load(a) for a in arrays]
+    width = arrays[0].shape[1]
+    mine = [slot.vmem((8, width), F32) for _ in range(3)]
+    came = [slot.vmem((8, width), F32) for _ in range(3)]
+    out = slot.store((8, width), F32)
+    base = slot.sems(6)
+    slot.axes |= {"ctx", "dp"}
+
+    def body():
+        place = slot.place
+        yield ("at", 2.0)
+        slot.need(*loads)
+        rows = []
+        for k in range(0, len(loads), 2):
+            rows.append(jnp.sum(loads[k].ref[...] + loads[k + 1].ref[...], axis=0, keepdims=True))
+        value = jnp.concatenate(rows + [jnp.zeros((8 - len(rows), width), F32)], axis=0)
+        for k, device in enumerate(({"ctx": place.ctx ^ 1}, {"ctx": place.ctx ^ 2}, {"dp": place.dp ^ 1})):
+            mine[k].ref[...] = value
+            copy = remote(mine[k].ref, came[k].ref, slot, base + 2 * k, base + 2 * k + 1, device)
+            copy.start()
+            yield ("at", 9.0 + 4.0 * k)
+            copy.wait()
+            value = mine[k].ref[...] + came[k].ref[...]
+        out.ref[...] = value
+        slot.flush(out)
+
+    slot.add(body, True)
+    return out.target
+
+
+def tall_grad(slot, plane, lefts, rights, out, starts, prefix):
+    tall, wide = lefts[0].shape[1], rights[0].shape[1]
+    lefts, rights = [slot.load(a) for a in lefts], [slot.load(a) for a in rights]
+    count = wide // 512
+    flags = [prefix + str(k) for k in range(count)]
+    blocks = [slot.hbm_out((tall, 512), BF) for _ in range(count)]
+    weight_grad(slot, lefts, rights, (blocks, (tall, 512)), [(0, 512 * k) for k in range(count)], flags, 4.5)
+    for k in range(count):
+        plane.scatter(blocks[k], 0, True, 1, starts[k], flags[k], None, (out, (0, 512 * k)))
+
+
+def wide_grad(slot, plane, lefts, rights, out, starts, prefix):
+    tall, wide = lefts[0].shape[1], rights[0].shape[1]
+    lefts, rights = [slot.load(a) for a in lefts], [slot.load(a) for a in rights]
+    count = tall // 512
+    flags = [prefix + str(k) for k in range(count)]
+    blocks = [slot.hbm_out((512, wide), BF) for _ in range(count)]
+    weight_grad(slot, lefts, rights, (blocks, (512, wide)), [(512 * k, 0) for k in range(count)], flags, 4.5)
+    for k in range(count):
+        plane.scatter(blocks[k], 1, True, 1, starts[k], flags[k], None, (out, (512 * k, 0)))
 
 
 def general_row_total(value):
@@ -1555,11 +1714,6 @@
     )
 
 
-def weight_grad(left, right):
-    value = dot_tn(left[0], right[0]) + dot_tn(left[1], right[1])
-    return value.astype(BF)
-
-
 class Batch:
     pass
 
@@ -1586,49 +1740,61 @@
     seg_pad = jnp.concatenate([segments, jnp.zeros((8 - seqs, count), segments.dtype)], axis=0)
     norms = (q_gain, k_gain)
 
+    quarters = [(512 * k, 512) for k in range(ff // 512)]
+    wg, wu = [], []
+
     s = Slot("slot0", 0)
     line = Line(s, rows, width, gather=one.x)
-    full = [attach(s, PlaneGather(w, 0, True, 4.0 * i, done="w%d" % i))[0] for i, w in enumerate((w_query, w_key, w_value))]
-    w_out_h = attach(s, PlaneGather(w_out, 1, True, 12.0))[0]
-    seg_h = attach(s, PlaneGather(seg_pad, 0, False, 2.0))[0]
+    plane = Plane(s)
+    seg_h = plane.gather(seg_pad, 0, False)
+    full = [plane.gather(w, 0, True, done="w%d" % i) for i, w in enumerate((w_query, w_key, w_value))]
+    w_out_h = plane.gather(w_out, 1, True)
+    some = [plane.gather(w_gate, 0, True, cols=c) for c in quarters[:2]]
     cosine, sine = tables(s, pos_cols, freqs, sign)
     made = project(s, line, rows, width, full, ("w0", "w1", "w2"), norms, cosine, sine, 0)
     s.run()
     wq, wk, wv = (h.value for h in full)
+    wg += [h.value for h in some]
     wo, seg_all, cosine, sine = w_out_h.value, seg_h.value, cosine.target.value, sine.target.value
     one.q_raw, one.k_raw, one.q, one.kv, one.qk_factor = (h.value for h in made)
     one.wide = line.out.value
 
     s = Slot("slot1", 1)
     line = Line(s, rows, width, gather=two.x)
-    kvs = attach(s, PlaneGather(one.kv, 0, False, done="kv"))[0]
-    w_gate_h = attach(s, PlaneGather(w_gate, 0, True, 9.0, lean=True))[0]
+    plane = Plane(s)
+    kvs = plane.gather(one.kv, 0, False, 4, done="kv")
+    some = [plane.gather(w_gate, 0, True, cols=c) for c in quarters[2:]]
+    more = plane.gather(w_up, 0, True, cols=quarters[0])
     s.mark_early("tables")
-    made = project(s, line, rows, width, (wq, wk, wv), None, norms, s.load(cosine), s.load(sine), rows)
     mask = Mask(s, seg_all, seg_cols, 0, count)
     felt = attend(s, "kv", kvs, one.q, mask, rows, width)
+    made = project(s, line, rows, width, (wq, wk, wv), None, norms, s.load(cosine), s.load(sine), rows)
     s.run()
-    wg, one.kvs = w_gate_h.value, kvs.value
+    wg += [h.value for h in some]
+    wu.append(more.value)
+    one.kvs = kvs.value
     two.q_raw, two.k_raw, two.q, two.kv, two.qk_factor = (h.value for h in made)
     one.heads, one.heads_b, one.logsum = (h.value for h in felt)
     two.wide = line.out.value
 
     s = Slot("slot2", 2)
     line = Line(s, rows, width, scatter=True)
-    kvs = attach(s, PlaneGather(two.kv, 0, False, done="kv"))[0]
-    w_up_h = attach(s, PlaneGather(w_up, 0, True, 9.0, lean=True))[0]
+    plane = Plane(s)
+    kvs = plane.gather(two.kv, 0, False, 4, done="kv")
+    some = [plane.gather(w_up, 0, True, cols=c) for c in quarters[1:]]
     ends = attn_finish(s, line, rows, width, one.x, attn_gain)
     produce(s, line, [s.load(one.heads_b)], [wo], (width, width), col_block, dot_nn, 0.6)
     mask = Mask(s, seg_all, seg_cols, per, count)
     felt = attend(s, "kv", kvs, two.q, mask, rows, width)
     s.run()
-    wu, two.kvs = w_up_h.value, kvs.value
+    wu += [h.value for h in some]
+    two.kvs = kvs.value
     one.attn, one.resid, one.resid_b, one.factor = (h.value for h in ends)
     two.heads, two.heads_b, two.logsum = (h.value for h in felt)
 
     s = Slot("slot3", 3)
     line = Line(s, rows, width, gather=one.resid_b, scatter=True)
-    w_down_h = attach(s, PlaneGather(w_down, 1, True))[0]
+    w_down_h = Plane(s).gather(w_down, 1, True, 4)
     ends = attn_finish(s, line, rows, width, two.x, attn_gain)
     produce(s, line, [s.load(two.heads_b)], [wo], (width, width), col_block, dot_nn, 0.6)
     inner = gate_up(s, line, rows, wg, wu)
@@ -1660,76 +1826,78 @@
     s = Slot("slot6", 6)
     line = Line(s, rows, width, gather=two.g_mlp_b, scatter=True)
     ends = resid_finish(s, line, rows, width, one.cot, one.attn, one.factor, attn_gain)
-    produce(s, line, [s.load(one.g_gate), s.load(one.g_up)], [wg, wu], (512, ff), row_block, dot_nt, 3.6)
+    produce(s, line, [s.load(one.g_gate), s.load(one.g_up)], wg + wu, (512, 512), row_block, dot_nt, 4.4)
     inner = act_back(s, line, rows, wd, two.gate, two.up)
     s.run()
     two.g_mlp = line.out.value
     one.g_resid, one.g_attn_b, one.g_attn_gain = (h.value for h in ends)
     two.g_gate, two.g_up = (h.value for h in inner)
 
-    d_down = weight_grad((one.act, two.act), (one.g_mlp, two.g_mlp))
     s = Slot("slot7", 7)
     line = Line(s, rows, width, gather=one.g_attn_b, scatter=True)
-    g_down = attach(s, PlaneScatter(d_down, 1, True))[0]
+    plane = Plane(s)
+    g_down = s.hbm_out(w_down.shape, F32)
     ends = resid_finish(s, line, rows, width, two.cot, two.attn, two.factor, attn_gain)
-    produce(s, line, [s.load(two.g_gate), s.load(two.g_up)], [wg, wu], (512, ff), row_block, dot_nt, 3.6)
+    produce(s, line, [s.load(two.g_gate), s.load(two.g_up)], wg + wu, (512, 512), row_block, dot_nt, 4.4)
     mask = Mask(s, seg_all, seg_cols, 0, count)
     back = attend_back(s, line, one.kvs, one.q, one.heads, one.logsum, mask, rows, width, wo)
+    wide_grad(s, plane, (one.act, two.act), (one.g_mlp, two.g_mlp), g_down, (22.0, 27.0, 31.0, 36.0), "d")
     s.run()
     one.g_attn = line.out.value
     two.g_resid, two.g_attn_b, two.g_attn_gain = (h.value for h in ends)
     one.g_q, one.g_kv = (h.value for h in back)
 
-    d_gate = weight_grad((one.mid, two.mid), (one.g_gate, two.g_gate))
     s = Slot("slot8", 8)
     line = Line(s, rows, width, gather=two.g_attn_b)
-    g_kv = attach(s, PlaneScatter(one.g_kv, 0, False, done="kv"))[0]
-    g_gate = attach(s, PlaneScatter(d_gate, 0, True, lean=True))[0]
+    plane = Plane(s)
+    g_kv = plane.scatter(one.g_kv, 0, False, 4, done="kv")
+    g_gate = s.hbm_out(w_gate.shape, F32)
     raws = project_back(s, "kv", one.g_q, g_kv, (one.q_raw, one.k_raw), one.qk_factor, norms, cosine, sine, 0, rows, width)
     mask = Mask(s, seg_all, seg_cols, per, count)
     back = attend_back(s, line, two.kvs, two.q, two.heads, two.logsum, mask, rows, width, wo)
+    tall_grad(s, plane, (one.mid, two.mid), (one.g_gate, two.g_gate), g_gate, (8.0, 13.0, 18.0, 22.0), "g")
     s.run()
     two.g_attn = line.out.value
     one.g_qr, one.g_kr, one.g_vr, one.g_q_gain, one.g_k_gain = (h.value for h in raws)
     two.g_q, two.g_kv = (h.value for h in back)
 
-    d_up = weight_grad((one.mid, two.mid), (one.g_up, two.g_up))
     s = Slot("slot9", 9)
     line = Line(s, rows, width, scatter=True)
-    g_kv = attach(s, PlaneScatter(two.g_kv, 0, False, done="kv"))[0]
-    g_up = attach(s, PlaneScatter(d_up, 0, True, lean=True))[0]
+    plane = Plane(s)
+    g_kv = plane.scatter(two.g_kv, 0, False, 4, done="kv")
+    g_up = s.hbm_out(w_up.shape, F32)
     fin_one = last_finish(s, line, rows, width, one.g_resid)[0]
     produce(s, line, [s.load(g) for g in (one.g_qr, one.g_kr, one.g_vr)], [wq, wk, wv], (512, width), row_block, dot_nt, 1.6)
     raws = project_back(s, "kv", two.g_q, g_kv, (two.q_raw, two.k_raw), two.qk_factor, norms, cosine, sine, rows, rows, width)
+    tall_grad(s, plane, (one.mid, two.mid), (one.g_up, two.g_up), g_up, (13.0, 18.0, 22.0, 27.0), "u")
     s.run()
     two.g_qr, two.g_kr, two.g_vr, two.g_q_gain, two.g_k_gain = (h.value for h in raws)
 
-    wides = (one.wide, two.wide)
-    grads = [
-        weight_grad(wides, (one.g_qr, two.g_qr)),
-        weight_grad(wides, (one.g_kr, two.g_kr)),
-        weight_grad(wides, (one.g_vr, two.g_vr)),
-        weight_grad((one.heads_b, two.heads_b), (one.g_attn, two.g_attn)),
-    ]
     s = Slot("slot10", 10)
     line = Line(s, rows, width, scatter=True)
-    planes = [attach(s, PlaneScatter(g, i // 3, True))[0] for i, g in enumerate(grads)]
+    plane = Plane(s)
     fin_two = last_finish(s, line, rows, width, two.g_resid)[0]
     produce(s, line, [s.load(g) for g in (two.g_qr, two.g_kr, two.g_vr)], [wq, wk, wv], (512, width), row_block, dot_nt, 1.6)
+    sums = gain_sums(
+        s,
+        (one.g_q_gain, two.g_q_gain, one.g_k_gain, two.g_k_gain)
+        + (one.g_attn_gain, two.g_attn_gain, one.g_mlp_gain, two.g_mlp_gain),
+    )
+    wides = (one.wide, two.wide)
+    g_q, g_k, g_v = (s.hbm_out(w_query.shape, F32) for _ in range(3))
+    g_out = s.hbm_out(w_out.shape, F32)
+    tall_grad(s, plane, wides, (one.g_qr, two.g_qr), g_q, (13.0,), "q")
+    tall_grad(s, plane, wides, (one.g_kr, two.g_kr), g_k, (18.0,), "k")
+    tall_grad(s, plane, wides, (one.g_vr, two.g_vr), g_v, (22.0,), "v")
+    wide_grad(s, plane, (one.heads_b, two.heads_b), (one.g_attn, two.g_attn), g_out, (27.0,), "o")
     s.run()
-    g_q, g_k, g_v, g_out = (h.value for h in planes)
-    gains = (
-        one.g_q_gain + two.g_q_gain,
-        one.g_k_gain + two.g_k_gain,
-        one.g_attn_gain + two.g_attn_gain,
-        one.g_mlp_gain + two.g_mlp_gain,
-    )
-    gains = lax.psum(tuple(jnp.sum(g, axis=0) for g in gains), ("dp", "ctx"))
+    gains = [sums.value[k] for k in range(4)]
     shape = (per, count, width)
     return (
         jnp.concatenate([one.out.reshape(shape), two.out.reshape(shape)], axis=0),
         jnp.concatenate([fin_one.value.reshape(shape), fin_two.value.reshape(shape)], axis=0),
-        g_q, g_k, g_v, g_out, g_gate.value, g_up.value, g_down.value, *gains,
+        *(g.value for g in (g_q, g_k, g_v, g_out, g_gate, g_up, g_down)),
+        *gains,
     )
 
 

time: 856 us -> 752 us (0.88)
  matrix products: 92.2 us -> 0 us
  blocking collectives: 12.6 us -> 0 us
    dot_general x14 -> x0, matrix products: 92.2 us -> none  [dot_tn(): lax.dot_general(left, right, (((0,), (0,)), ((), ())), preferred_element_...]
    psum x1 -> x0, blocking collectives: 12.6 us -> none  [planned(): gains = lax.psum(tuple((jnp.sum(g, axis=0) for g in gains)), ('dp', 'ctx'))]
where the time goes in v3:
time: 752 us; the launch traced here: 746 us
  Pallas kernels  724 us (96%)
  local copies, waits for them, and re-layouts  17.7 us (2%)
    pallas_call x11, Pallas kernels, run(): pl.pallas_call(self.kernel, out_shape=tuple((o for o, _ in self.outputs))...  724 us

profile of v3, /device:TPU:0, one launch (start us, length us, event | category | flops | bytes accessed | tf_op | source)
XLA Modules:
  0.0 745.8 jit_solution(2297096162796286240)
XLA Ops:
  0.6 0.0 copy-start.3
  0.7 0.6 maximum_bitcast_fusion.refs_9_
  1.3 0.7 copy.28
  1.9 0.7 copy.29
  2.6 1.3 concatenate.12.refs_1_
  3.9 1.0 broadcast_in_dim.18.refs_6_.refs_9_.refs_16_.refs_11_
  4.9 1.0 broadcast_in_dim.16.refs_8_
  5.9 2.2 fusion.1
  8.1 0.0 copy-done.3
  8.1 1.0 fusion
  9.2 68.0 %slot0.1 = (bf16[512,2048]{1,0:T(8,128)(2,1)}, s32[32,256]{1,0:T(8,128)}, bf16[2048,512]{1,0:T(8,128)(2,1)}, bf16[2048,512]{1,0:T(8,128)(2,1)}, bf16[2048,512]{1...) custom-call(bf16[512,512]{1,0:T(8,128)(2,1)} %bitcast.28, ...), custom_call_target="tpu_custom_call" | custom-call | tf_op jit(solution)/shard_map/slot0/pallas_call | solution.py:510
  77.2 63.2 %slot1.1 = (bf16[512,2048]{1,0:T(8,128)(2,1)}, bf16[2048,1024]{1,0:T(8,128)(2,1)}, bf16[2048,512]{1,0:T(8,128)(2,1)}, bf16[2048,512]{1,0:T(8,128)(2,1)}, bf16[20...) custom-call(bf16[512,512]{1,0:T(8,128)(2,1)} %bitcast.26, ...), custom_call_target="tpu_custom_call" | custom-call | tf_op jit(solution)/shard_map/slot1/pallas_call | solution.py:510
  140.4 64.2 %slot2.1 = (bf16[2048,1024]{1,0:T(8,128)(2,1)}, bf16[2048,512]{1,0:T(8,128)(2,1)}, bf16[2048,512]{1,0:T(8,128)(2,1)}, bf16[2048,512]{1,0:T(8,128)(2,1)}, f32[512...) custom-call(bf16[512,1024]{1,0:T(8,128)(2,1)} %get-tuple-element.117, ...), custom_call_target="tpu_custom_call" | custom-call | tf_op jit(solution)/shard_map/slot2/pallas_call | solution.py:510
  204.6 58.5 %slot3.1 = (bf16[512,2048]{1,0:T(8,128)(2,1)}, bf16[2048,2048]{1,0:T(8,128)(2,1)}, f32[512,512]{1,0:T(8,128)}, f32[512,512]{1,0:T(8,128)}, bf16[512,512]{1,0:T(8...) custom-call(bf16[512,512]{1,0:T(8,128)(2,1)} %get-tuple-element.121., ...), custom_call_target="tpu_custom_call" | custom-call | tf_op jit(solution)/shard_map/slot3/pallas_call | solution.py:510
  263.1 57.1 %slot4.1 = (bf16[512,2048]{1,0:T(8,128)(2,1)}, bf16[512,512]{1,0:T(8,128)(2,1)}, bf16[512,512]{1,0:T(8,128)(2,1)}, f32[8,512]{1,0:T(8,128)}, bf16[512,2048]{1,0:...) custom-call(bf16[512,512]{1,0:T(8,128)(2,1)} %get-tuple-element.131.refs_0_, ...), custom_call_target="tpu_custom_call" | custom-call | tf_op jit(solution)/shard_map/slot4/pallas_call | solution.py:510
  320.2 56.4 %slot5.1 = (bf16[512,2048]{1,0:T(8,128)(2,1)}, bf16[512,512]{1,0:T(8,128)(2,1)}, bf16[512,512]{1,0:T(8,128)(2,1)}, f32[8,512]{1,0:T(8,128)}, bf16[512,2048]{1,0:T(8,128)(2,1)}, /*index=5*/bf16[512,2048]{1,0:T(8,128)(2,1)}) custom-call(bf16[512,512]{1,0:T(8,128)(2,1)} %get-tuple-element.136.refs_0_, f32[512,512]{1,0:T(8,128)} %get-tuple-element.137.refs_1_, ...), custom_call_target="tpu_custom_call" | custom-call | tf_op jit(solution)/shard_map/slot5/pallas_call | solution.py:510
  376.7 55.3 %slot6.1 = (bf16[512,2048]{1,0:T(8,128)(2,1)}, f32[512,512]{1,0:T(8,128)}, bf16[512,512]{1,0:T(8,128)(2,1)}, f32[8,512]{1,0:T(8,128)}, bf16[512,2048]{1,0:T(8,128)(2,1)}, /*index=5*/bf16[512,2048]{1,0:T(8,128)(2,1)}) custom-call(bf16[512,512]{1,0:T(8,128)(2,1)} %get-tuple-element.142.refs_0_, bf16[512,512]{1,0:T(8,128)(2,1)} %bitcast.25, ...), custom_call_target="tpu_custom_call" | custom-call | tf_op jit(solution)/shard_map/slot6/pallas_call | solution.py:510
  432.0 78.7 %slot7.1 = (bf16[512,2048]{1,0:T(8,128)(2,1)}, f32[2048,256]{1,0:T(8,128)}, f32[512,512]{1,0:T(8,128)}, bf16[512,512]{1,0:T(8,128)(2,1)}, f32[8,512]{1,0:T(8,128...) custom-call(bf16[512,512]{1,0:T(8,128)(2,1)} %get-tuple-element.149., ...), custom_call_target="tpu_custom_call" | custom-call | tf_op jit(solution)/shard_map/slot7/pallas_call | solution.py:510
  510.7 77.8 %slot8.1 = (bf16[512,2048]{1,0:T(8,128)(2,1)}, f32[512,1024]{1,0:T(8,128)}, f32[256,2048]{1,0:T(8,128)}, bf16[512,512]{1,0:T(8,128)(2,1)}, bf16[512,512]{1,0:T(8...) custom-call(bf16[512,512]{1,0:T(8,128)(2,1)} %get-tuple-element.159., ...), custom_call_target="tpu_custom_call" | custom-call | tf_op jit(solution)/shard_map/slot8/pallas_call | solution.py:510
  588.6 78.6 %slot9.1 = (f32[512,1024]{1,0:T(8,128)}, f32[256,2048]{1,0:T(8,128)}, bf16[512,512]{1,0:T(8,128)(2,1)}, bf16[512,512]{1,0:T(8,128)(2,1)}, bf16[512,512]{1,0:T(8,...) custom-call(bf16[2048,1024]{1,0:T(8,128)(2,1)} %get-tuple-element.17, ...), custom_call_target="tpu_custom_call" | custom-call | tf_op jit(solution)/shard_map/slot9/pallas_call | solution.py:510
  667.1 0.0 copy-start.8
  667.1 0.0 copy-start.9
  667.1 0.0 copy-start.10
  667.1 65.7 %slot10.1 = (bf16[512,512]{1,0:T(8,128)(2,1)}, f32[8,512]{1,0:T(8,128)}, f32[256,512]{1,0:T(8,128)}, f32[256,512]{1,0:T(8,128)}, f32[256,512]{1,0:T(8,128)}, /*i...) custom-call(f32[512,512]{1,0:T(8,128)} %get-tuple-element.180.refs_0, ...), custom_call_target="tpu_custom_call" | custom-call | tf_op jit(solution)/shard_map/slot10/pallas_call | solution.py:510
  732.9 0.0 copy-done.8
  732.9 0.0 copy-done.9
  732.9 0.0 copy-done.10
  732.9 0.0 copy-start.11
  732.9 0.0 copy-start.7
  732.9 0.0 copy-start.6
  732.9 2.6 pad_maximum_fusion
  735.6 0.0 copy-start.5
  735.6 0.0 copy-done.11
  735.6 0.6 fusion.2
  736.2 0.0 copy-done.7
  736.2 0.8 copy.37
  737.0 0.0 copy-done.6
  737.0 0.8 copy.38
  737.8 0.0 copy-done.5
  737.8 0.8 copy.39
  738.6 0.0 copy-done.4
  738.6 0.8 copy.40
  739.4 0.0 copy-done.1
  739.4 1.3 copy.41
  740.7 1.0 copy-done.2
  741.7 1.3 copy.42
  743.0 1.0 copy-done
  744.1 1.3 copy.43
  (5 shorter events, 0.0 us)
Async XLA Ops:
  0.6 7.5 %copy-start.3 = (bf16[4,256,512]{2,1,0:T(8,128)(2,1)S(1)}, bf16[4,256,512]{2,1,0:T(8,128)(2,1)}, u32[]{:S(2)}) copy-start(bf16[4,256,512]{2,1,0:T(8,128)(2,1)} %param.16) | copy-start | bytes 3145732
  667.1 65.8 %copy-start.8 = (bf16[512,512]{1,0:T(8,128)(2,1)S(1)}, bf16[512,512]{1,0:T(8,128)(2,1)}, u32[]{:S(2)}) copy-start(bf16[512,512]{1,0:T(8,128)(2,1)} %get-tuple-element.135) | copy-start | bytes 1572868
  667.1 65.8 %copy-start.9 = (bf16[512,512]{1,0:T(8,128)(2,1)S(1)}, bf16[512,512]{1,0:T(8,128)(2,1)}, u32[]{:S(2)}) copy-start(bf16[512,512]{1,0:T(8,128)(2,1)} %get-tuple-element.141) | copy-start | bytes 1572868
  667.1 65.8 %copy-start.10 = (bf16[512,512]{1,0:T(8,128)(2,1)S(1)}, bf16[512,512]{1,0:T(8,128)(2,1)}, u32[]{:S(2)}) copy-start(bf16[512,512]{1,0:T(8,128)(2,1)} %get-tuple-element.179) | copy-start | bytes 1572868
  732.9 2.7 copy-start.11
  732.9 3.3 copy-start.7
  732.9 4.0 copy-start.6
  735.6 2.2 copy-start.5
  735.6 3.0 copy-start.4
  736.2 3.2 copy-start.1
  739.4 2.3 copy-start.2
  741.7 2.3 copy-start

commit v4 on v3

--- a/solution.py
+++ b/solution.py
@@ -62,19 +62,30 @@
         return job.out
 
     def plan(self):
-        load = [0.0, 0.0]
-        for job in self.jobs:
-            load[0] += job.unit * job.pieces
-            load[1] += job.unit * job.pieces if job.with_dp else 0.0
-        steps = []
-        for job in self.jobs:
-            for p in range(job.pieces):
-                via = 0 if load[0] < load[1] else 1
-                if job.with_dp:
-                    load[via] += job.unit
-                steps += job.steps(p, via)
+        pieces = [(job, p) for job in self.jobs for p in range(job.pieces)]
+        choice, load = {}, [0.0, 0.0]
+        for job, p in pieces:
+            load[0] += job.unit
+            load[1] += job.unit if job.with_dp else 0.0
+        for job, p in pieces:
+            via = 0 if load[0] < load[1] else 1
+            choice[job, p] = via
+            if job.with_dp:
+                load[via] += job.unit
+        best = self.lay(choice)
+        for _ in range(2):
+            for key in pieces:
+                if key[0].with_dp:
+                    trial = dict(choice)
+                    trial[key] = 1 - trial[key]
+                    result = self.lay(trial)
+                    if result[0] < best[0] - 0.01:
+                        choice, best = trial, result
+        self.actions = best[1]
+
+    def lay(self, choice):
+        steps = [step for job in self.jobs for p in range(job.pieces) for step in job.steps(p, choice[job, p])]
         times, free, actions = {}, [0.0, 0.0], []
-        begun = [0.0, 0.0]
         pending = list(steps)
         while pending:
             best = None
@@ -82,23 +93,22 @@
                 if any((step.job, d) not in times for d in step.deps):
                     continue
                 ready = max([step.job.start] + [times[step.job, d] for d in step.deps])
-                when_free = ready if step.link is None else max(ready, free[step.link])
-                key = (when_free, step.job.number, step.rank)
+                key = (ready, step.job.number, step.rank)
                 if best is None or key < best[0]:
-                    best = (key, step, ready, when_free)
-            _, step, ready, begin = best
+                    best = (key, step)
+            (ready, _, _), step = best
             pending.remove(step)
-            end = begin + step.time
-            if step.link is not None:
-                issue_at = max(ready, begun[step.link])
-                begun[step.link], free[step.link] = begin, end
-                actions.append((issue_at, 1, len(actions), step.job, step.issue))
-            arrive_at = end + (0.7 if step.link is not None else 0.0)
+            if step.link is None:
+                arrive_at = ready + step.time
+            else:
+                begin = max(ready, free[step.link])
+                free[step.link] = begin + step.time
+                actions.append((ready, 1, len(actions), step.job, step.issue))
+                arrive_at = begin + step.time + 0.7
             actions.append((arrive_at, 0, len(actions), step.job, step.arrive))
             times[step.job, step.name] = arrive_at
         actions.sort(key=lambda a: a[:3])
-        self.actions = actions
-        self.end = max(a[0] for a in actions)
+        return sum(times.values()) / len(times) / 10 + max(times.values()), actions
 
 
 class Job:
@@ -112,6 +122,8 @@
         shift = max(0.0, slot.now - self.start) if self.after is not None else 0.0
         yield ("at", self.start)
         self.begin()
+        yield ("at", self.start + shift + 1.0)
+        self.settle()
         for time, _, _, job, emit in plane.actions:
             if job is self:
                 yield ("at", time + shift)
@@ -128,6 +140,9 @@
 
     def got(self, index, target):
         remote(target, target, self.slot, self.base + 2 * index, self.base + 2 * index + 1, self.cdev).wait_recv()
+
+    def settle(self):
+        pass
 
     def coordinates(self):
         self.dp, self.ctx = self.slot.place.dp, self.slot.place.ctx
@@ -145,10 +160,11 @@
         if cols is not None:
             shape[1] = cols[1]
         self.size, self.rows = shape[dim], shape[0]
-        self.unit = math.prod(shape) * 2 / 43e3 / pieces
+        self.unit = math.prod(shape) * 2 / (slot.rates[1] * 1e3) / pieces
+        self.hold = slot.vmem(tuple(shape), array.dtype)
         shape[dim] *= 8 if with_dp else 4
         self.out = slot.hbm_out(tuple(shape), array.dtype)
-        self.own = slot.sems(1)
+        self.own = slot.sems(2)
         self.base = slot.sems(2 * pieces * 7)
 
     def spot(self, d, c, p):
@@ -171,7 +187,12 @@
         else:
             block = self.dp * 4 + self.ctx if self.with_dp else self.ctx
             mine = self.out.ref.at[pl.ds(pl.multiple_of(block * self.size, self.size), self.size)]
-        self.kept = pltpu.make_async_copy(src, mine, self.slot.sem(self.own))
+        self.held = pltpu.make_async_copy(src, self.hold.ref, self.slot.sem(self.own))
+        self.kept = pltpu.make_async_copy(self.hold.ref, mine, self.slot.sem(self.own + 1))
+        self.held.start()
+
+    def settle(self):
+        self.held.wait()
         self.kept.start()
 
     def steps(self, p, via):
@@ -228,7 +249,7 @@
         shape[dim] //= 2 * chips
         self.size = shape[dim]
         self.rows, self.width = shape
-        self.unit = math.prod(shape) * 2 / 43e3 / pieces
+        self.unit = math.prod(shape) * 2 / (slot.rates[1] * 1e3) / pieces
         if out is None:
             self.out, self.where = slot.hbm_out(tuple(shape), F32), None
         else:
@@ -364,6 +385,7 @@
     sem = None
     waited = False
     lazy = False
+    halves = False
     value = None
 
     def __init__(self, shape=None, dtype=None):
@@ -371,13 +393,15 @@
 
 
 class Slot:
-    def __init__(self, name, ident):
+    def __init__(self, name, ident, line_rate=97.0, plane_rate=48.0):
         self.name, self.ident = name, ident
+        self.rates = (line_rate, plane_rate)
         self.inputs, self.outputs, self.scratch = [], [], []
         self.sem_count = 0
         self.tasks = []
         self.axes = set()
         self.early = []
+        self.prologue = []
         self.plane = None
         self.loads, self.stores = [], []
         self.flags = {}
@@ -415,7 +439,7 @@
     def store(self, shape, dtype):
         handle = self.vmem(shape, dtype)
         handle.target = self.hbm_out(shape, dtype)
-        handle.sem = self.sems(1)
+        handle.sem = self.sems(2)
         self.stores.append(handle)
         return handle
 
@@ -440,6 +464,13 @@
     def flush(self, *handles):
         for handle in handles:
             pltpu.make_async_copy(handle.ref, handle.target.ref, self.sem(handle.sem)).start()
+
+    def flush_half(self, h, *handles):
+        for handle in handles:
+            half = handle.shape[0] // 2
+            part = pl.ds(h * half, half)
+            handle.halves = True
+            pltpu.make_async_copy(handle.ref.at[part], handle.target.ref.at[part], self.sem(handle.sem + h)).start()
 
     def sem(self, index):
         return self.sem_ref.at[index]
@@ -467,6 +498,8 @@
             handle.waited = False
             if not handle.lazy:
                 pltpu.make_async_copy(handle.source.ref, handle.ref, self.sem(handle.sem)).start()
+        for begin in self.prologue:
+            begin()
         self.place = place = Place(4)
         barrier = pltpu.get_barrier_semaphore()
         peers = []
@@ -504,7 +537,13 @@
                 got = ("at", self.now)
             entry[0] = got
         for handle in self.stores:
-            pltpu.make_async_copy(handle.ref, handle.target.ref, self.sem(handle.sem)).wait()
+            if not handle.halves:
+                pltpu.make_async_copy(handle.ref, handle.target.ref, self.sem(handle.sem)).wait()
+                continue
+            half = handle.shape[0] // 2
+            for h in (0, 1):
+                part = pl.ds(h * half, half)
+                pltpu.make_async_copy(handle.ref.at[part], handle.target.ref.at[part], self.sem(handle.sem + h)).wait()
 
     def run(self):
         values = pl.pallas_call(
@@ -565,7 +604,7 @@
             self.skip = self.steps - 3
             self.came = slot.vmem((2, 3, rows, width), BF)
         self.base = slot.sems(4 * self.steps * pieces)
-        self.unit = rows * width * 4 / 88e3
+        self.unit = rows * width * 4 / (slot.rates[0] * 1e3)
         slot.add(self.body, True)
 
     def chunk(self, k):
@@ -655,10 +694,10 @@
         for p in range(self.pieces):
             yield ("at", start + (self.steps - 1 + (p + 1) / self.pieces) * self.unit + 0.5)
             self.arrivals(self.steps - 1, p)
+            if self.scatter and (2 * p + 2) % self.pieces == 0:
+                slot.mark("reduced%d" % (2 * (p + 1) // self.pieces - 1))
         if self.gather and self.steps == 3:
             slot.mark("chunk3")
-        if self.scatter:
-            slot.mark("reduced")
         outs = []
         if self.gather and self.keep:
             for c in range(4):
@@ -688,21 +727,23 @@
 
 
 class Weights:
-    def __init__(self, slot, arrays, shape, order, where):
+    def __init__(self, slot, groups, shape, order, where):
         self.slot, self.order, self.where = slot, order, where
-        self.arrays = [slot.hbm_in(a) for a in arrays]
-        self.buffer = slot.vmem((2, len(arrays)) + shape, BF)
-        self.base = slot.sems(2 * len(arrays))
-        self.step = 0
+        self.groups = [[slot.hbm_in(a) for a in group] for group in groups]
+        self.wide = shape[1] // len(groups[0])
+        self.buffer = slot.vmem((2, len(groups)) + shape, BF)
+        self.base = slot.sems(2 * sum(len(g) for g in groups))
 
     def copies(self, step):
         block = self.order[step] if not callable(self.order) else self.order(step)
-        for j, array in enumerate(self.arrays):
-            yield pltpu.make_async_copy(
-                self.where(array.ref, block),
-                self.buffer.ref.at[step % 2, j],
-                self.slot.sem(self.base + 2 * j + step % 2),
-            )
+        index = self.base + step % 2
+        for j, group in enumerate(self.groups):
+            for k, array in enumerate(group):
+                target = self.buffer.ref.at[step % 2, j]
+                if len(group) > 1:
+                    target = target.at[:, pl.ds(k * self.wide, self.wide)]
+                yield pltpu.make_async_copy(self.where(array.ref, block), target, self.slot.sem(index))
+                index += 2
 
     def start(self, step):
         for copy in self.copies(step):
@@ -711,7 +752,7 @@
     def take(self, step):
         for copy in self.copies(step):
             copy.wait()
-        return [self.buffer.ref.at[step % 2, j] for j in range(len(self.arrays))]
+        return [self.buffer.ref.at[step % 2, j] for j in range(len(self.groups))]
 
 
 def row_block(ref, c):
@@ -722,8 +763,8 @@
     return ref.at[:, pl.ds(pl.multiple_of(c * 512, 512), 512)]
 
 
-def consume(slot, line, arrays, shape, where, last, multiply, cost, flag):
-    weights = Weights(slot, arrays, shape, line.chunk, where)
+def consume(slot, line, groups, shape, where, last, multiply, parts, cost):
+    weights = Weights(slot, groups, shape, line.chunk, where)
 
     def body():
         weights.start(0)
@@ -734,10 +775,10 @@
             blocks = weights.take(k)
             chunk = line.chunk(k)
             for j, block in enumerate(blocks):
-                multiply(k == 0, line.wide.ref.at[chunk], block, j)
-                yield ("did", cost)
+                for part in range(parts):
+                    multiply(k == 0, line.wide.ref.at[chunk], block, j, part)
+                    yield ("did", cost)
         yield from last()
-        slot.mark(flag)
 
     slot.add(body)
 
@@ -750,54 +791,81 @@
     return lax.dot_general(left, right, (((1,), (1,)), ((), ())), preferred_element_type=F32)
 
 
-def produce(slot, line, lefts, arrays, shape, where, dot, cost):
+def produce(slot, line, lefts, groups, shape, where, dot, cost, gate=None):
     order = (3, 0, 2, 1)
-    weights = Weights(slot, arrays, shape, order, where)
-    each = len(arrays) // len(lefts)
+    weights = Weights(slot, groups, shape, order, where)
 
     def body():
         weights.start(0)
+        if gate is not None:
+            yield ("flag", gate)
         slot.need(*lefts)
+        half = line.rows // 2
         for k, c in enumerate(order):
             if k < 3:
                 weights.start(k + 1)
             blocks = weights.take(k)
-            value = None
-            for j, block in enumerate(blocks):
-                left = lefts[j // each].ref
-                wide = left.shape[1] // each
-                term = dot(left[:, pl.ds((j % each) * wide, wide)], block[...])
-                value = term if value is None else value + term
-            line.mine.ref[c] = value.astype(BF)
-            yield ("did", cost)
+            for h in (0, 1):
+                part = pl.ds(h * half, half)
+                value = None
+                for left, block in zip(lefts, blocks):
+                    term = dot(left.ref[part], block[...])
+                    value = term if value is None else value + term
+                line.mine.ref[c, part] = value.astype(BF)
+                yield ("did", cost / 2)
             slot.mark("part%d" % c)
 
     slot.add(body)
 
 
-def weight_grad(slot, lefts, rights, out, where, flags, cost):
+def joined(slot, arrays):
+    rows = arrays[0].shape[0]
+    handle = slot.vmem((len(arrays) * rows, arrays[0].shape[1]), arrays[0].dtype)
+    sources = [slot.hbm_in(a) for a in arrays]
+    base = slot.sems(len(arrays))
+
+    def copies():
+        return [
+            pltpu.make_async_copy(a.ref, handle.ref.at[pl.ds(b * rows, rows)], slot.sem(base + b)) for b, a in enumerate(sources)
+        ]
+
+    def begin():
+        handle.waited = False
+        for copy in copies():
+            copy.start()
+
+    def ready():
+        if not handle.waited:
+            handle.waited = True
+            for copy in copies():
+                copy.wait()
+
+    slot.prologue.append(begin)
+    handle.ready = ready
+    return handle
+
+
+def weight_grad(slot, left, right, out, where, flags, cost, gates):
     buffer = slot.vmem(out[1], BF)
     base = slot.sems(1)
 
     def body():
-        slot.need(*lefts, *rights)
+        yield ("at", 2.5)
         tall, wide = out[1]
+        target = buffer.ref
         for k, (rows, cols) in enumerate(where):
-            target = buffer.ref
-
-            @pl.loop(0, (tall // 512) * (wide // 512))
-            def _(i):
-                r, c = (i, 0) if wide == 512 else (0, i)
-                row = pl.ds(pl.multiple_of(rows + r * 512, 512), 512)
-                col = pl.ds(pl.multiple_of(cols + c * 512, 512), 512)
-                value = dot_tn(lefts[0].ref[:, row], rights[0].ref[:, col])
-                value = value + dot_tn(lefts[1].ref[:, row], rights[1].ref[:, col])
-                here = (pl.ds(pl.multiple_of(r * 512, 512), 512), pl.ds(pl.multiple_of(c * 512, 512), 512))
-                target[here] = value.astype(BF)
-
+            if gates is not None:
+                yield ("flag", gates[k])
+            left.ready()
+            right.ready()
+            for i in range((tall // 512) * (wide // 512)):
+                r, c = (512 * i, 0) if wide == 512 else (0, 512 * i)
+                value = dot_tn(left.ref[:, pl.ds(rows + r, 512)], right.ref[:, pl.ds(cols + c, 512)])
+                target[pl.ds(r, 512), pl.ds(c, 512)] = value.astype(BF)
+                yield ("did", cost / 4)
             copy = pltpu.make_async_copy(target, out[0][k].ref, slot.sem(base))
             copy.start()
-            yield ("did", cost)
+            yield ("at", slot.now + 0.7)
             copy.wait()
             slot.mark(flags[k])
 
@@ -841,36 +909,70 @@
         return self.total.ref[part, k : k + 1]
 
 
+def finish(slot, line, rows, begin, first, second, flushed, ended, needs):
+    half = rows // 2
+    left = []
+
+    def make(h):
+        totals = RowTotals(slot, half)
+
+        def body():
+            yield ("flag", "reduced%d" % h)
+            if h == 0:
+                left[:] = [0, 1]
+                slot.need(*needs)
+                begin()
+            for i in range(2):
+                tiled_at(h * half + i * (half // 2), half // 2, 32, lambda part, here: first(totals, part, here), i * (half // 2))
+                yield ("did", 0.5)
+            yield from totals.exchange()
+            tiled_at(h * half, half, 32, lambda part, here: second(totals, part, here), 0)
+            slot.flush_half(h, *flushed)
+            left.remove(h)
+            if not left:
+                slot.flush(*ended)
+            yield ("did", 1.5)
+
+        slot.add(body)
+
+    make(0)
+    make(1)
+
+
+def tiled_at(row, count, tile, body, local):
+    @pl.loop(0, count // tile)
+    def _(i):
+        body(
+            pl.ds(pl.multiple_of(row + i * tile, tile), tile),
+            pl.ds(pl.multiple_of(local + i * tile, tile), tile),
+        )
+
+
+def fold_rows(value):
+    total = value[0:8]
+    for i in range(1, value.shape[0] // 8):
+        total = total + value[8 * i : 8 * i + 8]
+    return total
+
+
 def attn_finish(slot, line, rows, width, x, gain):
     x, gain = slot.load(x), slot.load(gain.reshape(1, width))
     raw, resid = slot.store((rows, width), F32), slot.store((rows, width), F32)
     resid_b, factor = slot.store((rows, width), BF), slot.store((rows, 128), F32)
-    totals = RowTotals(slot, rows)
-
-    def body():
-        yield ("flag", "reduced")
-
-        def first(part):
-            value = line.total(part)
-            raw.ref[part] = value
-            totals.put(part, jnp.sum(value * value, axis=1, keepdims=True))
-
-        tiled(rows, 32, first)
-        slot.need(x, gain)
-        slot.flush(raw)
-        yield from totals.exchange()
-
-        def second(part):
-            scale = lax.rsqrt(totals.column(part, 0) / D + EPS)
-            value = x.ref[part].astype(F32) + raw.ref[part] * scale * gain.ref[...]
-            resid.ref[part] = value
-            resid_b.ref[part] = value.astype(BF)
-            factor.ref[part] = jnp.broadcast_to(scale, (32, 128))
-
-        tiled(rows, 32, second)
-        slot.flush(resid_b, resid, factor)
-
-    slot.add(body)
+
+    def first(totals, part, here):
+        value = line.total(part)
+        raw.ref[part] = value
+        totals.put(here, jnp.sum(value * value, axis=1, keepdims=True))
+
+    def second(totals, part, here):
+        scale = lax.rsqrt(totals.column(here, 0) / D + EPS)
+        value = x.ref[part].astype(F32) + raw.ref[part] * scale * gain.ref[...]
+        resid.ref[part] = value
+        resid_b.ref[part] = value.astype(BF)
+        factor.ref[part] = jnp.broadcast_to(scale, (32, 128))
+
+    finish(slot, line, rows, lambda: None, first, second, (resid_b, raw, resid, factor), (), (x, gain))
     return [raw.target, resid.target, resid_b.target, factor.target]
 
 
@@ -879,38 +981,27 @@
     raw = slot.vmem((rows, width), F32)
     out, grad = slot.store((rows, width), BF), slot.store((rows, width), BF)
     gain_grad = slot.store((8, width), F32)
-    totals = RowTotals(slot, rows)
-
-    def body():
-        yield ("flag", "reduced")
-        slot.need(resid, cot, gain)
-
-        def first(part):
-            value = line.total(part)
-            raw.ref[part] = value
-            scaled = cot.ref[part].astype(F32) * gain.ref[...]
-            totals.put(part, jnp.sum(value * value, axis=1, keepdims=True), jnp.sum(scaled * value, axis=1, keepdims=True))
-
-        tiled(rows, 32, first)
+
+    def begin():
         gain_grad.ref[...] = jnp.zeros((8, width), F32)
-        yield from totals.exchange()
-
-        def second(part):
-            scale = lax.rsqrt(totals.column(part, 0) / D + EPS)
-            inner = totals.column(part, 1)
-            value = raw.ref[part]
-            given = cot.ref[part].astype(F32)
-            normed = value * scale
-            grad.ref[part] = (scale * (given * gain.ref[...]) - value * (scale * scale * scale * inner / D)).astype(BF)
-            out.ref[part] = (resid.ref[part] + normed * gain.ref[...]).astype(BF)
-            terms = given * normed
-            for i in range(4):
-                gain_grad.ref[...] += terms[8 * i : 8 * i + 8]
-
-        tiled(rows, 32, second)
-        slot.flush(grad, out, gain_grad)
-
-    slot.add(body)
+
+    def first(totals, part, here):
+        value = line.total(part)
+        raw.ref[part] = value
+        scaled = cot.ref[part].astype(F32) * gain.ref[...]
+        totals.put(here, jnp.sum(value * value, axis=1, keepdims=True), jnp.sum(scaled * value, axis=1, keepdims=True))
+
+    def second(totals, part, here):
+        scale = lax.rsqrt(totals.column(here, 0) / D + EPS)
+        inner = totals.column(here, 1)
+        value = raw.ref[part]
+        given = cot.ref[part].astype(F32)
+        normed = value * scale
+        grad.ref[part] = (scale * (given * gain.ref[...]) - value * (scale * scale * scale * inner / D)).astype(BF)
+        out.ref[part] = (resid.ref[part] + normed * gain.ref[...]).astype(BF)
+        gain_grad.ref[...] += fold_rows(given * normed)
+
+    finish(slot, line, rows, begin, first, second, (grad, out), (gain_grad,), (resid, cot, gain))
     return [out.target, grad.target, gain_grad.target]
 
 
@@ -918,102 +1009,78 @@
     cot, attn, factor, gain = slot.load(cot), slot.load(attn), slot.load(factor), slot.load(gain.reshape(1, width))
     resid, grad = slot.store((rows, width), F32), slot.store((rows, width), BF)
     gain_grad = slot.store((8, width), F32)
-    totals = RowTotals(slot, rows)
-
-    def body():
-        yield ("flag", "reduced")
-        slot.need(cot, attn, factor, gain)
-
-        def first(part):
-            value = line.total(part) + cot.ref[part].astype(F32)
-            resid.ref[part] = value
-            totals.put(part, jnp.sum(value * gain.ref[...] * attn.ref[part], axis=1, keepdims=True))
-
-        tiled(rows, 32, first)
+
+    def begin():
         gain_grad.ref[...] = jnp.zeros((8, width), F32)
-        slot.flush(resid)
-        yield from totals.exchange()
-
-        def second(part):
-            scale = factor.ref[part, 0:1]
-            inner = totals.column(part, 0)
-            value, given = attn.ref[part], resid.ref[part]
-            grad.ref[part] = (scale * (given * gain.ref[...]) - value * (scale * scale * scale * inner / D)).astype(BF)
-            terms = given * value * scale
-            for i in range(4):
-                gain_grad.ref[...] += terms[8 * i : 8 * i + 8]
-
-        tiled(rows, 32, second)
-        slot.flush(grad, gain_grad)
-
-    slot.add(body)
+
+    def first(totals, part, here):
+        value = line.total(part) + cot.ref[part].astype(F32)
+        resid.ref[part] = value
+        totals.put(here, jnp.sum(value * gain.ref[...] * attn.ref[part], axis=1, keepdims=True))
+
+    def second(totals, part, here):
+        scale = factor.ref[part, 0:1]
+        inner = totals.column(here, 0)
+        value, given = attn.ref[part], resid.ref[part]
+        grad.ref[part] = (scale * (given * gain.ref[...]) - value * (scale * scale * scale * inner / D)).astype(BF)
+        gain_grad.ref[...] += fold_rows(given * value * scale)
+
+    finish(slot, line, rows, begin, first, second, (grad, resid), (gain_grad,), (cot, attn, factor, gain))
     return [resid.target, grad.target, gain_grad.target]
 
 
 def last_finish(slot, line, rows, width, resid):
     resid = slot.load(resid)
     out = slot.store((rows, width), BF)
-
-    def body():
-        yield ("flag", "reduced")
-        slot.need(resid)
-
-        def first(part):
-            out.ref[part] = (line.total(part) + resid.ref[part]).astype(BF)
-
-        tiled(rows, 32, first)
-        slot.flush(out)
-
-    slot.add(body)
+    half = rows // 2
+
+    def make(h):
+        def body():
+            yield ("flag", "reduced%d" % h)
+            slot.need(resid)
+
+            def only(part, here):
+                out.ref[part] = (line.total(part) + resid.ref[part]).astype(BF)
+
+            tiled_at(h * half, half, 32, only, 0)
+            slot.flush_half(h, out)
+            yield ("did", 0.7)
+
+        slot.add(body)
+
+    make(0)
+    make(1)
     return [out.target]
 
 
-def given_partial(slot, line, array):
-    source = slot.hbm_in(array)
-    base = slot.sems(4)
-
-    def body():
-        copies = {}
-        for c in (3, 0, 2, 1):
-            copies[c] = pltpu.make_async_copy(
-                source.ref.at[:, pl.ds(c * line.width, line.width)], line.mine.ref.at[c], slot.sem(base + c)
-            )
-            copies[c].start()
-        yield ("at", 1.0)
-        for c in (3, 0, 2, 1):
-            copies[c].wait()
-            slot.mark("part%d" % c)
-
-    slot.add(body)
-
-
 def gate_up(slot, line, rows, w_gate, w_up):
-    parts, wide = len(w_gate), w_gate[0].shape[1]
-    ff = parts * wide
+    ff = len(w_gate) * w_gate[0].shape[1]
     acc = slot.vmem((2, rows, ff), F32)
     gate, up, act = (slot.store((rows, ff), BF) for _ in range(3))
-
-    def multiply(first, left, block, j):
-        cols = pl.ds((j % parts) * wide, wide)
-        value = dot_nn(left[...], block[...])
-        acc.ref[j // parts, :, cols] = value if first else acc.ref[j // parts, :, cols] + value
+    wide = ff // 2
+
+    def multiply(first, left, block, j, part):
+        cols = pl.ds(part * wide, wide)
+        value = dot_nn(left[...], block[:, cols])
+        acc.ref[j, :, cols] = value if first else acc.ref[j, :, cols] + value
 
     def last():
-        half = rows // 2
-        for h in (0, 1):
-
-            @pl.loop(0, half // 16)
+        piece = rows // 4
+        for h in range(4):
+
+            @pl.loop(0, piece // 16)
             def _(i):
-                part = pl.ds(pl.multiple_of(h * half + i * 16, 16), 16)
+                part = pl.ds(pl.multiple_of(h * piece + i * 16, 16), 16)
                 g, u = acc.ref[0, part], acc.ref[1, part]
                 gate.ref[part] = g.astype(BF)
                 up.ref[part] = u.astype(BF)
                 act.ref[part] = (g * jax.nn.sigmoid(g) * u).astype(BF)
 
-            yield ("did", 2.0)
-        slot.flush(act, gate, up)
-
-    consume(slot, line, tuple(w_gate) + tuple(w_up), (512, wide), row_block, last, multiply, 0.6, "mlp")
+            if h % 2:
+                slot.flush_half(h // 2, act, gate, up)
+            yield ("did", 1.0)
+
+    consume(slot, line, (w_gate, w_up), (512, ff), row_block, last, multiply, 2, 1.1)
     return [gate.target, up.target, act.target]
 
 
@@ -1022,31 +1089,31 @@
     acc = slot.vmem((rows, ff), F32)
     gate, up = slot.load(gate), slot.load(up)
     g_gate, g_up = slot.store((rows, ff), BF), slot.store((rows, ff), BF)
-
-    def multiply(first, left, block, j):
-        @pl.loop(0, ff // 1024)
-        def _(i):
-            cols = pl.ds(pl.multiple_of(i * 1024, 1024), 1024)
-            value = dot_nt(left[...], block[cols])
-            acc.ref[:, cols] = value if first else acc.ref[:, cols] + value
+    wide = ff // 2
+
+    def multiply(first, left, block, j, part):
+        cols = pl.ds(part * wide, wide)
+        value = dot_nt(left[...], block[cols])
+        acc.ref[:, cols] = value if first else acc.ref[:, cols] + value
 
     def last():
         slot.need(gate, up)
-        half = rows // 2
-        for h in (0, 1):
-
-            @pl.loop(0, half // 16)
+        piece = rows // 4
+        for h in range(4):
+
+            @pl.loop(0, piece // 16)
             def _(i):
-                part = pl.ds(pl.multiple_of(h * half + i * 16, 16), 16)
+                part = pl.ds(pl.multiple_of(h * piece + i * 16, 16), 16)
                 grad, g, u = acc.ref[part], gate.ref[part].astype(F32), up.ref[part].astype(F32)
                 sigma = jax.nn.sigmoid(g)
                 g_gate.ref[part] = (grad * u * sigma * (1.0 + g * (1.0 - sigma))).astype(BF)
                 g_up.ref[part] = (grad * g * sigma).astype(BF)
 
-            yield ("did", 2.5)
-        slot.flush(g_gate, g_up)
-
-    consume(slot, line, (w_down,), (ff, 512), col_block, last, multiply, 2.4, "back")
+            if h % 2:
+                slot.flush_half(h // 2, g_gate, g_up)
+            yield ("did", 1.2)
+
+    consume(slot, line, ((w_down,),), (ff, 512), col_block, last, multiply, 2, 1.2)
     return [g_gate.target, g_up.target]
 
 
@@ -1086,23 +1153,25 @@
     raws = [slot.store((rows, width), F32) for _ in (0, 1)]
     query, kv = slot.store((rows, width), BF), slot.store((rows, 2 * width), BF)
     factor = slot.store((rows, 128), F32)
-    totals = RowTotals(slot, rows)
     half = rows // 2
 
-    def body():
-        for j in range(3):
-            if flags is not None:
-                yield ("flag", flags[j])
-            slot.fetch(stages[j])
-        yield ("flag", "chunk3")
-        wide = line.wide.ref
-        for j in range(3):
-            slot.need(stages[j])
-            weight = stages[j].ref
-
-            @pl.loop(0, 2)
-            def _(i):
-                part = pl.ds(pl.multiple_of(i * half, half), half)
+    def make(h):
+        totals = RowTotals(slot, half)
+
+        def body():
+            part = pl.ds(h * half, half)
+            if h == 0:
+                for j in range(3):
+                    if flags is not None:
+                        yield ("flag", flags[j])
+                    slot.fetch(stages[j])
+                yield ("flag", "chunk3")
+            else:
+                yield ("flag", "stages")
+            wide = line.wide.ref
+            for j in range(3):
+                slot.need(stages[j])
+                weight = stages[j].ref
                 value = dot_nn(wide[0, part], weight[0:width])
                 for c in (1, 2, 3):
                     value = value + dot_nn(wide[c, part], weight[c * width : (c + 1) * width])
@@ -1110,57 +1179,64 @@
                     raws[j].ref[part] = value
                 else:
                     kv.ref[part, width : 2 * width] = value.astype(BF)
-
-            yield ("did", 2.0)
-
-        def first(part):
-            q, k = raws[0].ref[part], raws[1].ref[part]
-            totals.put(part, jnp.sum(q * q, axis=1, keepdims=True), jnp.sum(k * k, axis=1, keepdims=True))
-
-        tiled(rows, 32, first)
-        slot.flush(*raws)
-        yield from totals.exchange()
-        yield ("flag", "tables")
-        slot.need(*gains)
-        slot.need(*[t for t in (cosine, sine) if hasattr(t, "source")])
-
-        def second(part, trig):
-            lane = lax.broadcasted_iota(jnp.int32, (32, 128), 1)
-            scales = [lax.rsqrt(totals.column(part, j) / D + EPS) for j in (0, 1)]
-            factor.ref[part] = jnp.where(lane == 0, scales[0], scales[1])
-            co, si = cosine.ref[trig], sine.ref[trig]
-            for j, target in ((0, query), (1, kv)):
-                for h in range(width // HEAD_DIM):
-                    value = raws[j].ref[part, head_cols(h)] * scales[j] * gains[j].ref[:, head_cols(h)]
-                    target.ref[part, head_cols(h)] = (value * co + half_turn(value) * si).astype(BF)
-
-        @pl.loop(0, rows // 32)
-        def _(i):
-            second(pl.ds(pl.multiple_of(i * 32, 32), 32), pl.ds(pl.multiple_of(first_row + i * 32, 32), 32))
-
-        slot.flush(kv, query, factor)
-
-    slot.add(body)
+                yield ("did", 1.1)
+
+            def first(part, here):
+                q, k = raws[0].ref[part], raws[1].ref[part]
+                totals.put(here, jnp.sum(q * q, axis=1, keepdims=True), jnp.sum(k * k, axis=1, keepdims=True))
+
+            tiled_at(h * half, half, 32, first, 0)
+            slot.flush_half(h, *raws)
+            if h == 0:
+                slot.mark("stages")
+            yield from totals.exchange()
+            yield ("flag", "tables")
+            slot.need(*gains)
+            slot.need(*[t for t in (cosine, sine) if hasattr(t, "source")])
+
+            def second(part, here):
+                trig = pl.ds(pl.multiple_of(first_row + h * half + here.start, 32), 32)
+                lane = lax.broadcasted_iota(jnp.int32, (32, 128), 1)
+                scales = [lax.rsqrt(totals.column(here, j) / D + EPS) for j in (0, 1)]
+                factor.ref[part] = jnp.where(lane == 0, scales[0], scales[1])
+                co, si = cosine.ref[trig], sine.ref[trig]
+                for j, target in ((0, query), (1, kv)):
+                    for n in range(width // HEAD_DIM):
+                        value = raws[j].ref[part, head_cols(n)] * scales[j] * gains[j].ref[:, head_cols(n)]
+                        target.ref[part, head_cols(n)] = (value * co + half_turn(value) * si).astype(BF)
+
+            tiled_at(h * half, half, 32, second, 0)
+            slot.flush_half(h, kv, query, factor)
+            yield ("did", 1.5)
+
+        slot.add(body)
+
+    make(0)
+    make(1)
     return [raws[0].target, raws[1].target, query.target, kv.target, factor.target]
 
 
 class Mask:
-    def __init__(self, slot, seg_all, seg_cols, first, count):
-        self.slot, self.first, self.count = slot, first, count
+    def __init__(self, slot, seg_all, seg_cols, first, count, turned=False):
+        self.slot, self.first, self.count, self.turned = slot, first, count, turned
         self.keys, self.mine = slot.load(seg_all), slot.load(seg_cols)
-        self.mask = slot.vmem((count, 4 * count), F32)
+        self.mask = slot.vmem((4 * count, count) if turned else (count, 4 * count), F32)
 
     def fill(self, s):
         self.slot.need(self.keys, self.mine)
         count = self.count
         ctx = self.slot.place.ctx
-        mine = self.mine.ref[(self.first + s) * count : (self.first + s + 1) * count, 0:1]
+        mine = self.mine.ref[(self.first + s) * count : (self.first + s + 1) * count]
         for c in range(4):
             keys = self.keys.ref[8 * c + self.first + s : 8 * c + self.first + s + 1, :]
             row = ctx * count + lax.broadcasted_iota(jnp.int32, (count, count), 0)
             col = c * count + lax.broadcasted_iota(jnp.int32, (count, count), 1)
-            fine = jnp.logical_and(mine == keys, row >= col)
-            self.mask.ref[:, c * count : (c + 1) * count] = jnp.where(fine, 0.0, NEG)
+            fine = jnp.logical_and(mine[:, 0:1] == keys, row >= col)
+            block = jnp.where(fine, 0.0, NEG)
+            if self.turned:
+                self.mask.ref[c * count : (c + 1) * count] = jnp.transpose(block)
+            else:
+                self.mask.ref[:, c * count : (c + 1) * count] = block
 
 
 def attend(slot, flag, kv, query, mask, rows, width):
@@ -1182,34 +1258,37 @@
             mine = pl.ds(s * count, count)
             if s:
                 mask.fill(s)
-
-            @pl.loop(0, width // HEAD_DIM)
-            def _(h):
-                cols = pl.ds(pl.multiple_of(h * HEAD_DIM, HEAD_DIM), HEAD_DIM)
-                vcols = pl.ds(pl.multiple_of(width + h * HEAD_DIM, HEAD_DIM), HEAD_DIM)
-                q = query.ref[mine, cols]
-                peak = jnp.full((count, 1), NEG, F32)
-                for c in range(4):
-                    keys = kv.ref[pl.ds(c * rows + s * count, count), cols]
-                    block = pl.ds(c * count, count)
-                    value = dot_nt(q, keys) * scale + mask.mask.ref[:, block]
-                    logits.ref[:, block] = value
-                    peak = jnp.maximum(peak, jnp.max(value, axis=1, keepdims=True))
-                total = jnp.zeros((count, 1), F32)
-                acc = jnp.zeros((count, HEAD_DIM), F32)
-                for c in range(4):
-                    vals = kv.ref[pl.ds(c * rows + s * count, count), vcols]
-                    weight = jnp.exp(logits.ref[:, pl.ds(c * count, count)] - peak)
-                    total = total + jnp.sum(weight, axis=1, keepdims=True)
-                    acc = acc + dot_nn(weight.astype(BF), vals)
-                out = acc / total
-                heads.ref[mine, cols] = out
-                heads_b.ref[mine, cols] = out.astype(BF)
-                lane = lax.broadcasted_iota(jnp.int32, (count, 128), 1)
-                logsum.ref[mine] = jnp.where(lane == h, peak + jnp.log(total), logsum.ref[mine])
-
-            yield ("did", 4.0)
+                yield ("did", 1.0)
+            for pair in range(width // HEAD_DIM // 2):
+                heads_pair(s, mine, pair)
+                yield ("did", 2.2)
         slot.flush(heads_b, heads, logsum)
+
+    def heads_pair(s, mine, pair):
+        @pl.loop(2 * pair, 2 * pair + 2)
+        def _(h):
+            cols = pl.ds(pl.multiple_of(h * HEAD_DIM, HEAD_DIM), HEAD_DIM)
+            vcols = pl.ds(pl.multiple_of(width + h * HEAD_DIM, HEAD_DIM), HEAD_DIM)
+            q = query.ref[mine, cols]
+            peak = jnp.full((count, 1), NEG, F32)
+            for c in range(4):
+                keys = kv.ref[pl.ds(c * rows + s * count, count), cols]
+                block = pl.ds(c * count, count)
+                value = dot_nt(q, keys) * scale + mask.mask.ref[:, block]
+                logits.ref[:, block] = value
+                peak = jnp.maximum(peak, jnp.max(value, axis=1, keepdims=True))
+            total = jnp.zeros((count, 1), F32)
+            acc = jnp.zeros((count, HEAD_DIM), F32)
+            for c in range(4):
+                vals = kv.ref[pl.ds(c * rows + s * count, count), vcols]
+                weight = jnp.exp(logits.ref[:, pl.ds(c * count, count)] - peak)
+                total = total + jnp.sum(weight, axis=1, keepdims=True)
+                acc = acc + dot_nn(weight.astype(BF), vals)
+            out = acc / total
+            heads.ref[mine, cols] = out
+            heads_b.ref[mine, cols] = out.astype(BF)
+            lane = lax.broadcasted_iota(jnp.int32, (count, 128), 1)
+            logsum.ref[mine] = jnp.where(lane == h, peak + jnp.log(total), logsum.ref[mine])
 
     slot.add(body)
     return [heads.target, heads_b.target, logsum.target]
@@ -1221,9 +1300,10 @@
     grad = slot.vmem((rows, width), BF)
     g_query, g_kv = slot.store((rows, width), F32), slot.store((4 * rows, 2 * width), BF)
     acc = g_query
+    rows_of = slot.vmem((2, 128, count), F32)
     scale = 1.0 / math.sqrt(HEAD_DIM)
 
-    def multiply(first, left, block, j):
+    def multiply(first, left, block, j, part):
         value = dot_nt(left[...], block[...])
         acc.ref[...] = value if first else acc.ref[...] + value
 
@@ -1233,32 +1313,40 @@
         for s in range(rows // count):
             mine = pl.ds(s * count, count)
             mask.fill(s)
-            yield ("did", 1.0)
-
-            @pl.loop(0, width // HEAD_DIM)
-            def _(h):
-                cols = pl.ds(pl.multiple_of(h * HEAD_DIM, HEAD_DIM), HEAD_DIM)
-                vcols = pl.ds(pl.multiple_of(width + h * HEAD_DIM, HEAD_DIM), HEAD_DIM)
-                q, g = query.ref[mine, cols], grad.ref[mine, cols]
-                delta = jnp.sum(g.astype(F32) * heads.ref[mine, cols], axis=1, keepdims=True)
-                lane = lax.broadcasted_iota(jnp.int32, (count, 128), 1)
-                logs = jnp.sum(jnp.where(lane == h, logsum.ref[mine], 0.0), axis=1, keepdims=True)
-                total = jnp.zeros((count, HEAD_DIM), F32)
-                for c in range(4):
-                    there = pl.ds(c * rows + s * count, count)
-                    keys, vals = kv.ref[there, cols], kv.ref[there, vcols]
-                    value = dot_nt(q, keys) * scale + mask.mask.ref[:, pl.ds(c * count, count)]
-                    probs = jnp.exp(value - logs)
-                    slopes = (probs * (dot_nt(g, vals) - delta)).astype(BF)
-                    total = total + dot_nn(slopes, keys)
-                    g_kv.ref[there, cols] = (dot_tn(slopes, q) * scale).astype(BF)
-                    g_kv.ref[there, vcols] = dot_tn(probs.astype(BF), g).astype(BF)
-                g_query.ref[mine, cols] = total * scale
-
-            yield ("did", 8.0)
+            lane = lax.broadcasted_iota(jnp.int32, (count, 128), 1)
+            deltas = jnp.zeros((count, 128), F32)
+            for h in range(width // HEAD_DIM):
+                cols = head_cols(h)
+                delta = jnp.sum(grad.ref[mine, cols].astype(F32) * heads.ref[mine, cols], axis=1, keepdims=True)
+                deltas = jnp.where(lane == h, delta, deltas)
+            rows_of.ref[0] = jnp.transpose(logsum.ref[mine])
+            rows_of.ref[1] = jnp.transpose(deltas)
+            yield ("did", 1.5)
+            for pair in range(width // HEAD_DIM // 2):
+                heads_pair(s, mine, pair)
+                yield ("did", 3.0)
         slot.flush(g_kv, g_query)
 
-    consume(slot, line, (w_out,), (width, width), col_block, last, multiply, 0.6, "heads")
+    def heads_pair(s, mine, pair):
+        @pl.loop(2 * pair, 2 * pair + 2)
+        def _(h):
+            cols = pl.ds(pl.multiple_of(h * HEAD_DIM, HEAD_DIM), HEAD_DIM)
+            vcols = pl.ds(pl.multiple_of(width + h * HEAD_DIM, HEAD_DIM), HEAD_DIM)
+            q, g = query.ref[mine, cols], grad.ref[mine, cols]
+            logs, delta = rows_of.ref[0, pl.ds(h, 1)], rows_of.ref[1, pl.ds(h, 1)]
+            total = jnp.zeros((count, HEAD_DIM), F32)
+            for c in range(4):
+                there = pl.ds(c * rows + s * count, count)
+                keys, vals = kv.ref[there, cols], kv.ref[there, vcols]
+                value = dot_nt(keys, q) * scale + mask.mask.ref[pl.ds(c * count, count)]
+                probs = jnp.exp(value - logs)
+                slopes = (probs * (dot_nt(vals, g) - delta)).astype(BF)
+                total = total + dot_tn(slopes, keys)
+                g_kv.ref[there, cols] = (dot_nn(slopes, q) * scale).astype(BF)
+                g_kv.ref[there, vcols] = dot_nn(probs.astype(BF), g).astype(BF)
+            g_query.ref[mine, cols] = total * scale
+
+    consume(slot, line, ((w_out,),), (width, width), col_block, last, multiply, 1, 0.7)
     return [g_query.target, g_kv.target]
 
 
@@ -1274,54 +1362,66 @@
     cosine, sine = slot.load(cosine), slot.load(sine)
     outs = [slot.store((rows, width), BF) for _ in range(3)]
     gain_grads = [slot.store((8, width), F32) for _ in range(2)]
-    totals = RowTotals(slot, rows)
-
-    def body():
-        yield ("flag", flag)
-        slot.fetch(g_kv)
-        yield ("at", slot.now + 1.0)
-        slot.need(g_kv, g_query, factor, cosine, sine, *raws, *gains)
-        for g in gain_grads:
-            g.ref[...] = jnp.zeros((8, width), F32)
-
-        @pl.loop(0, rows // 32)
-        def _(i):
-            part = pl.ds(pl.multiple_of(i * 32, 32), 32)
-            trig = pl.ds(pl.multiple_of(first_row + i * 32, 32), 32)
-            co, si = cosine.ref[trig], sine.ref[trig]
-            sums = []
-            for j, source in ((0, g_query), (1, g_kv)):
-                scale = factor.ref[part, j : j + 1]
-                total = jnp.zeros((32, 1), F32)
-                for h in range(width // HEAD_DIM):
-                    cols = head_cols(h)
-                    value = source.ref[part, cols]
-                    value = value * co - half_turn(value) * si
-                    source.ref[part, cols] = value
-                    raw = raws[j].ref[part, cols]
-                    total = total + jnp.sum(value * gains[j].ref[:, cols] * raw, axis=1, keepdims=True)
-                    terms = value * raw * scale
-                    for r in range(4):
-                        gain_grads[j].ref[:, cols] += terms[8 * r : 8 * r + 8]
-                sums.append(total)
-            totals.put(part, *sums)
-
-        slot.flush(*gain_grads)
-        yield ("did", 3.0)
-        yield from totals.exchange()
-
-        def second(part):
-            for j, source in ((0, g_query), (1, g_kv)):
-                scale = factor.ref[part, j : j + 1]
-                inner = totals.column(part, j)
-                value = source.ref[part, 0:width] * gains[j].ref[...]
-                outs[j].ref[part] = (scale * value - raws[j].ref[part] * (scale * scale * scale * inner / D)).astype(BF)
-            outs[2].ref[part] = g_kv.ref[part, width : 2 * width].astype(BF)
-
-        tiled(rows, 32, second)
-        slot.flush(*outs)
-
-    slot.add(body)
+    half = rows // 2
+    left = []
+
+    def make(h):
+        totals = RowTotals(slot, half)
+
+        def body():
+            yield ("flag", flag)
+            if h == 0:
+                left[:] = [0, 1]
+                slot.fetch(g_kv)
+                for g in gain_grads:
+                    g.ref[...] = jnp.zeros((8, width), F32)
+                slot.need(g_query, factor, cosine, sine, *raws, *gains)
+                slot.need(g_kv)
+                slot.mark("grads")
+            else:
+                yield ("flag", "grads")
+
+            def first(part, here):
+                trig = pl.ds(pl.multiple_of(first_row + h * half + here.start, 32), 32)
+                co, si = cosine.ref[trig], sine.ref[trig]
+                sums = []
+                for j, source in ((0, g_query), (1, g_kv)):
+                    scale = factor.ref[part, j : j + 1]
+                    total = jnp.zeros((32, HEAD_DIM), F32)
+                    for n in range(width // HEAD_DIM):
+                        cols = head_cols(n)
+                        value = source.ref[part, cols]
+                        value = value * co - half_turn(value) * si
+                        source.ref[part, cols] = value
+                        term = value * raws[j].ref[part, cols]
+                        total = total + term * gains[j].ref[:, cols]
+                        gain_grads[j].ref[:, cols] += fold_rows(term * scale)
+                    sums.append(jnp.sum(total, axis=1, keepdims=True))
+                totals.put(here, *sums)
+
+            tiled_at(h * half, half, 32, first, 0)
+            left.remove(h)
+            if not left:
+                slot.flush(*gain_grads)
+            yield ("did", 1.5)
+            yield from totals.exchange()
+
+            def second(part, here):
+                for j, source in ((0, g_query), (1, g_kv)):
+                    scale = factor.ref[part, j : j + 1]
+                    inner = totals.column(here, j)
+                    value = source.ref[part, 0:width] * gains[j].ref[...]
+                    outs[j].ref[part] = (scale * value - raws[j].ref[part] * (scale * scale * scale * inner / D)).astype(BF)
+                outs[2].ref[part] = g_kv.ref[part, width : 2 * width].astype(BF)
+
+            tiled_at(h * half, half, 32, second, 0)
+            slot.flush_half(h, *outs)
+            yield ("did", 1.5)
+
+        slot.add(body)
+
+    make(0)
+    make(1)
     return [h.target for h in outs + gain_grads]
 
 
@@ -1356,26 +1456,22 @@
     return out.target
 
 
-def tall_grad(slot, plane, lefts, rights, out, starts, prefix):
-    tall, wide = lefts[0].shape[1], rights[0].shape[1]
-    lefts, rights = [slot.load(a) for a in lefts], [slot.load(a) for a in rights]
-    count = wide // 512
-    flags = [prefix + str(k) for k in range(count)]
-    blocks = [slot.hbm_out((tall, 512), BF) for _ in range(count)]
-    weight_grad(slot, lefts, rights, (blocks, (tall, 512)), [(0, 512 * k) for k in range(count)], flags, 4.5)
-    for k in range(count):
-        plane.scatter(blocks[k], 0, True, 1, starts[k], flags[k], None, (out, (0, 512 * k)))
-
-
-def wide_grad(slot, plane, lefts, rights, out, starts, prefix):
-    tall, wide = lefts[0].shape[1], rights[0].shape[1]
-    lefts, rights = [slot.load(a) for a in lefts], [slot.load(a) for a in rights]
-    count = tall // 512
-    flags = [prefix + str(k) for k in range(count)]
-    blocks = [slot.hbm_out((512, wide), BF) for _ in range(count)]
-    weight_grad(slot, lefts, rights, (blocks, (512, wide)), [(512 * k, 0) for k in range(count)], flags, 4.5)
-    for k in range(count):
-        plane.scatter(blocks[k], 1, True, 1, starts[k], flags[k], None, (out, (512 * k, 0)))
+def grad_blocks(left, right, tall):
+    rows, cols = left.shape[1], right.shape[1]
+    if tall:
+        return (rows, 512), [(0, 512 * k) for k in range(cols // 512)]
+    return (512, cols), [(512 * k, 0) for k in range(rows // 512)]
+
+
+def full_grad(slot, plane, left, right, tall, out, starts, prefix, chosen=None, gates=None):
+    shape, where = grad_blocks(left, right, tall)
+    chosen = range(len(where)) if chosen is None else chosen
+    flags = [prefix + str(k) for k in chosen]
+    blocks = [slot.hbm_out(shape, BF) for _ in chosen]
+    base = where[chosen[0]]
+    weight_grad(slot, left, right, (blocks, shape), [where[k] for k in chosen], flags, 3.6, gates)
+    for i, k in enumerate(chosen):
+        plane.scatter(blocks[i], 0 if tall else 1, True, 1, starts[i], flags[i], None, (out, (where[k][0] - base[0], where[k][1] - base[1])))
 
 
 def general_row_total(value):
@@ -1748,8 +1844,8 @@
     plane = Plane(s)
     seg_h = plane.gather(seg_pad, 0, False)
     full = [plane.gather(w, 0, True, done="w%d" % i) for i, w in enumerate((w_query, w_key, w_value))]
-    w_out_h = plane.gather(w_out, 1, True)
-    some = [plane.gather(w_gate, 0, True, cols=c) for c in quarters[:2]]
+    w_out_h = plane.gather(w_out, 1, True, 1, 12.0)
+    some = [plane.gather(w_gate, 0, True, 1, t, cols=c) for t, c in zip((18.0, 26.0), quarters)]
     cosine, sine = tables(s, pos_cols, freqs, sign)
     made = project(s, line, rows, width, full, ("w0", "w1", "w2"), norms, cosine, sine, 0)
     s.run()
@@ -1777,13 +1873,13 @@
     one.heads, one.heads_b, one.logsum = (h.value for h in felt)
     two.wide = line.out.value
 
-    s = Slot("slot2", 2)
+    s = Slot("slot2", 2, 160.0, 80.0)
     line = Line(s, rows, width, scatter=True)
     plane = Plane(s)
     kvs = plane.gather(two.kv, 0, False, 4, done="kv")
     some = [plane.gather(w_up, 0, True, cols=c) for c in quarters[1:]]
     ends = attn_finish(s, line, rows, width, one.x, attn_gain)
-    produce(s, line, [s.load(one.heads_b)], [wo], (width, width), col_block, dot_nn, 0.6)
+    produce(s, line, [s.load(one.heads_b)], [[wo]], (width, width), col_block, dot_nn, 0.6)
     mask = Mask(s, seg_all, seg_cols, per, count)
     felt = attend(s, "kv", kvs, two.q, mask, rows, width)
     s.run()
@@ -1792,31 +1888,31 @@
     one.attn, one.resid, one.resid_b, one.factor = (h.value for h in ends)
     two.heads, two.heads_b, two.logsum = (h.value for h in felt)
 
-    s = Slot("slot3", 3)
+    s = Slot("slot3", 3, 200.0, 80.0)
     line = Line(s, rows, width, gather=one.resid_b, scatter=True)
     w_down_h = Plane(s).gather(w_down, 1, True, 4)
     ends = attn_finish(s, line, rows, width, two.x, attn_gain)
-    produce(s, line, [s.load(two.heads_b)], [wo], (width, width), col_block, dot_nn, 0.6)
+    produce(s, line, [s.load(two.heads_b)], [[wo]], (width, width), col_block, dot_nn, 0.6)
     inner = gate_up(s, line, rows, wg, wu)
     s.run()
     wd, one.mid = w_down_h.value, line.out.value
     two.attn, two.resid, two.resid_b, two.factor = (h.value for h in ends)
     one.gate, one.up, one.act = (h.value for h in inner)
 
-    s = Slot("slot4", 4)
+    s = Slot("slot4", 4, 160.0, 80.0)
     line = Line(s, rows, width, gather=two.resid_b, scatter=True)
     ends = mlp_finish(s, line, rows, width, one.resid, one.cot, mlp_gain)
-    produce(s, line, [s.load(one.act)], [wd], (ff, 512), col_block, dot_nn, 1.8)
+    produce(s, line, [s.load(one.act)], [[wd]], (ff, 512), col_block, dot_nn, 1.8)
     inner = gate_up(s, line, rows, wg, wu)
     s.run()
     two.mid = line.out.value
     one.out, one.g_mlp_b, one.g_mlp_gain = (h.value for h in ends)
     two.gate, two.up, two.act = (h.value for h in inner)
 
-    s = Slot("slot5", 5)
+    s = Slot("slot5", 5, 250.0, 80.0)
     line = Line(s, rows, width, gather=one.g_mlp_b, scatter=True)
     ends = mlp_finish(s, line, rows, width, two.resid, two.cot, mlp_gain)
-    produce(s, line, [s.load(two.act)], [wd], (ff, 512), col_block, dot_nn, 1.8)
+    produce(s, line, [s.load(two.act)], [[wd]], (ff, 512), col_block, dot_nn, 1.8)
     inner = act_back(s, line, rows, wd, one.gate, one.up)
     s.run()
     one.g_mlp = line.out.value
@@ -1826,7 +1922,7 @@
     s = Slot("slot6", 6)
     line = Line(s, rows, width, gather=two.g_mlp_b, scatter=True)
     ends = resid_finish(s, line, rows, width, one.cot, one.attn, one.factor, attn_gain)
-    produce(s, line, [s.load(one.g_gate), s.load(one.g_up)], wg + wu, (512, 512), row_block, dot_nt, 4.4)
+    produce(s, line, [s.load(one.g_gate), s.load(one.g_up)], [wg, wu], (512, ff), row_block, dot_nt, 3.4)
     inner = act_back(s, line, rows, wd, two.gate, two.up)
     s.run()
     two.g_mlp = line.out.value
@@ -1836,12 +1932,13 @@
     s = Slot("slot7", 7)
     line = Line(s, rows, width, gather=one.g_attn_b, scatter=True)
     plane = Plane(s)
-    g_down = s.hbm_out(w_down.shape, F32)
+    g_down = s.hbm_out((ff - 512, w_down.shape[1]), F32)
     ends = resid_finish(s, line, rows, width, two.cot, two.attn, two.factor, attn_gain)
-    produce(s, line, [s.load(two.g_gate), s.load(two.g_up)], wg + wu, (512, 512), row_block, dot_nt, 4.4)
-    mask = Mask(s, seg_all, seg_cols, 0, count)
+    acts, g_mlps = joined(s, (one.act, two.act)), joined(s, (one.g_mlp, two.g_mlp))
+    full_grad(s, plane, acts, g_mlps, False, g_down, (12.0, 23.0, 28.0), "d", (0, 1, 2), ("part0", "part1", "part1"))
+    produce(s, line, [s.load(two.g_gate), s.load(two.g_up)], [wg, wu], (512, ff), row_block, dot_nt, 3.4)
+    mask = Mask(s, seg_all, seg_cols, 0, count, True)
     back = attend_back(s, line, one.kvs, one.q, one.heads, one.logsum, mask, rows, width, wo)
-    wide_grad(s, plane, (one.act, two.act), (one.g_mlp, two.g_mlp), g_down, (22.0, 27.0, 31.0, 36.0), "d")
     s.run()
     one.g_attn = line.out.value
     two.g_resid, two.g_attn_b, two.g_attn_gain = (h.value for h in ends)
@@ -1853,9 +1950,10 @@
     g_kv = plane.scatter(one.g_kv, 0, False, 4, done="kv")
     g_gate = s.hbm_out(w_gate.shape, F32)
     raws = project_back(s, "kv", one.g_q, g_kv, (one.q_raw, one.k_raw), one.qk_factor, norms, cosine, sine, 0, rows, width)
-    mask = Mask(s, seg_all, seg_cols, per, count)
+    mids, g_gates = joined(s, (one.mid, two.mid)), joined(s, (one.g_gate, two.g_gate))
+    full_grad(s, plane, mids, g_gates, True, g_gate, (7.0, 11.0, 15.0, 19.0), "g")
+    mask = Mask(s, seg_all, seg_cols, per, count, True)
     back = attend_back(s, line, two.kvs, two.q, two.heads, two.logsum, mask, rows, width, wo)
-    tall_grad(s, plane, (one.mid, two.mid), (one.g_gate, two.g_gate), g_gate, (8.0, 13.0, 18.0, 22.0), "g")
     s.run()
     two.g_attn = line.out.value
     one.g_qr, one.g_kr, one.g_vr, one.g_q_gain, one.g_k_gain = (h.value for h in raws)
@@ -1867,9 +1965,10 @@
     g_kv = plane.scatter(two.g_kv, 0, False, 4, done="kv")
     g_up = s.hbm_out(w_up.shape, F32)
     fin_one = last_finish(s, line, rows, width, one.g_resid)[0]
-    produce(s, line, [s.load(g) for g in (one.g_qr, one.g_kr, one.g_vr)], [wq, wk, wv], (512, width), row_block, dot_nt, 1.6)
     raws = project_back(s, "kv", two.g_q, g_kv, (two.q_raw, two.k_raw), two.qk_factor, norms, cosine, sine, rows, rows, width)
-    tall_grad(s, plane, (one.mid, two.mid), (one.g_up, two.g_up), g_up, (13.0, 18.0, 22.0, 27.0), "u")
+    produce(s, line, [s.load(g) for g in (one.g_qr, one.g_kr, one.g_vr)], [[wq], [wk], [wv]], (512, width), row_block, dot_nt, 1.6, "u0")
+    mids, g_ups = joined(s, (one.mid, two.mid)), joined(s, (one.g_up, two.g_up))
+    full_grad(s, plane, mids, g_ups, True, g_up, (7.0, 18.0, 22.0, 26.0), "u")
     s.run()
     two.g_qr, two.g_kr, two.g_vr, two.g_q_gain, two.g_k_gain = (h.value for h in raws)
 
@@ -1877,26 +1976,30 @@
     line = Line(s, rows, width, scatter=True)
     plane = Plane(s)
     fin_two = last_finish(s, line, rows, width, two.g_resid)[0]
-    produce(s, line, [s.load(g) for g in (two.g_qr, two.g_kr, two.g_vr)], [wq, wk, wv], (512, width), row_block, dot_nt, 1.6)
+    produce(s, line, [s.load(g) for g in (two.g_qr, two.g_kr, two.g_vr)], [[wq], [wk], [wv]], (512, width), row_block, dot_nt, 1.6, "d3")
     sums = gain_sums(
         s,
         (one.g_q_gain, two.g_q_gain, one.g_k_gain, two.g_k_gain)
         + (one.g_attn_gain, two.g_attn_gain, one.g_mlp_gain, two.g_mlp_gain),
     )
-    wides = (one.wide, two.wide)
     g_q, g_k, g_v = (s.hbm_out(w_query.shape, F32) for _ in range(3))
-    g_out = s.hbm_out(w_out.shape, F32)
-    tall_grad(s, plane, wides, (one.g_qr, two.g_qr), g_q, (13.0,), "q")
-    tall_grad(s, plane, wides, (one.g_kr, two.g_kr), g_k, (18.0,), "k")
-    tall_grad(s, plane, wides, (one.g_vr, two.g_vr), g_v, (22.0,), "v")
-    wide_grad(s, plane, (one.heads_b, two.heads_b), (one.g_attn, two.g_attn), g_out, (27.0,), "o")
+    g_out, g_last = s.hbm_out(w_out.shape, F32), s.hbm_out((512, w_down.shape[1]), F32)
+    acts, g_mlps = joined(s, (one.act, two.act)), joined(s, (one.g_mlp, two.g_mlp))
+    full_grad(s, plane, acts, g_mlps, False, g_last, (7.0,), "d", (3,))
+    wides = joined(s, (one.wide, two.wide))
+    full_grad(s, plane, wides, joined(s, (one.g_qr, two.g_qr)), True, g_q, (18.0,), "q")
+    full_grad(s, plane, wides, joined(s, (one.g_kr, two.g_kr)), True, g_k, (22.0,), "k")
+    full_grad(s, plane, wides, joined(s, (one.g_vr, two.g_vr)), True, g_v, (26.0,), "v")
+    heads_b, g_attns = joined(s, (one.heads_b, two.heads_b)), joined(s, (one.g_attn, two.g_attn))
+    full_grad(s, plane, heads_b, g_attns, False, g_out, (30.0,), "o")
     s.run()
     gains = [sums.value[k] for k in range(4)]
     shape = (per, count, width)
     return (
         jnp.concatenate([one.out.reshape(shape), two.out.reshape(shape)], axis=0),
         jnp.concatenate([fin_one.value.reshape(shape), fin_two.value.reshape(shape)], axis=0),
-        *(g.value for g in (g_q, g_k, g_v, g_out, g_gate, g_up, g_down)),
+        *(g.value for g in (g_q, g_k, g_v, g_out, g_gate, g_up)),
+        jnp.concatenate([g_down.value, g_last.value], axis=0),
         *gains,
     )
 

time: 752 us -> 713 us (0.948)
  Pallas kernels: 724 us -> 682 us
    pallas_call x11, Pallas kernels: 724 us -> 682 us  [run(): pl.pallas_call(self.kernel, out_shape=tuple((o for o, _ in self.outputs))...]
where the time goes in v4:
time: 713 us; the launch traced here: 704 us
  Pallas kernels  682 us (96%)
  local copies, waits for them, and re-layouts  15.4 us (2%)
    pallas_call x11, Pallas kernels, run(): pl.pallas_call(self.kernel, out_shape=tuple((o for o, _ in self.outputs))...  682 us

profile of v4, /device:TPU:0, one launch (start us, length us, event | category | flops | bytes accessed | tf_op | source)
XLA Modules:
  0.0 703.8 jit_solution(10737570424180360523)
XLA Ops:
  0.6 0.0 copy-start.3
  0.7 0.6 maximum_bitcast_fusion.refs_9_
  1.3 0.7 copy.28
  1.9 0.7 copy.29
  2.6 1.3 concatenate.15.refs_1_
  3.9 1.0 broadcast_in_dim.18.refs_6_.refs_9_.refs_20_.refs_15_
  4.9 1.0 broadcast_in_dim.16.refs_8_
  5.9 2.2 fusion.1
  8.1 0.0 copy-done.3
  8.1 1.0 fusion
  9.2 68.3 %slot0.1 = (bf16[512,2048]{1,0:T(8,128)(2,1)}, s32[32,256]{1,0:T(8,128)}, bf16[2048,512]{1,0:T(8,128)(2,1)}, bf16[2048,512]{1,0:T(8,128)(2,1)}, bf16[2048,512]{1...) custom-call(bf16[512,512]{1,0:T(8,128)(2,1)} %bitcast.28, ...), custom_call_target="tpu_custom_call" | custom-call | tf_op jit(solution)/shard_map/slot0/pallas_call | solution.py:549
  77.5 61.6 %slot1.1 = (bf16[512,2048]{1,0:T(8,128)(2,1)}, bf16[2048,1024]{1,0:T(8,128)(2,1)}, bf16[2048,512]{1,0:T(8,128)(2,1)}, bf16[2048,512]{1,0:T(8,128)(2,1)}, bf16[20...) custom-call(bf16[512,512]{1,0:T(8,128)(2,1)} %bitcast.26, ...), custom_call_target="tpu_custom_call" | custom-call | tf_op jit(solution)/shard_map/slot1/pallas_call | solution.py:549
  139.1 55.6 %slot2.1 = (bf16[2048,1024]{1,0:T(8,128)(2,1)}, bf16[2048,512]{1,0:T(8,128)(2,1)}, bf16[2048,512]{1,0:T(8,128)(2,1)}, bf16[2048,512]{1,0:T(8,128)(2,1)}, f32[512...) custom-call(bf16[512,1024]{1,0:T(8,128)(2,1)} %get-tuple-element.118, ...), custom_call_target="tpu_custom_call" | custom-call | tf_op jit(solution)/shard_map/slot2/pallas_call | solution.py:549
  194.8 59.3 %slot3.1 = (bf16[512,2048]{1,0:T(8,128)(2,1)}, bf16[2048,2048]{1,0:T(8,128)(2,1)}, f32[512,512]{1,0:T(8,128)}, f32[512,512]{1,0:T(8,128)}, bf16[512,512]{1,0:T(8...) custom-call(bf16[512,512]{1,0:T(8,128)(2,1)} %get-tuple-element.122., ...), custom_call_target="tpu_custom_call" | custom-call | tf_op jit(solution)/shard_map/slot3/pallas_call | solution.py:549
  254.1 57.3 %slot4.1 = (bf16[512,2048]{1,0:T(8,128)(2,1)}, bf16[512,512]{1,0:T(8,128)(2,1)}, bf16[512,512]{1,0:T(8,128)(2,1)}, f32[8,512]{1,0:T(8,128)}, bf16[512,2048]{1,0:...) custom-call(bf16[512,512]{1,0:T(8,128)(2,1)} %get-tuple-element.132.refs_0_, ...), custom_call_target="tpu_custom_call" | custom-call | tf_op jit(solution)/shard_map/slot4/pallas_call | solution.py:549
  311.4 56.2 %slot5.1 = (bf16[512,2048]{1,0:T(8,128)(2,1)}, bf16[512,512]{1,0:T(8,128)(2,1)}, bf16[512,512]{1,0:T(8,128)(2,1)}, f32[8,512]{1,0:T(8,128)}, bf16[512,2048]{1,0:T(8,128)(2,1)}, /*index=5*/bf16[512,2048]{1,0:T(8,128)(2,1)}) custom-call(bf16[512,512]{1,0:T(8,128)(2,1)} %get-tuple-element.137.refs_0_, f32[512,512]{1,0:T(8,128)} %get-tuple-element.138.refs_1_, ...), custom_call_target="tpu_custom_call" | custom-call | tf_op jit(solution)/shard_map/slot5/pallas_call | solution.py:549
  367.6 57.2 %slot6.1 = (bf16[512,2048]{1,0:T(8,128)(2,1)}, f32[512,512]{1,0:T(8,128)}, bf16[512,512]{1,0:T(8,128)(2,1)}, f32[8,512]{1,0:T(8,128)}, bf16[512,2048]{1,0:T(8,128)(2,1)}, /*index=5*/bf16[512,2048]{1,0:T(8,128)(2,1)}) custom-call(bf16[512,512]{1,0:T(8,128)(2,1)} %get-tuple-element.143.refs_0_, bf16[512,512]{1,0:T(8,128)(2,1)} %bitcast.25, ...), custom_call_target="tpu_custom_call" | custom-call | tf_op jit(solution)/shard_map/slot6/pallas_call | solution.py:549
  424.8 66.8 %slot7.1 = (bf16[512,2048]{1,0:T(8,128)(2,1)}, f32[1536,256]{1,0:T(8,128)}, f32[512,512]{1,0:T(8,128)}, bf16[512,512]{1,0:T(8,128)(2,1)}, f32[8,512]{1,0:T(8,128...) custom-call(bf16[512,512]{1,0:T(8,128)(2,1)} %get-tuple-element.150., ...), custom_call_target="tpu_custom_call" | custom-call | tf_op jit(solution)/shard_map/slot7/pallas_call | solution.py:549
  491.6 67.7 %slot8.1 = (bf16[512,2048]{1,0:T(8,128)(2,1)}, f32[512,1024]{1,0:T(8,128)}, f32[256,2048]{1,0:T(8,128)}, bf16[512,512]{1,0:T(8,128)(2,1)}, bf16[512,512]{1,0:T(8...) custom-call(bf16[512,512]{1,0:T(8,128)(2,1)} %get-tuple-element.160., ...), custom_call_target="tpu_custom_call" | custom-call | tf_op jit(solution)/shard_map/slot8/pallas_call | solution.py:549
  559.3 64.2 %slot9.1 = (f32[512,1024]{1,0:T(8,128)}, f32[256,2048]{1,0:T(8,128)}, bf16[512,512]{1,0:T(8,128)(2,1)}, bf16[512,512]{1,0:T(8,128)(2,1)}, bf16[512,512]{1,0:T(8,...) custom-call(bf16[2048,1024]{1,0:T(8,128)(2,1)} %get-tuple-element.17, ...), custom_call_target="tpu_custom_call" | custom-call | tf_op jit(solution)/shard_map/slot9/pallas_call | solution.py:549
  623.5 0.0 copy-start.8
  623.5 0.0 copy-start.9
  623.5 0.0 copy-start.10
  623.5 68.1 %slot10.1 = (bf16[512,512]{1,0:T(8,128)(2,1)}, f32[8,512]{1,0:T(8,128)}, f32[256,512]{1,0:T(8,128)}, f32[256,512]{1,0:T(8,128)}, f32[256,512]{1,0:T(8,128)}, /*i...) custom-call(f32[512,512]{1,0:T(8,128)} %get-tuple-element.181.refs_0, ...), custom_call_target="tpu_custom_call" | custom-call | tf_op jit(solution)/shard_map/slot10/pallas_call | solution.py:549
  691.6 0.0 copy-done.8
  691.6 0.0 copy-done.9
  691.6 0.0 copy-done.10
  691.7 0.0 copy-start.12
  691.7 0.0 copy-start.2
  691.7 0.0 copy-start.11
  691.7 2.7 pad_maximum_fusion.1
  694.4 0.0 copy-done.12
  694.4 0.6 fusion.2
  695.0 0.0 copy-done.2
  695.0 0.0 copy-done.11
  695.0 0.0 copy-start.6
  695.0 0.0 copy-start.5
  695.0 1.5 pad_maximum_fusion
  696.5 0.0 copy-done.7
  696.5 0.8 copy.36
  697.3 0.0 copy-done.6
  697.3 0.8 copy.37
  698.1 0.0 copy-done.5
  698.1 0.8 copy.38
  698.9 0.8 copy.39
  699.7 1.3 copy.40
  701.0 1.0 copy-done.1
  702.0 1.3 copy.41
  (7 shorter events, 0.0 us)
Async XLA Ops:
  0.6 7.5 %copy-start.3 = (bf16[4,256,512]{2,1,0:T(8,128)(2,1)S(1)}, bf16[4,256,512]{2,1,0:T(8,128)(2,1)}, u32[]{:S(2)}) copy-start(bf16[4,256,512]{2,1,0:T(8,128)(2,1)} %param.16) | copy-start | bytes 3145732
  623.5 68.2 %copy-start.8 = (bf16[512,512]{1,0:T(8,128)(2,1)S(1)}, bf16[512,512]{1,0:T(8,128)(2,1)}, u32[]{:S(2)}) copy-start(bf16[512,512]{1,0:T(8,128)(2,1)} %get-tuple-element.136) | copy-start | bytes 1572868
  623.5 68.2 %copy-start.9 = (bf16[512,512]{1,0:T(8,128)(2,1)S(1)}, bf16[512,512]{1,0:T(8,128)(2,1)}, u32[]{:S(2)}) copy-start(bf16[512,512]{1,0:T(8,128)(2,1)} %get-tuple-element.142) | copy-start | bytes 1572868
  623.5 68.2 %copy-start.10 = (bf16[512,512]{1,0:T(8,128)(2,1)S(1)}, bf16[512,512]{1,0:T(8,128)(2,1)}, u32[]{:S(2)}) copy-start(bf16[512,512]{1,0:T(8,128)(2,1)} %get-tuple-element.180) | copy-start | bytes 1572868
  691.7 2.7 copy-start.12
  691.7 3.3 copy-start.2
  691.7 3.3 copy-start.11
  695.0 1.5 copy-start.7
  695.0 2.3 copy-start.6
  695.0 3.1 copy-start.5
  696.5 2.4 copy-start.4
  696.5 3.2 copy-start
  699.7 2.3 copy-start.1

commit v5 on v4

--- a/solution.py
+++ b/solution.py
@@ -386,10 +386,17 @@
     waited = False
     lazy = False
     halves = False
+    cut = None
     value = None
 
     def __init__(self, shape=None, dtype=None):
         self.shape, self.dtype = shape, dtype
+
+
+class Rows:
+    def __init__(self, array, first, count):
+        self.array, self.first = array, first
+        self.shape, self.dtype = (count,) + array.shape[1:], array.dtype
 
 
 class Slot:
@@ -416,6 +423,9 @@
         if isinstance(array, Handle):
             return array
         handle = Handle(array.shape, array.dtype)
+        if isinstance(array, Rows):
+            handle.cut = pl.ds(array.first, array.shape[0])
+            array = array.array
         self.inputs.append((array, handle))
         return handle
 
@@ -492,6 +502,8 @@
         for group in (self.inputs, self.outputs, self.scratch):
             for _, handle in group:
                 handle.ref = refs.pop(0)
+                if handle.cut is not None:
+                    handle.ref = handle.ref.at[handle.cut]
         self.sem_ref = refs.pop(0)
         self.flags, self.now = {flag: True for flag in self.early}, 0.0
         for handle in self.loads:
@@ -794,12 +806,13 @@
 def produce(slot, line, lefts, groups, shape, where, dot, cost, gate=None):
     order = (3, 0, 2, 1)
     weights = Weights(slot, groups, shape, order, where)
+    lefts = [h.held if hasattr(h, "held") else h for h in lefts]
 
     def body():
         weights.start(0)
         if gate is not None:
             yield ("flag", gate)
-        slot.need(*lefts)
+        slot.need(*[h for h in lefts if hasattr(h, "source")])
         half = line.rows // 2
         for k, c in enumerate(order):
             if k < 3:
@@ -1153,33 +1166,32 @@
     raws = [slot.store((rows, width), F32) for _ in (0, 1)]
     query, kv = slot.store((rows, width), BF), slot.store((rows, 2 * width), BF)
     factor = slot.store((rows, 128), F32)
+    value = slot.vmem((rows, width), F32)
     half = rows // 2
+
+    def products():
+        for j in range(3):
+            if flags is not None:
+                yield ("flag", flags[j])
+            slot.fetch(stages[j])
+        for k in range(4):
+            yield ("flag", "chunk%d" % k)
+            slot.need(*stages)
+            chunk = line.chunk(k)
+            block = pl.ds(pl.multiple_of(chunk * width, width), width)
+            for j, acc in enumerate((raws[0], raws[1], value)):
+                term = dot_nn(line.wide.ref[chunk], stages[j].ref[block])
+                acc.ref[...] = term if k == 0 else acc.ref[...] + term
+                yield ("did", 0.6)
+        slot.mark("products")
+
+    slot.add(products)
 
     def make(h):
         totals = RowTotals(slot, half)
 
         def body():
-            part = pl.ds(h * half, half)
-            if h == 0:
-                for j in range(3):
-                    if flags is not None:
-                        yield ("flag", flags[j])
-                    slot.fetch(stages[j])
-                yield ("flag", "chunk3")
-            else:
-                yield ("flag", "stages")
-            wide = line.wide.ref
-            for j in range(3):
-                slot.need(stages[j])
-                weight = stages[j].ref
-                value = dot_nn(wide[0, part], weight[0:width])
-                for c in (1, 2, 3):
-                    value = value + dot_nn(wide[c, part], weight[c * width : (c + 1) * width])
-                if j < 2:
-                    raws[j].ref[part] = value
-                else:
-                    kv.ref[part, width : 2 * width] = value.astype(BF)
-                yield ("did", 1.1)
+            yield ("flag", "products")
 
             def first(part, here):
                 q, k = raws[0].ref[part], raws[1].ref[part]
@@ -1187,8 +1199,7 @@
 
             tiled_at(h * half, half, 32, first, 0)
             slot.flush_half(h, *raws)
-            if h == 0:
-                slot.mark("stages")
+            yield ("did", 0.7)
             yield from totals.exchange()
             yield ("flag", "tables")
             slot.need(*gains)
@@ -1202,8 +1213,9 @@
                 co, si = cosine.ref[trig], sine.ref[trig]
                 for j, target in ((0, query), (1, kv)):
                     for n in range(width // HEAD_DIM):
-                        value = raws[j].ref[part, head_cols(n)] * scales[j] * gains[j].ref[:, head_cols(n)]
-                        target.ref[part, head_cols(n)] = (value * co + half_turn(value) * si).astype(BF)
+                        turned = raws[j].ref[part, head_cols(n)] * scales[j] * gains[j].ref[:, head_cols(n)]
+                        target.ref[part, head_cols(n)] = (turned * co + half_turn(turned) * si).astype(BF)
+                kv.ref[part, width : 2 * width] = value.ref[part].astype(BF)
 
             tiled_at(h * half, half, 32, second, 0)
             slot.flush_half(h, kv, query, factor)
@@ -1334,16 +1346,18 @@
             vcols = pl.ds(pl.multiple_of(width + h * HEAD_DIM, HEAD_DIM), HEAD_DIM)
             q, g = query.ref[mine, cols], grad.ref[mine, cols]
             logs, delta = rows_of.ref[0, pl.ds(h, 1)], rows_of.ref[1, pl.ds(h, 1)]
+            there = [pl.ds(c * rows + s * count, count) for c in range(4)]
+            values = [dot_nt(kv.ref[t, cols], q) for t in there]
+            slopes = [dot_nt(kv.ref[t, vcols], g) for t in there]
+            probs = [
+                jnp.exp(v * scale + mask.mask.ref[pl.ds(c * count, count)] - logs) for c, v in enumerate(values)
+            ]
+            slopes = [(p * (v - delta)).astype(BF) for p, v in zip(probs, slopes)]
             total = jnp.zeros((count, HEAD_DIM), F32)
-            for c in range(4):
-                there = pl.ds(c * rows + s * count, count)
-                keys, vals = kv.ref[there, cols], kv.ref[there, vcols]
-                value = dot_nt(keys, q) * scale + mask.mask.ref[pl.ds(c * count, count)]
-                probs = jnp.exp(value - logs)
-                slopes = (probs * (dot_nt(vals, g) - delta)).astype(BF)
-                total = total + dot_tn(slopes, keys)
-                g_kv.ref[there, cols] = (dot_nn(slopes, q) * scale).astype(BF)
-                g_kv.ref[there, vcols] = dot_nn(probs.astype(BF), g).astype(BF)
+            for t, p, v in zip(there, probs, slopes):
+                total = total + dot_tn(v, kv.ref[t, cols])
+                g_kv.ref[t, cols] = (dot_nn(v, q) * scale).astype(BF)
+                g_kv.ref[t, vcols] = dot_nn(p.astype(BF), g).astype(BF)
             g_query.ref[mine, cols] = total * scale
 
     consume(slot, line, ((w_out,),), (width, width), col_block, last, multiply, 1, 0.7)
@@ -1361,6 +1375,7 @@
     gains = [slot.load(g.reshape(1, width)) for g in gains]
     cosine, sine = slot.load(cosine), slot.load(sine)
     outs = [slot.store((rows, width), BF) for _ in range(3)]
+    ended = []
     gain_grads = [slot.store((8, width), F32) for _ in range(2)]
     half = rows // 2
     left = []
@@ -1372,14 +1387,15 @@
             yield ("flag", flag)
             if h == 0:
                 left[:] = [0, 1]
+                ended[:] = [0, 1]
                 slot.fetch(g_kv)
                 for g in gain_grads:
                     g.ref[...] = jnp.zeros((8, width), F32)
                 slot.need(g_query, factor, cosine, sine, *raws, *gains)
                 slot.need(g_kv)
-                slot.mark("grads")
+                slot.mark(flag + "_in")
             else:
-                yield ("flag", "grads")
+                yield ("flag", flag + "_in")
 
             def first(part, here):
                 trig = pl.ds(pl.multiple_of(first_row + h * half + here.start, 32), 32)
@@ -1416,12 +1432,17 @@
 
             tiled_at(h * half, half, 32, second, 0)
             slot.flush_half(h, *outs)
+            ended.remove(h)
+            if not ended:
+                slot.mark(flag + "_done")
             yield ("did", 1.5)
 
         slot.add(body)
 
     make(0)
     make(1)
+    for out in outs:
+        out.target.held = out
     return [h.target for h in outs + gain_grads]
 
 
@@ -1825,8 +1846,8 @@
     batches = (Batch(), Batch())
     one, two = batches
     for b, batch in enumerate(batches):
-        batch.x = hidden[b * per : (b + 1) * per].reshape(rows, width)
-        batch.cot = cotangent[b * per : (b + 1) * per].reshape(rows, width)
+        batch.x = Rows(hidden.reshape(seqs * count, width), b * rows, rows)
+        batch.cot = Rows(cotangent.reshape(seqs * count, width), b * rows, rows)
     seg_cols = jnp.broadcast_to(segments.reshape(seqs * count, 1), (seqs * count, 128))
     pos_cols = jnp.broadcast_to(positions.reshape(seqs * count, 1), (seqs * count, 128))
     half = HEAD_DIM // 2
@@ -1839,7 +1860,7 @@
     quarters = [(512 * k, 512) for k in range(ff // 512)]
     wg, wu = [], []
 
-    s = Slot("slot0", 0)
+    s = Slot("slot0", 0, 97.0, 48.0)
     line = Line(s, rows, width, gather=one.x)
     plane = Plane(s)
     seg_h = plane.gather(seg_pad, 0, False)
@@ -1855,7 +1876,7 @@
     one.q_raw, one.k_raw, one.q, one.kv, one.qk_factor = (h.value for h in made)
     one.wide = line.out.value
 
-    s = Slot("slot1", 1)
+    s = Slot("slot1", 1, 85.0, 42.0)
     line = Line(s, rows, width, gather=two.x)
     plane = Plane(s)
     kvs = plane.gather(one.kv, 0, False, 4, done="kv")
@@ -1873,7 +1894,7 @@
     one.heads, one.heads_b, one.logsum = (h.value for h in felt)
     two.wide = line.out.value
 
-    s = Slot("slot2", 2, 160.0, 80.0)
+    s = Slot("slot2", 2, 130.0, 60.0)
     line = Line(s, rows, width, scatter=True)
     plane = Plane(s)
     kvs = plane.gather(two.kv, 0, False, 4, done="kv")
@@ -1899,7 +1920,7 @@
     two.attn, two.resid, two.resid_b, two.factor = (h.value for h in ends)
     one.gate, one.up, one.act = (h.value for h in inner)
 
-    s = Slot("slot4", 4, 160.0, 80.0)
+    s = Slot("slot4", 4, 130.0, 60.0)
     line = Line(s, rows, width, gather=two.resid_b, scatter=True)
     ends = mlp_finish(s, line, rows, width, one.resid, one.cot, mlp_gain)
     produce(s, line, [s.load(one.act)], [[wd]], (ff, 512), col_block, dot_nn, 1.8)
@@ -1909,7 +1930,7 @@
     one.out, one.g_mlp_b, one.g_mlp_gain = (h.value for h in ends)
     two.gate, two.up, two.act = (h.value for h in inner)
 
-    s = Slot("slot5", 5, 250.0, 80.0)
+    s = Slot("slot5", 5, 130.0, 60.0)
     line = Line(s, rows, width, gather=one.g_mlp_b, scatter=True)
     ends = mlp_finish(s, line, rows, width, two.resid, two.cot, mlp_gain)
     produce(s, line, [s.load(two.act)], [[wd]], (ff, 512), col_block, dot_nn, 1.8)
@@ -1919,7 +1940,7 @@
     two.out, two.g_mlp_b, two.g_mlp_gain = (h.value for h in ends)
     one.g_gate, one.g_up = (h.value for h in inner)
 
-    s = Slot("slot6", 6)
+    s = Slot("slot6", 6, 130.0, 60.0)
     line = Line(s, rows, width, gather=two.g_mlp_b, scatter=True)
     ends = resid_finish(s, line, rows, width, one.cot, one.attn, one.factor, attn_gain)
     produce(s, line, [s.load(one.g_gate), s.load(one.g_up)], [wg, wu], (512, ff), row_block, dot_nt, 3.4)
@@ -1929,7 +1950,7 @@
     one.g_resid, one.g_attn_b, one.g_attn_gain = (h.value for h in ends)
     two.g_gate, two.g_up = (h.value for h in inner)
 
-    s = Slot("slot7", 7)
+    s = Slot("slot7", 7, 97.0, 48.0)
     line = Line(s, rows, width, gather=one.g_attn_b, scatter=True)
     plane = Plane(s)
     g_down = s.hbm_out((ff - 512, w_down.shape[1]), F32)
@@ -1944,7 +1965,7 @@
     two.g_resid, two.g_attn_b, two.g_attn_gain = (h.value for h in ends)
     one.g_q, one.g_kv = (h.value for h in back)
 
-    s = Slot("slot8", 8)
+    s = Slot("slot8", 8, 92.0, 46.0)
     line = Line(s, rows, width, gather=two.g_attn_b)
     plane = Plane(s)
     g_kv = plane.scatter(one.g_kv, 0, False, 4, done="kv")
@@ -1959,7 +1980,7 @@
     one.g_qr, one.g_kr, one.g_vr, one.g_q_gain, one.g_k_gain = (h.value for h in raws)
     two.g_q, two.g_kv = (h.value for h in back)
 
-    s = Slot("slot9", 9)
+    s = Slot("slot9", 9, 75.0, 38.0)
     line = Line(s, rows, width, scatter=True)
     plane = Plane(s)
     g_kv = plane.scatter(two.g_kv, 0, False, 4, done="kv")
@@ -1972,7 +1993,7 @@
     s.run()
     two.g_qr, two.g_kr, two.g_vr, two.g_q_gain, two.g_k_gain = (h.value for h in raws)
 
-    s = Slot("slot10", 10)
+    s = Slot("slot10", 10, 75.0, 38.0)
     line = Line(s, rows, width, scatter=True)
     plane = Plane(s)
     fin_two = last_finish(s, line, rows, width, two.g_resid)[0]

time: 713 us -> 694 us (0.973)
  Pallas kernels: 682 us -> 667 us
    pallas_call x11, Pallas kernels: 682 us -> 667 us  [run(): pl.pallas_call(self.kernel, out_shape=tuple((o for o, _ in self.outputs))...]
where the time goes in v5:
time: 694 us; the launch traced here: 685 us
  Pallas kernels  667 us (96%)
  local copies, waits for them, and re-layouts  12.1 us (2%)
    pallas_call x11, Pallas kernels, run(): pl.pallas_call(self.kernel, out_shape=tuple((o for o, _ in self.outputs))...  667 us

profile of v5, /device:TPU:0, one launch (start us, length us, event | category | flops | bytes accessed | tf_op | source)
XLA Modules:
  0.0 684.9 jit_solution(6853006853846962533)
XLA Ops:
  0.7 0.6 maximum_bitcast_fusion.refs_9_
  1.2 0.7 copy.28
  1.9 0.7 copy.29
  2.6 1.3 concatenate.15.refs_1_
  3.9 1.0 broadcast_in_dim.18.refs_6_.refs_9_.refs_20_.refs_15_
  4.9 1.0 broadcast_in_dim.16.refs_8_
  5.9 67.7 %slot0.1 = (bf16[512,2048]{1,0:T(8,128)(2,1)}, s32[32,256]{1,0:T(8,128)}, bf16[2048,512]{1,0:T(8,128)(2,1)}, bf16[2048,512]{1,0:T(8,128)(2,1)}, bf16[2048,512]{1...) custom-call(bf16[1024,512]{1,0:T(8,128)(2,1)} %bitcast.20, ...), custom_call_target="tpu_custom_call" | custom-call | tf_op jit(solution)/shard_map/slot0/pallas_call | solution.py:561
  73.6 57.7 %slot1.1 = (bf16[512,2048]{1,0:T(8,128)(2,1)}, bf16[2048,1024]{1,0:T(8,128)(2,1)}, bf16[2048,512]{1,0:T(8,128)(2,1)}, bf16[2048,512]{1,0:T(8,128)(2,1)}, bf16[20...) custom-call(bf16[1024,512]{1,0:T(8,128)(2,1)} %bitcast.21, ...), custom_call_target="tpu_custom_call" | custom-call | tf_op jit(solution)/shard_map/slot1/pallas_call | solution.py:561
  131.3 53.6 %slot2.1 = (bf16[2048,1024]{1,0:T(8,128)(2,1)}, bf16[2048,512]{1,0:T(8,128)(2,1)}, bf16[2048,512]{1,0:T(8,128)(2,1)}, bf16[2048,512]{1,0:T(8,128)(2,1)}, f32[512...) custom-call(bf16[512,1024]{1,0:T(8,128)(2,1)} %get-tuple-element.118, ...), custom_call_target="tpu_custom_call" | custom-call | tf_op jit(solution)/shard_map/slot2/pallas_call | solution.py:561
  184.9 59.6 %slot3.1 = (bf16[512,2048]{1,0:T(8,128)(2,1)}, bf16[2048,2048]{1,0:T(8,128)(2,1)}, f32[512,512]{1,0:T(8,128)}, f32[512,512]{1,0:T(8,128)}, bf16[512,512]{1,0:T(8...) custom-call(bf16[512,512]{1,0:T(8,128)(2,1)} %get-tuple-element.122., ...), custom_call_target="tpu_custom_call" | custom-call | tf_op jit(solution)/shard_map/slot3/pallas_call | solution.py:561
  244.5 57.9 %slot4.1 = (bf16[512,2048]{1,0:T(8,128)(2,1)}, bf16[512,512]{1,0:T(8,128)(2,1)}, bf16[512,512]{1,0:T(8,128)(2,1)}, f32[8,512]{1,0:T(8,128)}, bf16[512,2048]{1,0:...) custom-call(bf16[512,512]{1,0:T(8,128)(2,1)} %get-tuple-element.132.refs_0_, ...), custom_call_target="tpu_custom_call" | custom-call | tf_op jit(solution)/shard_map/slot4/pallas_call | solution.py:561
  302.4 56.1 %slot5.1 = (bf16[512,2048]{1,0:T(8,128)(2,1)}, bf16[512,512]{1,0:T(8,128)(2,1)}, bf16[512,512]{1,0:T(8,128)(2,1)}, f32[8,512]{1,0:T(8,128)}, bf16[512,2048]{1,0:T(8,128)(2,1)}, /*index=5*/bf16[512,2048]{1,0:T(8,128)(2,1)}) custom-call(bf16[512,512]{1,0:T(8,128)(2,1)} %get-tuple-element.137.refs_0_, f32[512,512]{1,0:T(8,128)} %get-tuple-element.138.refs_1_, ...), custom_call_target="tpu_custom_call" | custom-call | tf_op jit(solution)/shard_map/slot5/pallas_call | solution.py:561
  358.4 55.6 %slot6.1 = (bf16[512,2048]{1,0:T(8,128)(2,1)}, f32[512,512]{1,0:T(8,128)}, bf16[512,512]{1,0:T(8,128)(2,1)}, f32[8,512]{1,0:T(8,128)}, bf16[512,2048]{1,0:T(8,128)(2,1)}, /*index=5*/bf16[512,2048]{1,0:T(8,128)(2,1)}) custom-call(bf16[512,512]{1,0:T(8,128)(2,1)} %get-tuple-element.143.refs_0_, bf16[1024,512]{1,0:T(8,128)(2,1)} %bitcast.26, ...), custom_call_target="tpu_custom_call" | custom-call | tf_op jit(solution)/shard_map/slot6/pallas_call | solution.py:561
  414.0 64.3 %slot7.1 = (bf16[512,2048]{1,0:T(8,128)(2,1)}, f32[1536,256]{1,0:T(8,128)}, f32[512,512]{1,0:T(8,128)}, bf16[512,512]{1,0:T(8,128)(2,1)}, f32[8,512]{1,0:T(8,128...) custom-call(bf16[512,512]{1,0:T(8,128)(2,1)} %get-tuple-element.150., ...), custom_call_target="tpu_custom_call" | custom-call | tf_op jit(solution)/shard_map/slot7/pallas_call | solution.py:561
  478.3 65.8 %slot8.1 = (bf16[512,2048]{1,0:T(8,128)(2,1)}, f32[512,1024]{1,0:T(8,128)}, f32[256,2048]{1,0:T(8,128)}, bf16[512,512]{1,0:T(8,128)(2,1)}, bf16[512,512]{1,0:T(8...) custom-call(bf16[512,512]{1,0:T(8,128)(2,1)} %get-tuple-element.160., ...), custom_call_target="tpu_custom_call" | custom-call | tf_op jit(solution)/shard_map/slot8/pallas_call | solution.py:561
  544.1 63.0 %slot9.1 = (f32[512,1024]{1,0:T(8,128)}, f32[256,2048]{1,0:T(8,128)}, bf16[512,512]{1,0:T(8,128)(2,1)}, bf16[512,512]{1,0:T(8,128)(2,1)}, bf16[512,512]{1,0:T(8,...) custom-call(bf16[2048,1024]{1,0:T(8,128)(2,1)} %get-tuple-element.17, ...), custom_call_target="tpu_custom_call" | custom-call | tf_op jit(solution)/shard_map/slot9/pallas_call | solution.py:561
  607.1 0.0 copy-start.7
  607.1 0.0 copy-start.8
  607.1 0.0 copy-start.9
  607.1 65.6 %slot10.1 = (bf16[512,512]{1,0:T(8,128)(2,1)}, f32[8,512]{1,0:T(8,128)}, f32[256,512]{1,0:T(8,128)}, f32[256,512]{1,0:T(8,128)}, f32[256,512]{1,0:T(8,128)}, /*i...) custom-call(f32[512,512]{1,0:T(8,128)} %get-tuple-element.181.refs_0, ...), custom_call_target="tpu_custom_call" | custom-call | tf_op jit(solution)/shard_map/slot10/pallas_call | solution.py:561
  672.7 0.0 copy-done.7
  672.8 0.0 copy-done.8
  672.8 0.0 copy-done.9
  672.8 0.0 copy-start.11
  672.8 0.0 copy-start.2
  672.8 0.0 copy-start.10
  672.8 2.7 pad_maximum_fusion.1
  675.5 0.0 copy-done.11
  675.5 0.6 fusion
  676.1 0.0 copy-done.2
  676.1 0.0 copy-done.10
  676.1 0.0 copy-start.5
  676.1 0.0 copy-start.4
  676.1 1.5 pad_maximum_fusion
  677.6 0.0 copy-done.6
  677.6 0.0 copy-start.3
  677.6 0.0 copy-start
  677.6 0.8 copy.36
  678.4 0.0 copy-done.5
  678.4 0.8 copy.37
  679.2 0.0 copy-done.4
  679.2 0.8 copy.38
  680.0 0.0 copy-done.3
  680.0 0.8 copy.39
  680.8 0.0 copy-done
  680.8 1.3 copy.40
  682.1 1.0 copy-done.1
  683.1 1.3 copy.41
  (3 shorter events, 0.0 us)
Async XLA Ops:
  607.1 65.7 %copy-start.7 = (bf16[512,512]{1,0:T(8,128)(2,1)S(1)}, bf16[512,512]{1,0:T(8,128)(2,1)}, u32[]{:S(2)}) copy-start(bf16[512,512]{1,0:T(8,128)(2,1)} %get-tuple-element.136) | copy-start | bytes 1572868
  607.1 65.7 %copy-start.8 = (bf16[512,512]{1,0:T(8,128)(2,1)S(1)}, bf16[512,512]{1,0:T(8,128)(2,1)}, u32[]{:S(2)}) copy-start(bf16[512,512]{1,0:T(8,128)(2,1)} %get-tuple-element.142) | copy-start | bytes 1572868
  607.1 65.7 %copy-start.9 = (bf16[512,512]{1,0:T(8,128)(2,1)S(1)}, bf16[512,512]{1,0:T(8,128)(2,1)}, u32[]{:S(2)}) copy-start(bf16[512,512]{1,0:T(8,128)(2,1)} %get-tuple-element.180) | copy-start | bytes 1572868
  672.8 2.7 copy-start.11
  672.8 3.3 copy-start.2
  672.8 3.3 copy-start.10
  676.1 1.5 copy-start.6
  676.1 2.3 copy-start.5
  676.1 3.1 copy-start.4
  677.6 2.4 copy-start.3
  677.6 3.2 copy-start
  680.8 2.3 copy-start.1

commit v6 on v5

--- a/solution.py
+++ b/solution.py
@@ -1863,10 +1863,10 @@
     s = Slot("slot0", 0, 97.0, 48.0)
     line = Line(s, rows, width, gather=one.x)
     plane = Plane(s)
-    seg_h = plane.gather(seg_pad, 0, False)
     full = [plane.gather(w, 0, True, done="w%d" % i) for i, w in enumerate((w_query, w_key, w_value))]
     w_out_h = plane.gather(w_out, 1, True, 1, 12.0)
     some = [plane.gather(w_gate, 0, True, 1, t, cols=c) for t, c in zip((18.0, 26.0), quarters)]
+    seg_h = plane.gather(seg_pad, 0, False, 1, 20.0)
     cosine, sine = tables(s, pos_cols, freqs, sign)
     made = project(s, line, rows, width, full, ("w0", "w1", "w2"), norms, cosine, sine, 0)
     s.run()
@@ -1876,7 +1876,7 @@
     one.q_raw, one.k_raw, one.q, one.kv, one.qk_factor = (h.value for h in made)
     one.wide = line.out.value
 
-    s = Slot("slot1", 1, 85.0, 42.0)
+    s = Slot("slot1", 1, 92.0, 44.0)
     line = Line(s, rows, width, gather=two.x)
     plane = Plane(s)
     kvs = plane.gather(one.kv, 0, False, 4, done="kv")
@@ -1909,7 +1909,7 @@
     one.attn, one.resid, one.resid_b, one.factor = (h.value for h in ends)
     two.heads, two.heads_b, two.logsum = (h.value for h in felt)
 
-    s = Slot("slot3", 3, 200.0, 80.0)
+    s = Slot("slot3", 3, 160.0, 70.0)
     line = Line(s, rows, width, gather=one.resid_b, scatter=True)
     w_down_h = Plane(s).gather(w_down, 1, True, 4)
     ends = attn_finish(s, line, rows, width, two.x, attn_gain)
@@ -1920,7 +1920,7 @@
     two.attn, two.resid, two.resid_b, two.factor = (h.value for h in ends)
     one.gate, one.up, one.act = (h.value for h in inner)
 
-    s = Slot("slot4", 4, 130.0, 60.0)
+    s = Slot("slot4", 4, 160.0, 80.0)
     line = Line(s, rows, width, gather=two.resid_b, scatter=True)
     ends = mlp_finish(s, line, rows, width, one.resid, one.cot, mlp_gain)
     produce(s, line, [s.load(one.act)], [[wd]], (ff, 512), col_block, dot_nn, 1.8)
@@ -1980,16 +1980,16 @@
     one.g_qr, one.g_kr, one.g_vr, one.g_q_gain, one.g_k_gain = (h.value for h in raws)
     two.g_q, two.g_kv = (h.value for h in back)
 
-    s = Slot("slot9", 9, 75.0, 38.0)
+    s = Slot("slot9", 9, 80.0, 40.0)
     line = Line(s, rows, width, scatter=True)
     plane = Plane(s)
     g_kv = plane.scatter(two.g_kv, 0, False, 4, done="kv")
     g_up = s.hbm_out(w_up.shape, F32)
     fin_one = last_finish(s, line, rows, width, one.g_resid)[0]
     raws = project_back(s, "kv", two.g_q, g_kv, (two.q_raw, two.k_raw), two.qk_factor, norms, cosine, sine, rows, rows, width)
-    produce(s, line, [s.load(g) for g in (one.g_qr, one.g_kr, one.g_vr)], [[wq], [wk], [wv]], (512, width), row_block, dot_nt, 1.6, "u0")
+    produce(s, line, [s.load(g) for g in (one.g_qr, one.g_kr, one.g_vr)], [[wq], [wk], [wv]], (512, width), row_block, dot_nt, 1.6, "u1")
     mids, g_ups = joined(s, (one.mid, two.mid)), joined(s, (one.g_up, two.g_up))
-    full_grad(s, plane, mids, g_ups, True, g_up, (7.0, 18.0, 22.0, 26.0), "u")
+    full_grad(s, plane, mids, g_ups, True, g_up, (7.0, 11.0, 22.0, 26.0), "u")
     s.run()
     two.g_qr, two.g_kr, two.g_vr, two.g_q_gain, two.g_k_gain = (h.value for h in raws)
 

time: 694 us -> 689 us (level)
  no operation moved by 1% of the time
where the time goes in v6:
time: 689 us; the launch traced here: 680 us
  Pallas kernels  662 us (96%)
  local copies, waits for them, and re-layouts  12.1 us (2%)
    pallas_call x11, Pallas kernels, run(): pl.pallas_call(self.kernel, out_shape=tuple((o for o, _ in self.outputs))...  662 us

profile of v6, /device:TPU:0, one launch (start us, length us, event | category | flops | bytes accessed | tf_op | source)
XLA Modules:
  0.0 680.0 jit_solution(10754857717491230863)
XLA Ops:
  0.7 0.6 maximum_bitcast_fusion.refs_9_
  1.2 0.7 copy.28
  1.9 0.7 copy.29
  2.6 1.3 concatenate.15.refs_7_
  3.9 1.0 broadcast_in_dim.18.refs_6_.refs_9_.refs_20_.refs_15_
  4.9 1.0 broadcast_in_dim.16.refs_8_
  5.9 65.2 %slot0.1 = (bf16[512,2048]{1,0:T(8,128)(2,1)}, bf16[2048,512]{1,0:T(8,128)(2,1)}, bf16[2048,512]{1,0:T(8,128)(2,1)}, bf16[2048,512]{1,0:T(8,128)(2,1)}, bf16[512...) custom-call(bf16[1024,512]{1,0:T(8,128)(2,1)} %bitcast.20, ...), custom_call_target="tpu_custom_call" | custom-call | tf_op jit(solution)/shard_map/slot0/pallas_call | solution.py:561
  71.1 55.9 %slot1.1 = (bf16[512,2048]{1,0:T(8,128)(2,1)}, bf16[2048,1024]{1,0:T(8,128)(2,1)}, bf16[2048,512]{1,0:T(8,128)(2,1)}, bf16[2048,512]{1,0:T(8,128)(2,1)}, bf16[20...) custom-call(bf16[1024,512]{1,0:T(8,128)(2,1)} %bitcast.21, ...), custom_call_target="tpu_custom_call" | custom-call | tf_op jit(solution)/shard_map/slot1/pallas_call | solution.py:561
  127.0 54.6 %slot2.1 = (bf16[2048,1024]{1,0:T(8,128)(2,1)}, bf16[2048,512]{1,0:T(8,128)(2,1)}, bf16[2048,512]{1,0:T(8,128)(2,1)}, bf16[2048,512]{1,0:T(8,128)(2,1)}, f32[512...) custom-call(bf16[512,1024]{1,0:T(8,128)(2,1)} %get-tuple-element.118, ...), custom_call_target="tpu_custom_call" | custom-call | tf_op jit(solution)/shard_map/slot2/pallas_call | solution.py:561
  181.6 59.6 %slot3.1 = (bf16[512,2048]{1,0:T(8,128)(2,1)}, bf16[2048,2048]{1,0:T(8,128)(2,1)}, f32[512,512]{1,0:T(8,128)}, f32[512,512]{1,0:T(8,128)}, bf16[512,512]{1,0:T(8...) custom-call(bf16[512,512]{1,0:T(8,128)(2,1)} %get-tuple-element.122., ...), custom_call_target="tpu_custom_call" | custom-call | tf_op jit(solution)/shard_map/slot3/pallas_call | solution.py:561
  241.2 56.8 %slot4.1 = (bf16[512,2048]{1,0:T(8,128)(2,1)}, bf16[512,512]{1,0:T(8,128)(2,1)}, bf16[512,512]{1,0:T(8,128)(2,1)}, f32[8,512]{1,0:T(8,128)}, bf16[512,2048]{1,0:...) custom-call(bf16[512,512]{1,0:T(8,128)(2,1)} %get-tuple-element.132.refs_0_, ...), custom_call_target="tpu_custom_call" | custom-call | tf_op jit(solution)/shard_map/slot4/pallas_call | solution.py:561
  298.0 56.1 %slot5.1 = (bf16[512,2048]{1,0:T(8,128)(2,1)}, bf16[512,512]{1,0:T(8,128)(2,1)}, bf16[512,512]{1,0:T(8,128)(2,1)}, f32[8,512]{1,0:T(8,128)}, bf16[512,2048]{1,0:T(8,128)(2,1)}, /*index=5*/bf16[512,2048]{1,0:T(8,128)(2,1)}) custom-call(bf16[512,512]{1,0:T(8,128)(2,1)} %get-tuple-element.137.refs_0_, f32[512,512]{1,0:T(8,128)} %get-tuple-element.138.refs_1_, ...), custom_call_target="tpu_custom_call" | custom-call | tf_op jit(solution)/shard_map/slot5/pallas_call | solution.py:561
  354.2 55.5 %slot6.1 = (bf16[512,2048]{1,0:T(8,128)(2,1)}, f32[512,512]{1,0:T(8,128)}, bf16[512,512]{1,0:T(8,128)(2,1)}, f32[8,512]{1,0:T(8,128)}, bf16[512,2048]{1,0:T(8,128)(2,1)}, /*index=5*/bf16[512,2048]{1,0:T(8,128)(2,1)}) custom-call(bf16[512,512]{1,0:T(8,128)(2,1)} %get-tuple-element.143.refs_0_, bf16[1024,512]{1,0:T(8,128)(2,1)} %bitcast.26, ...), custom_call_target="tpu_custom_call" | custom-call | tf_op jit(solution)/shard_map/slot6/pallas_call | solution.py:561
  409.7 63.6 %slot7.1 = (bf16[512,2048]{1,0:T(8,128)(2,1)}, f32[1536,256]{1,0:T(8,128)}, f32[512,512]{1,0:T(8,128)}, bf16[512,512]{1,0:T(8,128)(2,1)}, f32[8,512]{1,0:T(8,128...) custom-call(bf16[512,512]{1,0:T(8,128)(2,1)} %get-tuple-element.150., ...), custom_call_target="tpu_custom_call" | custom-call | tf_op jit(solution)/shard_map/slot7/pallas_call | solution.py:561
  473.3 65.9 %slot8.1 = (bf16[512,2048]{1,0:T(8,128)(2,1)}, f32[512,1024]{1,0:T(8,128)}, f32[256,2048]{1,0:T(8,128)}, bf16[512,512]{1,0:T(8,128)(2,1)}, bf16[512,512]{1,0:T(8...) custom-call(bf16[512,512]{1,0:T(8,128)(2,1)} %get-tuple-element.160., ...), custom_call_target="tpu_custom_call" | custom-call | tf_op jit(solution)/shard_map/slot8/pallas_call | solution.py:561
  539.2 62.9 %slot9.1 = (f32[512,1024]{1,0:T(8,128)}, f32[256,2048]{1,0:T(8,128)}, bf16[512,512]{1,0:T(8,128)(2,1)}, bf16[512,512]{1,0:T(8,128)(2,1)}, bf16[512,512]{1,0:T(8,...) custom-call(bf16[2048,1024]{1,0:T(8,128)(2,1)} %get-tuple-element.17, ...), custom_call_target="tpu_custom_call" | custom-call | tf_op jit(solution)/shard_map/slot9/pallas_call | solution.py:561
  602.1 0.0 copy-start.7
  602.1 0.0 copy-start.8
  602.1 0.0 copy-start.9
  602.1 65.7 %slot10.1 = (bf16[512,512]{1,0:T(8,128)(2,1)}, f32[8,512]{1,0:T(8,128)}, f32[256,512]{1,0:T(8,128)}, f32[256,512]{1,0:T(8,128)}, f32[256,512]{1,0:T(8,128)}, /*i...) custom-call(f32[512,512]{1,0:T(8,128)} %get-tuple-element.181.refs_0, ...), custom_call_target="tpu_custom_call" | custom-call | tf_op jit(solution)/shard_map/slot10/pallas_call | solution.py:561
  667.9 0.0 copy-done.7
  667.9 0.0 copy-done.8
  667.9 0.0 copy-done.9
  667.9 0.0 copy-start.11
  667.9 0.0 copy-start.2
  667.9 0.0 copy-start.10
  667.9 2.7 pad_maximum_fusion.1
  670.6 0.0 copy-done.11
  670.6 0.6 fusion
  671.2 0.0 copy-done.2
  671.2 0.0 copy-done.10
  671.2 0.0 copy-start.6
  671.2 0.0 copy-start.5
  671.2 0.0 copy-start.4
  671.3 1.5 pad_maximum_fusion
  672.7 0.0 copy-done.6
  672.7 0.0 copy-start.3
  672.7 0.8 copy.36
  673.5 0.0 copy-done.5
  673.5 0.8 copy.37
  674.3 0.0 copy-done.4
  674.3 0.8 copy.38
  675.1 0.0 copy-done.3
  675.1 0.8 copy.39
  675.9 0.0 copy-done
  675.9 1.3 copy.40
  677.2 1.0 copy-done.1
  678.2 1.3 copy.41
  (3 shorter events, 0.0 us)
Async XLA Ops:
  602.1 65.8 %copy-start.7 = (bf16[512,512]{1,0:T(8,128)(2,1)S(1)}, bf16[512,512]{1,0:T(8,128)(2,1)}, u32[]{:S(2)}) copy-start(bf16[512,512]{1,0:T(8,128)(2,1)} %get-tuple-element.136) | copy-start | bytes 1572868
  602.1 65.8 %copy-start.8 = (bf16[512,512]{1,0:T(8,128)(2,1)S(1)}, bf16[512,512]{1,0:T(8,128)(2,1)}, u32[]{:S(2)}) copy-start(bf16[512,512]{1,0:T(8,128)(2,1)} %get-tuple-element.142) | copy-start | bytes 1572868
  602.1 65.8 %copy-start.9 = (bf16[512,512]{1,0:T(8,128)(2,1)S(1)}, bf16[512,512]{1,0:T(8,128)(2,1)}, u32[]{:S(2)}) copy-start(bf16[512,512]{1,0:T(8,128)(2,1)} %get-tuple-element.180) | copy-start | bytes 1572868
  667.9 2.7 copy-start.11
  667.9 3.3 copy-start.2
  667.9 3.3 copy-start.10
  671.2 1.5 copy-start.6
  671.2 2.3 copy-start.5
  671.2 3.1 copy-start.4
  672.7 2.4 copy-start.3
  672.7 3.2 copy-start
  675.9 2.3 copy-start.1
